TPU v7x, 128 devices: a whole 4x4x4 slice. The times are simulated.
128 devices in a mesh: band: 16 (over x, z_lo, core), grid: 8 (over y, z_hi).
Axes of the slice: x: 4, y: 4, z: 4 (z_hi: 2, z_lo: 2; z = z_hi * 2 + z_lo), core: 2. Of those that a mesh axis runs over, the one named last changes fastest.
Arguments:
- valence: bfloat16 [32, 2, 160, 160, 160], P('band', None, 'grid'), may hold values from -6 to 6
- conduction: bfloat16 [16, 2, 160, 160, 160], P('band', None, 'grid'), may hold values from -6 to 6
- val_energy: float32 [32], replicated, may hold values from -12 to -1
- cond_energy: float32 [16], replicated, may hold values from 1 to 16
- cond_band: int32 [16], P('band'), may hold values from 0 to 15, each once
- owners: int32 [2], replicated, may hold values from 0 to 15
- gvectors: int32 [3, 4096], replicated, may hold values from 0 to 159, as said below
Outputs:
- chi0: float32 [2, 4096, 4096], P(None, 'grid', 'band')
Inputs may be any that keep to these rules, and one draw needn't show every extreme that they name: `gvectors`: the G-vectors are distinct; each component, read between -80 and 80, lies within -10 to 10. `owners`: each entry is an index along band. `cond_band`: A permutation of the global conduction band numbers.
All inputs are finite; a program needn't handle non-finite values.
Results may differ from a plain program's by a relative error of at most 0.0092.
Values may be sent and summed in bfloat16 or wider, within the bound.
No kernel may reach another device: no remote copies, remote signals or barrier semaphores. Data moves between devices by JAX's collectives and lax.ppermute only.
A program may use at most 192 MiB of HBM per device.

v0:
```python
import functools
import math

import jax
import jax.numpy as jnp
import numpy as np
from jax import lax
from jax.experimental import pallas as pl
from jax.experimental.pallas import tpu as pltpu
from jax.sharding import PartitionSpec as P

LENGTH = 160
GMAX = 10
SIDE = 2 * GMAX + 1
PARTS = 16
ROWS = 200
TAIL = 104
WIRE = 2 * ROWS + TAIL
PAIRS = 64
PACK = 8
CONDS = 4
SLOTS = 12
KROWS = 24
GCHUNK = 256
BF = jnp.bfloat16
F32 = jnp.float32


def host_tables():
    freq = (np.arange(SIDE) - GMAX) % LENGTH
    pos = np.arange(LENGTH)
    angle = ((freq[:, None] * pos[None, :]) % LENGTH).astype(np.float32) * np.float32(2.0 * math.pi / LENGTH)
    rnd = lambda a: a.astype(np.float32).astype(jnp.bfloat16).astype(np.float32)
    return rnd(np.cos(angle)), rnd(np.sin(angle))


def z_table():
    cos, sin = host_tables()
    out = np.zeros((2 * KROWS, 384), np.float32)
    cm, sm, ct, st = cos[:, :128], sin[:, :128], cos[:, 128:], sin[:, 128:]
    out[:SIDE] = np.concatenate([cm, sm, ct, ct, st, -st], axis=1)
    out[KROWS : KROWS + SIDE] = np.concatenate([-sm, cm, -st, -st, ct, -ct], axis=1)
    return out.astype(jnp.bfloat16)


def y_tables():
    cos, sin = host_tables()
    out = np.zeros((4, 256, 4, 32), np.float32)
    for shift in range(4):
        for row in range(ROWS):
            flat = 40 * shift + row
            x, y = divmod(flat, LENGTH)
            out[shift, row, 2 * x, :SIDE] = cos[:, y]
            out[shift, row, 2 * x + 1, :SIDE] = sin[:, y]
    return out.reshape(4, 256, 128).astype(jnp.bfloat16)


def pack_band(src, out, fill):
    real, imag = src[0], src[1]
    out[0:ROWS] = real[:, :128]
    out[ROWS : 2 * ROWS] = imag[:, :128]
    tail = jnp.concatenate([real[:, 128:].astype(F32), imag[:, 128:].astype(F32)], axis=1)
    low = tail[:TAIL]
    high = jnp.concatenate([tail[TAIL:], jnp.full((2 * TAIL - ROWS, 64), 1.0, F32) * fill], axis=0)
    out[2 * ROWS :] = jnp.concatenate([low, high], axis=1).astype(BF)


def pack_cond_kernel(number_ref, cond_ref, out_ref):
    for t in range(PACK):
        rows = pl.ds(t * ROWS, ROWS)
        pack_band(cond_ref.at[:, rows], out_ref.at[t], number_ref[0].astype(F32))


def pack_cond(conduction, number):
    return pl.pallas_call(
        pack_cond_kernel,
        out_shape=jax.ShapeDtypeStruct((PARTS, WIRE, 128), BF),
        grid_spec=pltpu.PrefetchScalarGridSpec(
            num_scalar_prefetch=1,
            grid=(PARTS // PACK,),
            in_specs=[pl.BlockSpec((2, PACK * ROWS, LENGTH), lambda t, n: (0, t, 0))],
            out_specs=pl.BlockSpec((PACK, WIRE, 128), lambda t, n: (t, 0, 0)),
        ),
        cost_estimate=pl.CostEstimate(flops=0, transcendentals=0, bytes_accessed=6_000_000),
        name="packcond",
    )(number, conduction)


def pack_val_kernel(band_ref, val_ref, out_ref):
    for t in range(PACK):
        pack_band(val_ref.at[0, :, pl.ds(t * ROWS, ROWS)], out_ref.at[t], 0.0)


def pack_choice_kernel(band_ref, own_ref, val_ref, other_ref, out_ref):
    @pl.when(own_ref[0] == 1)
    def _():
        pack_val_kernel(band_ref, val_ref, out_ref)

    @pl.when(own_ref[0] == 0)
    def _():
        out_ref[...] = other_ref[...]


def pack_val(valence, band, own=None, other=None):
    wire_spec = pl.BlockSpec((PACK, WIRE, 128), lambda t, *_: (t, 0, 0))
    scalars, arrays, specs, kernel = (band,), (valence,), [], pack_val_kernel
    specs.append(pl.BlockSpec((1, 2, PACK * ROWS, LENGTH), lambda t, k, *_: (k[0], 0, t, 0)))
    if other is not None:
        scalars, arrays, kernel = (band, own), (valence, other), pack_choice_kernel
        specs.append(wire_spec)
    return pl.pallas_call(
        kernel,
        out_shape=jax.ShapeDtypeStruct((PARTS, WIRE, 128), BF),
        grid_spec=pltpu.PrefetchScalarGridSpec(
            num_scalar_prefetch=len(scalars),
            grid=(PARTS // PACK,),
            in_specs=specs,
            out_specs=wire_spec,
        ),
        cost_estimate=pl.CostEstimate(flops=0, transcendentals=0, bytes_accessed=8_000_000),
        compiler_params=pltpu.CompilerParams(vmem_limit_bytes=40 * 2**20),
        name="packval",
    )(*scalars, *arrays)


def unpack_tail(tail):
    return jnp.concatenate([tail[:, :64], tail[: ROWS - TAIL, 64:]], axis=0)


def plane_tables(shift):
    tab = lax.dynamic_index_in_dim(jnp.asarray(y_tables()), shift, 0, keepdims=False)
    tab = tab.reshape(256, 4, 32)[:, :, :SIDE].transpose(1, 0, 2)
    return jnp.pad(jnp.tile(tab, (1, 1, SLOTS)), ((0, 0), (0, 0), (0, 256 - SLOTS * SIDE)))


def z_kernel(chip_ref, v0_ref, v1_ref, cond_ref, table_ref, ytab_ref, out_ref, val_main, val_tail, low_ref, high_ref):
    step = pl.program_id(0)

    @pl.when(step == 0)
    def _():
        for i in range(4):
            src = (v0_ref if i < 2 else v1_ref).at[i % 2]
            val_main[i, 0] = src[0:ROWS].astype(F32)
            val_main[i, 1] = src[ROWS : 2 * ROWS].astype(F32)
            both = unpack_tail(src[2 * ROWS :].astype(F32))
            val_tail[i] = jnp.concatenate([both, both], axis=1)
        high_ref[...] = jnp.zeros_like(high_ref)

    @pl.loop(0, CONDS)
    def _(c):
        cre = cond_ref[c, 0:ROWS].astype(F32)
        cim = cond_ref[c, ROWS : 2 * ROWS].astype(F32)
        both = unpack_tail(cond_ref[c, 2 * ROWS :].astype(F32))
        ctail = jnp.concatenate([both, both[:, 32:], both[:, :32]], axis=1)
        for i in range(4):
            vre, vim = val_main[i, 0], val_main[i, 1]
            dre = vre * cre + vim * cim
            dim = vre * cim - vim * cre
            tail = val_tail[i] * ctail
            density = jnp.concatenate([dre, dim, tail], axis=1).astype(BF)
            along = lax.dot_general(
                table_ref[...], density, (((1,), (1,)), ((), ())), preferred_element_type=F32
            )
            for part in range(2):
                start = part * PAIRS + (step * CONDS + c) * 4 + i
                piece = along[part * KROWS : (part + 1) * KROWS]
                low_ref[pl.ds(start, KROWS, stride=128), :] = piece[:, :128]
                high_ref[pl.ds(start, KROWS, stride=128), 0 : ROWS - 128] = piece[:, 128:]

    @pl.when(step == pl.num_programs(0) - 1)
    def _():
        lane = lax.broadcasted_iota(jnp.int32, (256, 256), 1)
        acc = [None] * 4
        for s in range(SLOTS):
            left = []
            for k in (s, s + SLOTS):
                rows = pl.ds(k * 128, 128)
                left.append(jnp.concatenate([low_ref[rows], high_ref[rows]], axis=1).astype(BF))
            left = jnp.concatenate(left, axis=0)
            keep = (lane >= s * SIDE) & (lane < (s + 1) * SIDE)
            for t in range(4):
                right = jnp.where(keep, ytab_ref[t], jnp.zeros((256, 256), BF))
                term = jnp.dot(left, right, preferred_element_type=F32)
                acc[t] = term if acc[t] is None else acc[t] + term
        for x in range(2):
            for tile in range(2):
                c = acc[2 * x][tile * 128 : (tile + 1) * 128]
                s = acc[2 * x + 1][tile * 128 : (tile + 1) * 128]
                lanes = pl.ds(tile * 256, 256)
                out_ref[x * 128 : x * 128 + PAIRS, lanes] = (c[:PAIRS] + s[PAIRS:]).astype(BF)
                out_ref[x * 128 + PAIRS : (x + 1) * 128, lanes] = (c[PAIRS:] - s[:PAIRS]).astype(BF)


def z_transform(chip, val_wire, second, cond_wire, ytab):
    return pl.pallas_call(
        z_kernel,
        out_shape=jax.ShapeDtypeStruct((256, 512), BF),
        grid_spec=pltpu.PrefetchScalarGridSpec(
            num_scalar_prefetch=1,
            grid=(PARTS // CONDS,),
            in_specs=[
                pl.BlockSpec((2, WIRE, 128), lambda c, o: (o[0], 0, 0)),
                pl.BlockSpec((2, WIRE, 128), lambda c, o: (0, 0, 0)),
                pl.BlockSpec((CONDS, WIRE, 128), lambda c, o: (c, 0, 0)),
                pl.BlockSpec((2 * KROWS, 384), lambda c, o: (0, 0)),
                pl.BlockSpec((4, 256, 256), lambda c, o: (0, 0, 0)),
            ],
            out_specs=pl.BlockSpec((256, 512), lambda c, o: (0, 0)),
            scratch_shapes=[
                pltpu.VMEM((4, 2, ROWS, 128), F32),
                pltpu.VMEM((4, ROWS, 128), F32),
                pltpu.VMEM((KROWS * 128, 128), F32),
                pltpu.VMEM((KROWS * 128, 128), F32),
            ],
        ),
        compiler_params=pltpu.CompilerParams(vmem_limit_bytes=40 * 2**20),
        name="ztransform",
    )(chip, val_wire, second, cond_wire, jnp.asarray(z_table()), ytab)


def g_kernel(parity_ref, plane_ref, index_ref, phase_ref, out_ref):
    row = lax.broadcasted_iota(jnp.int32, (512, GCHUNK), 0)
    for chunk in range(out_ref.shape[0]):
        pick = jnp.where(row == index_ref[chunk, 0], 1.0, 0.0).astype(BF)
        at = jnp.dot(plane_ref[...], pick, preferred_element_type=F32)
        real = jnp.zeros((PAIRS, GCHUNK), F32)
        imag = jnp.zeros((PAIRS, GCHUNK), F32)
        for x in range(2):
            c = phase_ref[chunk, 0, 2 * x : 2 * x + 1]
            s = phase_ref[chunk, 0, 2 * x + 1 : 2 * x + 2]
            re = at[x * 128 : x * 128 + PAIRS]
            im = at[x * 128 + PAIRS : (x + 1) * 128]
            real = real + re * c + im * s
            imag = imag + im * c - re * s
        out_ref[chunk, :PAIRS] = real.astype(out_ref.dtype)
        out_ref[chunk, PAIRS:] = imag.astype(out_ref.dtype)


def g_elements(parity, plane, index, phase, dtype):
    chips = index.shape[0]
    return pl.pallas_call(
        g_kernel,
        out_shape=jax.ShapeDtypeStruct((chips, 128, GCHUNK), dtype),
        grid_spec=pltpu.PrefetchScalarGridSpec(
            num_scalar_prefetch=1,
            grid=(1,),
            in_specs=[
                pl.BlockSpec((256, 512), lambda i, k: (0, 0)),
                pl.BlockSpec((chips, 1, 1, GCHUNK), lambda i, k: (0, k[0], 0, 0)),
                pl.BlockSpec((chips, 1, 4, GCHUNK), lambda i, k: (0, k[0], 0, 0)),
            ],
            out_specs=pl.BlockSpec((chips, 128, GCHUNK), lambda i, k: (0, 0, 0)),
        ),
        compiler_params=pltpu.CompilerParams(vmem_limit_bytes=40 * 2**20),
        cost_estimate=pl.CostEstimate(flops=2 * 10**9, transcendentals=0, bytes_accessed=12_000_000),
        name="gelements",
    )(parity, plane, index, phase)


def shards(valence, conduction, val_energy, cond_energy, cond_band, owners, gvectors):
    grid_pos = lax.axis_index("grid")
    band_pos = lax.axis_index("band")
    x_local = valence.shape[2]
    n_grid = lax.axis_size("grid")

    rows_all = x_local * LENGTH
    cond_wire = pack_cond(conduction.reshape(2, rows_all, LENGTH), cond_band)
    cond_wire, core = lax.optimization_barrier((cond_wire, band_pos & 1))
    cond_wire = lax.all_to_all(cond_wire, "band", 0, 0, tiled=True)

    first, second = owners[0], owners[1]
    bands = valence.reshape(2, 2, rows_all, LENGTH)
    sibling = pack_val(bands, (1 - core)[None])
    sibling = lax.ppermute(sibling, "band", [(b, b ^ 1) for b in range(PARTS)])
    here = (first >> 1) == (band_pos >> 1)
    own = jnp.where(here, first == band_pos, second == band_pos)
    val_wire = pack_val(bands, core[None], own.astype(jnp.int32)[None], sibling)
    val_wire = lax.all_to_all(val_wire, "band", 0, 0, tiled=True)
    cond_wire, val_wire = lax.optimization_barrier((cond_wire, val_wire))

    ytab = plane_tables(band_pos & 3)
    chip = (first >> 1)[None]

    def exchange_again(operands):
        bands, sibling, val_wire, cond_wire, ytab = operands
        again = pack_val(bands, core[None], (second == band_pos).astype(jnp.int32)[None], sibling)
        again = lax.all_to_all(again, "band", 0, 0, tiled=True)
        again = lax.dynamic_slice_in_dim(again, (second >> 1) * 2, 2, 0)
        return z_transform(chip, val_wire, again, cond_wire, ytab)

    def from_first(operands):
        _, _, val_wire, cond_wire, ytab = operands
        again = lax.dynamic_slice_in_dim(val_wire, (second >> 1) * 2, 2, 0)
        return z_transform(chip, val_wire, again, cond_wire, ytab)

    both = (first != second) & ((first >> 1) == (second >> 1))
    plane = lax.cond(both, exchange_again, from_first, (bands, sibling, val_wire, cond_wire, ytab))

    numbers = cond_wire[:, WIRE - 1, 127].astype(jnp.int32)
    order = jnp.arange(cond_energy.shape[0], dtype=jnp.int32)
    levels = jnp.sum(jnp.where(numbers[:, None] == order[None, :], cond_energy[None, :], 0.0), axis=1)
    val_index = (owners[:, None] * 2 + jnp.arange(2, dtype=jnp.int32)[None, :]).reshape(4)
    val_levels = val_energy[val_index]
    weight = (2.0 / (PAIRS * (val_levels[None, :] - levels[:, None]))).reshape(PAIRS)

    signed = (gvectors + GMAX) % LENGTH
    slot = jnp.where(signed[2] < SLOTS, signed[2] * SIDE, 256 + (signed[2] - SLOTS) * SIDE)
    index = (slot + signed[1]).reshape(PARTS // 2, 2, 1, GCHUNK)
    x_first = grid_pos * x_local + 5 * (band_pos >> 2) + (band_pos & 3)
    norm = float(LENGTH) ** (-1.5)
    waves = []
    for x in range(2):
        angle = (gvectors[0] * (x_first + x) % LENGTH).astype(F32) * (2.0 * math.pi / LENGTH)
        waves += [jnp.cos(angle), jnp.sin(angle)]
    phase = jnp.stack(waves).astype(BF).astype(F32) * norm
    phase = phase.reshape(4, PARTS, GCHUNK).transpose(1, 0, 2).reshape(PARTS // 2, 2, 4, GCHUNK)

    core = band_pos & 1
    away = g_elements((1 - core)[None], plane, index, phase, BF)
    come = lax.ppermute(away, "band", [(b, b ^ 1) for b in range(PARTS)])
    keep = g_elements(core[None], plane, index, phase, F32)
    parts = (keep + come.astype(F32)).astype(BF)
    same_core = [[b for b in range(PARTS) if b % 2 == k] for k in range(2)]
    parts = lax.all_to_all(parts, "band", 0, 0, axis_index_groups=same_core, tiled=True)
    block = jnp.sum(parts.astype(F32), axis=0)
    zh_flip = [(g, g ^ 1) for g in range(n_grid)]
    y_flip = [(g, g ^ 2) for g in range(n_grid)]
    y_rest = [(g, 6 - (g & 6) + (g & 1)) for g in range(n_grid)]
    for perm in (zh_flip, y_flip, y_rest):
        block = block + lax.ppermute(block.astype(BF), "grid", perm).astype(F32)

    straight, crossed = [], []
    for b in range(PARTS):
        for g in range(n_grid):
            straight.append((b * n_grid + g, (2 * g + b % 2) * n_grid + b // 2))
            crossed.append((b * n_grid + g, (2 * g + 1 - b % 2) * n_grid + b // 2))
    block = block.astype(BF)
    same = lax.ppermute(block, ("band", "grid"), straight)
    other = lax.ppermute(block, ("band", "grid"), crossed)
    odd = (band_pos & 1) == 1
    left = jnp.where(odd, other, same)
    right = jnp.where(odd, same, other)
    rows = jnp.concatenate([left, right], axis=1).astype(F32)
    block = block.astype(F32)

    w2 = jnp.concatenate([weight, weight])[:, None]
    for_real = block * w2
    for_imag = jnp.concatenate([-for_real[PAIRS:], for_real[:PAIRS]], axis=0)
    high = lax.Precision.HIGHEST
    chi_re = jnp.einsum("pr,pc->rc", rows, for_real, precision=high)
    chi_im = jnp.einsum("pr,pc->rc", rows, for_imag, precision=high)
    return jnp.stack([chi_re, chi_im])


def solution(mesh):
    return jax.shard_map(
        shards,
        mesh=mesh,
        in_specs=(
            P("band", None, "grid", None, None),
            P("band", None, "grid", None, None),
            P(),
            P(),
            P("band"),
            P(),
            P(),
        ),
        out_specs=P(None, "grid", "band"),
        check_vma=False,
    )
```

profile of v0, /device:TPU:39, one launch (start us, length us, event | category | flops | bytes accessed | tf_op | source)
XLA Modules:
  0.0 134.9 jit_solution(14636215479291571462)
XLA Ops:
  0.7 3.5 %packcond.1 = bf16[16,504,128]{2,1,0:T(8,128)(2,1)} custom-call(s32[1]{0:T(128)S(6)} %copy.31.number_ref, bf16[2,3200,160]{2,1,0:T(8,128)(2,1)} %bitcast.37), custom_call_target="tpu_custom_call" | custom-call | bytes 6000000 | tf_op jit(solution)/shard_map/packcond/pallas_call | solution.py:75
  4.2 2.4 %packval.4 = bf16[16,504,128]{2,1,0:T(8,128)(2,1)S(1)} custom-call(s32[1]{0:T(128)} %bitcast.9.band_ref, bf16[2,2,3200,160]{3,2,1,0:T(8,128)(2,1)} %bitcast.34), custom_call_target="tpu_custom_call" | custom-call | bytes 8000000 | tf_op jit(solution)/shard_map/packval/pallas_call | solution.py:111
  7.4 5.4 %all-to-all-start.1 = ((bf16[16,504,128]{2,1,0:T(8,128)(2,1)}), bf16[16,504,128]{2,1,0:T(8,128)(2,1)}, u32[]{:S(2)}, u32[]{:S(2)}) async-start(bf16[16,504,128]{2,1,0:T(8,128)(2,1)} %packcond.1), calls=%async_computation.1 | async-start | bytes 4128768 | tf_op jit(solution)/shard_map/all_to_all | solution.py:269
  16.3 1.0 cosine_convert_fusion.1
  18.1 3.6 %packval.5 = bf16[16,504,128]{2,1,0:T(8,128)(2,1)} custom-call(s32[1]{0:T(128)} %bitcast.6.band_ref, s32[1]{0:T(128)} %bitcast.7.own_ref, bf16[2,2,3200,160]{3,2,1,0:T(8,128)(2,1)} %bitcast.35, bf16[16,504,128]{2,1,0:T(8,128)(2,1)} %collective-permute-done.other_ref), custom_call_target="tpu_custom_call" | custom-call | bytes 8000000 | tf_op jit(solution)/shard_map/packval/pallas_call | solution.py:111
  21.8 15.4 %all-to-all-done.1 = bf16[16,504,128]{2,1,0:T(8,128)(2,1)} async-done(((bf16[16,504,128]{2,1,0:T(8,128)(2,1)}), bf16[16,504,128]{2,1,0:T(8,128)(2,1)}, u32[]{:S(2)}, u32[]{:S(2)}) %all-to-all-start.1) | async-done | bytes 2064416 | tf_op jit(solution)/shard_map/all_to_all | solution.py:269
  37.2 7.9 %all-to-all-start.2 = ((bf16[16,504,128]{2,1,0:T(8,128)(2,1)}), bf16[16,504,128]{2,1,0:T(8,128)(2,1)S(1)}, u32[]{:S(2)}, u32[]{:S(2)}) async-start(bf16[16,504,128]{2,1,0:T(8,128)(2,1)} %packval.5), calls=%async_computation.2 | async-start | bytes 4128768 | tf_op jit(solution)/shard_map/all_to_all | solution.py:278
  47.7 21.7 %all-to-all-done.2 = bf16[16,504,128]{2,1,0:T(8,128)(2,1)S(1)} async-done(((bf16[16,504,128]{2,1,0:T(8,128)(2,1)}), bf16[16,504,128]{2,1,0:T(8,128)(2,1)S(1)}, u32[]{:S(2)}, u32[]{:S(2)}) %all-to-all-start.2) | async-done | bytes 2064416 | tf_op jit(solution)/shard_map/all_to_all | solution.py:278
  69.4 12.0 %conditional.1 = (bf16[256,512]{1,0:T(8,128)(2,1)S(1)}) conditional(s32[]{:T(128)} %convert_element_type.67, (s32[]{:T(128)}, bf16[16,504,128]{2,1,0:T(8,128)(2,1)S(1)}, s32[1]{0:T(128)}, bf16[16,504,128]{2,1,0:T(8,128)(2,1)}, bf16[48,384]{1,0:T(8,128)(2,1)S(1)}, /*index=5*/bf16[4,256,256]{1,0,2:T(4,128)(2,1)S(1)}) %tuple.33, (s32[]{:T(128)}, ...), branch_computations={%region_0.1_spmd, %region_1.2_spmd} | conditional | flops 7 | bytes 15757940 | solution.py:297
  70.4 11.0 %ztransform.2 = bf16[256,512]{1,0:T(8,128)(2,1)S(1)} custom-call(s32[1]{0:T(128)} %get-tuple-element.40.chip_ref, bf16[16,504,128]{2,1,0:T(8,128)(2,1)S(1)} %get-tuple-element.41.v0_ref, bf16[2,504,128]{2,1,0:T(8,128)(2,1)S(1)} %constant_dynamic-slice_fusion.v1_ref, bf16[16,504,128]{2,1,0:T(8,128)(2,1)} %get-tuple-element.43.cond_ref, ...), custom_call_target="tpu_custom_call" | custom-call | tf_op jit(solution)/shard_map/cond/branch_0_fun/ztransform/pallas_call | solution.py:195
  85.3 7.4 %all-to-all-start.3 = ((bf16[8,128,256]{2,1,0:T(8,128)(2,1)}), bf16[8,128,256]{2,1,0:T(8,128)(2,1)S(1)}, u32[]{:S(2)}, u32[]{:S(2)}) async-start(bf16[8,128,256]{2,1,0:T(8,128)(2,1)} %add_convert_fusion), calls=%async_computation.3 | async-start | bytes 1048576 | tf_op jit(solution)/shard_map/all_to_all | solution.py:324
  93.5 1.2 convert_reduce_fusion.1
  94.7 5.3 %all-to-all-done.3 = bf16[8,128,256]{2,1,0:T(8,128)(2,1)S(1)} async-done(((bf16[8,128,256]{2,1,0:T(8,128)(2,1)}), bf16[8,128,256]{2,1,0:T(8,128)(2,1)S(1)}, u32[]{:S(2)}, u32[]{:S(2)}) %all-to-all-start.3) | async-done | bytes 524320 | tf_op jit(solution)/shard_map/all_to_all | solution.py:324
  100.1 2.8 %collective-permute-start.2 = (bf16[128,256]{1,0:T(8,128)(2,1)S(1)}, bf16[128,256]{1,0:T(8,128)(2,1)S(1)}, u32[]{:S(2)}, u32[]{:S(2)}) collective-permute-start(bf16[128,256]{1,0:T(8,128)(2,1)S(1)} %convert_element_type.74), channel_id=1, source_target_pairs={{0,1},{1,0},{2,3},{3,2},{4,5},{5,4},{6,7},{7,6},{8,9},{9,8},{10,11... | collective-permute-start | bytes 196616 | tf_op jit(solution)/shard_map/ppermute | solution.py:330
  103.0 1.7 %collective-permute-done.2 = bf16[128,256]{1,0:T(8,128)(2,1)S(1)} collective-permute-done((bf16[128,256]{1,0:T(8,128)(2,1)S(1)}, bf16[128,256]{1,0:T(8,128)(2,1)S(1)}, u32[]{:S(2)}, u32[]{:S(2)}) %collective-permute-start.2) | collective-permute-done | bytes 65568 | tf_op jit(solution)/shard_map/ppermute | solution.py:330
  104.8 1.4 %collective-permute-start.3 = (bf16[128,256]{1,0:T(8,128)(2,1)S(1)}, bf16[128,256]{1,0:T(8,128)(2,1)S(1)}, u32[]{:S(2)}, u32[]{:S(2)}) collective-permute-start(bf16[128,256]{1,0:T(8,128)(2,1)S(1)} %fusion.3), channel_id=1, source_target_pairs={{0,2},{1,3},{2,0},{3,1},{4,6},{5,7},{6,4},{7,5},{8,10},{9,11},{10,... | collective-permute-start | bytes 196616 | tf_op jit(solution)/shard_map/ppermute | solution.py:330
  106.3 1.6 %collective-permute-done.3 = bf16[128,256]{1,0:T(8,128)(2,1)S(1)} collective-permute-done((bf16[128,256]{1,0:T(8,128)(2,1)S(1)}, bf16[128,256]{1,0:T(8,128)(2,1)S(1)}, u32[]{:S(2)}, u32[]{:S(2)}) %collective-permute-start.3) | collective-permute-done | bytes 65568 | tf_op jit(solution)/shard_map/ppermute | solution.py:330
  108.0 2.8 %collective-permute-start.4 = (bf16[128,256]{1,0:T(8,128)(2,1)S(1)}, bf16[128,256]{1,0:T(8,128)(2,1)S(1)}, u32[]{:S(2)}, u32[]{:S(2)}) collective-permute-start(bf16[128,256]{1,0:T(8,128)(2,1)S(1)} %fusion.4), channel_id=1, source_target_pairs={{0,6},{1,7},{2,4},{3,5},{4,2},{5,3},{6,0},{7,1},{8,14},{9,15},{10,... | collective-permute-start | bytes 196616 | tf_op jit(solution)/shard_map/ppermute | solution.py:330
  110.9 1.6 %collective-permute-done.4 = bf16[128,256]{1,0:T(8,128)(2,1)S(1)} collective-permute-done((bf16[128,256]{1,0:T(8,128)(2,1)S(1)}, bf16[128,256]{1,0:T(8,128)(2,1)S(1)}, u32[]{:S(2)}, u32[]{:S(2)}) %collective-permute-start.4) | collective-permute-done | bytes 65568 | tf_op jit(solution)/shard_map/ppermute | solution.py:330
  112.6 10.4 %collective-permute-start.5 = (bf16[128,256]{1,0:T(8,128)(2,1)S(1)}, bf16[128,256]{1,0:T(8,128)(2,1)S(1)}, u32[]{:S(2)}, u32[]{:S(2)}) collective-permute-start(bf16[128,256]{1,0:T(8,128)(2,1)S(1)} %get-tuple-element.97), channel_id=1, source_target_pairs={{0,8},{1,24},{2,40},{3,56},{4,72},{5,88},{6,104},{7,120},{8,0},{9,... | collective-permute-start | bytes 196616 | tf_op jit(solution)/shard_map/ppermute | solution.py:339
  123.0 1.9 %collective-permute-start.6 = (bf16[128,256]{1,0:T(8,128)(2,1)S(1)}, bf16[128,256]{1,0:T(8,128)(2,1)S(1)}, u32[]{:S(2)}, u32[]{:S(2)}) collective-permute-start(bf16[128,256]{1,0:T(8,128)(2,1)S(1)} %get-tuple-element.97), channel_id=1, source_target_pairs={{0,0},{1,16},{2,32},{3,48},{4,64},{5,80},{6,96},{7,112},{8,8},{9,2... | collective-permute-start | bytes 196616 | tf_op jit(solution)/shard_map/ppermute | solution.py:338
  125.0 1.8 %collective-permute-done.5 = bf16[128,256]{1,0:T(8,128)(2,1)S(1)} collective-permute-done((bf16[128,256]{1,0:T(8,128)(2,1)S(1)}, bf16[128,256]{1,0:T(8,128)(2,1)S(1)}, u32[]{:S(2)}, u32[]{:S(2)}) %collective-permute-start.5) | collective-permute-done | bytes 65568 | tf_op jit(solution)/shard_map/ppermute | solution.py:339
  126.8 6.1 %collective-permute-done.6 = bf16[128,256]{1,0:T(8,128)(2,1)S(1)} collective-permute-done((bf16[128,256]{1,0:T(8,128)(2,1)S(1)}, bf16[128,256]{1,0:T(8,128)(2,1)S(1)}, u32[]{:S(2)}, u32[]{:S(2)}) %collective-permute-start.6) | collective-permute-done | bytes 65568 | tf_op jit(solution)/shard_map/ppermute | solution.py:338
  133.9 1.0 pad_maximum_fusion
  (48 shorter events, 10.3 us)
Async XLA Ops:
  0.0 92.9 %copy-start = (f32[32]{0:T(128)S(1)}, f32[32]{0:T(128)}, u32[]{:S(2)}) copy-start(f32[32]{0:T(128)} %param.14) | copy-start | bytes 388
  6.6 6.2 %copy-start.3 = (s32[2]{0:T(128)S(1)}, s32[2]{0:T(128)}, u32[]{:S(2)}) copy-start(s32[2]{0:T(128)} %param.17) | copy-start | bytes 28
  6.7 9.6 %copy-start.2 = (s32[3,4096]{1,0:T(4,128)S(1)}, s32[3,4096]{1,0:T(4,128)}, u32[]{:S(2)}) copy-start(s32[3,4096]{1,0:T(4,128)} %param.18) | copy-start | bytes 147460
  6.7 11.5 %collective-permute-start = (bf16[16,504,128]{2,1,0:T(8,128)(2,1)S(1)}, bf16[16,504,128]{2,1,0:T(8,128)(2,1)}, u32[]{:S(2)}, u32[]{:S(2)}) collective-permute-start(bf16[16,504,128]{2,1,0:T(8,128)(2,1)S(1)} %packval.4), channel_id=1, source_target_pairs={{0,8},{8,0},{16,24},{24,16},{32,40},{40,32},{48,56},{56,48},{64,72... | collective-permute-start | bytes 6193160 | tf_op jit(solution)/shard_map/ppermute | solution.py:274
  7.4 29.8 %all-to-all-start.1 = ((bf16[16,504,128]{2,1,0:T(8,128)(2,1)}), bf16[16,504,128]{2,1,0:T(8,128)(2,1)}, u32[]{:S(2)}, u32[]{:S(2)}) async-start(bf16[16,504,128]{2,1,0:T(8,128)(2,1)} %packcond.1), calls=%async_computation.1 | async-start | bytes 4128768 | tf_op jit(solution)/shard_map/all_to_all | solution.py:269
  37.2 32.2 %all-to-all-start.2 = ((bf16[16,504,128]{2,1,0:T(8,128)(2,1)}), bf16[16,504,128]{2,1,0:T(8,128)(2,1)S(1)}, u32[]{:S(2)}, u32[]{:S(2)}) async-start(bf16[16,504,128]{2,1,0:T(8,128)(2,1)} %packval.5), calls=%async_computation.2 | async-start | bytes 4128768 | tf_op jit(solution)/shard_map/all_to_all | solution.py:278
  45.1 24.2 %copy-start.1 = (bf16[48,384]{1,0:T(8,128)(2,1)S(1)}, bf16[48,384]{1,0:T(8,128)(2,1)}, u32[]{:S(2)}) copy-start(bf16[48,384]{1,0:T(8,128)(2,1)} %constant.93.clone) | copy-start | bytes 110596
  82.3 2.1 %collective-permute-start.1 = (bf16[8,128,256]{2,1,0:T(8,128)(2,1)S(1)}, bf16[8,128,256]{2,1,0:T(8,128)(2,1)S(1)}, u32[]{:S(2)}, u32[]{:S(2)}) collective-permute-start(bf16[8,128,256]{2,1,0:T(8,128)(2,1)S(1)} %gelements.3), channel_id=1, source_target_pairs={{0,8},{8,0},{16,24},{24,16},{32,40},{40,32},{48,56},{56,48},{64,72... | collective-permute-start | bytes 1572872 | tf_op jit(solution)/shard_map/ppermute | solution.py:320
  83.6 19.2 %copy-start.4 = (f32[16]{0:T(128)S(1)}, f32[16]{0:T(128)}, u32[]{:S(2)}) copy-start(f32[16]{0:T(128)} %param.15) | copy-start | bytes 196
  85.3 14.7 %all-to-all-start.3 = ((bf16[8,128,256]{2,1,0:T(8,128)(2,1)}), bf16[8,128,256]{2,1,0:T(8,128)(2,1)S(1)}, u32[]{:S(2)}, u32[]{:S(2)}) async-start(bf16[8,128,256]{2,1,0:T(8,128)(2,1)} %add_convert_fusion), calls=%async_computation.3 | async-start | bytes 1048576 | tf_op jit(solution)/shard_map/all_to_all | solution.py:324
  100.1 4.7 %collective-permute-start.2 = (bf16[128,256]{1,0:T(8,128)(2,1)S(1)}, bf16[128,256]{1,0:T(8,128)(2,1)S(1)}, u32[]{:S(2)}, u32[]{:S(2)}) collective-permute-start(bf16[128,256]{1,0:T(8,128)(2,1)S(1)} %convert_element_type.74), channel_id=1, source_target_pairs={{0,1},{1,0},{2,3},{3,2},{4,5},{5,4},{6,7},{7,6},{8,9},{9,8},{10,11... | collective-permute-start | bytes 196616 | tf_op jit(solution)/shard_map/ppermute | solution.py:330
  104.8 3.2 %collective-permute-start.3 = (bf16[128,256]{1,0:T(8,128)(2,1)S(1)}, bf16[128,256]{1,0:T(8,128)(2,1)S(1)}, u32[]{:S(2)}, u32[]{:S(2)}) collective-permute-start(bf16[128,256]{1,0:T(8,128)(2,1)S(1)} %fusion.3), channel_id=1, source_target_pairs={{0,2},{1,3},{2,0},{3,1},{4,6},{5,7},{6,4},{7,5},{8,10},{9,11},{10,... | collective-permute-start | bytes 196616 | tf_op jit(solution)/shard_map/ppermute | solution.py:330
  108.0 4.5 %collective-permute-start.4 = (bf16[128,256]{1,0:T(8,128)(2,1)S(1)}, bf16[128,256]{1,0:T(8,128)(2,1)S(1)}, u32[]{:S(2)}, u32[]{:S(2)}) collective-permute-start(bf16[128,256]{1,0:T(8,128)(2,1)S(1)} %fusion.4), channel_id=1, source_target_pairs={{0,6},{1,7},{2,4},{3,5},{4,2},{5,3},{6,0},{7,1},{8,14},{9,15},{10,... | collective-permute-start | bytes 196616 | tf_op jit(solution)/shard_map/ppermute | solution.py:330
  112.6 14.2 %collective-permute-start.5 = (bf16[128,256]{1,0:T(8,128)(2,1)S(1)}, bf16[128,256]{1,0:T(8,128)(2,1)S(1)}, u32[]{:S(2)}, u32[]{:S(2)}) collective-permute-start(bf16[128,256]{1,0:T(8,128)(2,1)S(1)} %get-tuple-element.97), channel_id=1, source_target_pairs={{0,8},{1,24},{2,40},{3,56},{4,72},{5,88},{6,104},{7,120},{8,0},{9,... | collective-permute-start | bytes 196616 | tf_op jit(solution)/shard_map/ppermute | solution.py:339
  123.0 9.9 %collective-permute-start.6 = (bf16[128,256]{1,0:T(8,128)(2,1)S(1)}, bf16[128,256]{1,0:T(8,128)(2,1)S(1)}, u32[]{:S(2)}, u32[]{:S(2)}) collective-permute-start(bf16[128,256]{1,0:T(8,128)(2,1)S(1)} %get-tuple-element.97), channel_id=1, source_target_pairs={{0,0},{1,16},{2,32},{3,48},{4,64},{5,80},{6,96},{7,112},{8,8},{9,2... | collective-permute-start | bytes 196616 | tf_op jit(solution)/shard_map/ppermute | solution.py:338
where the time goes:
time: 135 us
  waiting for transfers between devices  56 us (41%)
  starting transfers between devices  41.5 us (31%)
  Pallas kernels  22.3 us (17%)
  other arithmetic  5.9 us (4%)
  between operations  4.63 us (3%)
  local copies, waits for them, and re-layouts  3.05 us (2%)
    all_to_all x1, waiting for transfers between devices, shards(): val_wire = lax.all_to_all(val_wire, 'band', 0, 0, tiled=True)  21.7 us
    all_to_all x1, waiting for transfers between devices, shards(): cond_wire = lax.all_to_all(cond_wire, 'band', 0, 0, tiled=True)  15.4 us
    pallas_call x1, Pallas kernels, z_transform(): pl.pallas_call(z_kernel, out_shape=jax.ShapeDtypeStruct((256, 512), BF),...  11 us
    ppermute x1, starting transfers between devices, shards(): other = lax.ppermute(block, ('band', 'grid'), crossed)  10.4 us
    all_to_all x1, starting transfers between devices, shards(): val_wire = lax.all_to_all(val_wire, 'band', 0, 0, tiled=True)  7.95 us
    all_to_all x1, starting transfers between devices, shards(): lax.all_to_all(parts, 'band', 0, 0, axis_index_groups=same_core, tiled=True)  7.43 us
    ppermute x3, starting transfers between devices, shards(): block = block + lax.ppermute(block.astype(BF), 'grid', perm).astype(F32)  6.99 us
    ppermute x1, waiting for transfers between devices, shards(): same = lax.ppermute(block, ('band', 'grid'), straight)  6.14 us
  transfers between devices with their start and end apart: 10, of which 9 were waited for; matrix products, arithmetic and copies ran while one was open for 5% of the time, Pallas kernels for 3%

commit v1 on v0

--- a/solution.py
+++ b/solution.py
@@ -17,8 +17,8 @@
 TAIL = 104
 WIRE = 2 * ROWS + TAIL
 PAIRS = 64
-PACK = 8
-CONDS = 4
+CHIPS = 8
+STEP = 4
 SLOTS = 12
 KROWS = 24
 GCHUNK = 256
@@ -65,62 +65,102 @@
     out[2 * ROWS :] = jnp.concatenate([low, high], axis=1).astype(BF)
 
 
-def pack_cond_kernel(number_ref, cond_ref, out_ref):
-    for t in range(PACK):
-        rows = pl.ds(t * ROWS, ROWS)
-        pack_band(cond_ref.at[:, rows], out_ref.at[t], number_ref[0].astype(F32))
-
-
-def pack_cond(conduction, number):
+def pack_cond_kernel(core_ref, number_ref, keep_ref, give_ref, keep_out, give_out):
+    number = number_ref[0].astype(F32)
+    for c in range(STEP):
+        pack_band(keep_ref.at[:, c, 0], keep_out.at[c], number)
+        pack_band(give_ref.at[:, c, 0], give_out.at[c], number)
+
+
+def pack_cond(conduction, core, number):
+    block = (2, STEP, 1, ROWS, LENGTH)
+    out = pltpu.HBM((CHIPS, WIRE, 128), BF)
     return pl.pallas_call(
         pack_cond_kernel,
-        out_shape=jax.ShapeDtypeStruct((PARTS, WIRE, 128), BF),
+        out_shape=(out, out),
+        grid_spec=pltpu.PrefetchScalarGridSpec(
+            num_scalar_prefetch=2,
+            grid=(CHIPS // STEP,),
+            in_specs=[
+                pl.BlockSpec(block, lambda t, k, n: (0, t, k[0], 0, 0)),
+                pl.BlockSpec(block, lambda t, k, n: (0, t, 1 - k[0], 0, 0)),
+            ],
+            out_specs=[
+                pl.BlockSpec((STEP, WIRE, 128), lambda t, k, n: (t, 0, 0)),
+                pl.BlockSpec((STEP, WIRE, 128), lambda t, k, n: (t, 0, 0)),
+            ],
+        ),
+        cost_estimate=pl.CostEstimate(flops=0, transcendentals=0, bytes_accessed=6_000_000),
+        compiler_params=pltpu.CompilerParams(vmem_limit_bytes=40 * 2**20),
+        name="packcond",
+    )(core, number, conduction, conduction)
+
+
+def pack_bands(val_ref, out_ref):
+    for c in range(STEP):
+        for band in range(2):
+            pack_band(val_ref.at[band, :, c, 0], out_ref.at[c, band], 0.0)
+
+
+def pack_give_kernel(core_ref, val_ref, out_ref):
+    pack_bands(val_ref, out_ref)
+
+
+VAL_BLOCK = (2, 2, STEP, 1, ROWS, LENGTH)
+
+
+def pack_give(valence, core):
+    return pl.pallas_call(
+        pack_give_kernel,
+        out_shape=pltpu.HBM((CHIPS, 2, WIRE, 128), BF),
         grid_spec=pltpu.PrefetchScalarGridSpec(
             num_scalar_prefetch=1,
-            grid=(PARTS // PACK,),
-            in_specs=[pl.BlockSpec((2, PACK * ROWS, LENGTH), lambda t, n: (0, t, 0))],
-            out_specs=pl.BlockSpec((PACK, WIRE, 128), lambda t, n: (t, 0, 0)),
+            grid=(CHIPS // STEP,),
+            in_specs=[pl.BlockSpec(VAL_BLOCK, lambda t, k: (0, 0, t, 1 - k[0], 0, 0))],
+            out_specs=pl.BlockSpec((STEP, 2, WIRE, 128), lambda t, k: (t, 0, 0, 0)),
         ),
         cost_estimate=pl.CostEstimate(flops=0, transcendentals=0, bytes_accessed=6_000_000),
-        name="packcond",
-    )(number, conduction)
-
-
-def pack_val_kernel(band_ref, val_ref, out_ref):
-    for t in range(PACK):
-        pack_band(val_ref.at[0, :, pl.ds(t * ROWS, ROWS)], out_ref.at[t], 0.0)
-
-
-def pack_choice_kernel(band_ref, own_ref, val_ref, other_ref, out_ref):
+        compiler_params=pltpu.CompilerParams(vmem_limit_bytes=40 * 2**20),
+        name="packgive",
+    )(core, valence)
+
+
+def pack_choice_kernel(core_ref, own_ref, val_ref, other_ref, *refs):
+    out_ref = refs[-1]
+
     @pl.when(own_ref[0] == 1)
     def _():
-        pack_val_kernel(band_ref, val_ref, out_ref)
+        pack_bands(val_ref, out_ref)
 
     @pl.when(own_ref[0] == 0)
     def _():
-        out_ref[...] = other_ref[...]
-
-
-def pack_val(valence, band, own=None, other=None):
-    wire_spec = pl.BlockSpec((PACK, WIRE, 128), lambda t, *_: (t, 0, 0))
-    scalars, arrays, specs, kernel = (band,), (valence,), [], pack_val_kernel
-    specs.append(pl.BlockSpec((1, 2, PACK * ROWS, LENGTH), lambda t, k, *_: (k[0], 0, t, 0)))
-    if other is not None:
-        scalars, arrays, kernel = (band, own), (valence, other), pack_choice_kernel
-        specs.append(wire_spec)
+        out_ref[:, 0:2] = other_ref[...]
+
+    if len(refs) == 2:
+        out_ref[:, 2] = refs[0][...]
+
+
+def pack_choice(valence, core, own, other, cond=None):
+    slots = 2 if cond is None else 3
+    arrays = (valence, other) if cond is None else (valence, other, cond)
+    specs = [
+        pl.BlockSpec(VAL_BLOCK, lambda t, k, o: (0, 0, t, k[0], 0, 0)),
+        pl.BlockSpec((STEP, 2, WIRE, 128), lambda t, k, o: (t, 0, 0, 0)),
+        pl.BlockSpec((STEP, WIRE, 128), lambda t, k, o: (t, 0, 0)),
+    ]
     return pl.pallas_call(
-        kernel,
-        out_shape=jax.ShapeDtypeStruct((PARTS, WIRE, 128), BF),
+        pack_choice_kernel,
+        out_shape=pltpu.HBM((CHIPS, slots, WIRE, 128), BF),
         grid_spec=pltpu.PrefetchScalarGridSpec(
-            num_scalar_prefetch=len(scalars),
-            grid=(PARTS // PACK,),
-            in_specs=specs,
-            out_specs=wire_spec,
-        ),
-        cost_estimate=pl.CostEstimate(flops=0, transcendentals=0, bytes_accessed=8_000_000),
+            num_scalar_prefetch=2,
+            grid=(CHIPS // STEP,),
+            in_specs=specs[: len(arrays)],
+            out_specs=pl.BlockSpec((STEP, slots, WIRE, 128), lambda t, k, o: (t, 0, 0, 0)),
+        ),
+        cost_estimate=pl.CostEstimate(flops=0, transcendentals=0, bytes_accessed=10_000_000),
         compiler_params=pltpu.CompilerParams(vmem_limit_bytes=40 * 2**20),
-        name="packval",
-    )(*scalars, *arrays)
+        name="packchoice",
+    )(core, own, *arrays)
 
 
 def unpack_tail(tail):
@@ -133,39 +173,47 @@
     return jnp.pad(jnp.tile(tab, (1, 1, SLOTS)), ((0, 0), (0, 0), (0, 256 - SLOTS * SIDE)))
 
 
-def z_kernel(chip_ref, v0_ref, v1_ref, cond_ref, table_ref, ytab_ref, out_ref, val_main, val_tail, low_ref, high_ref):
+def z_kernel(
+    where_ref, v0_ref, v1_ref, own_ref, sib_ref, table_ref, ytab_ref, out_ref, val_main, val_tail, low_ref, high_ref
+):
     step = pl.program_id(0)
 
     @pl.when(step == 0)
     def _():
         for i in range(4):
-            src = (v0_ref if i < 2 else v1_ref).at[i % 2]
+            src = (v0_ref if i < 2 else v1_ref).at[0, i % 2]
             val_main[i, 0] = src[0:ROWS].astype(F32)
             val_main[i, 1] = src[ROWS : 2 * ROWS].astype(F32)
             both = unpack_tail(src[2 * ROWS :].astype(F32))
             val_tail[i] = jnp.concatenate([both, both], axis=1)
         high_ref[...] = jnp.zeros_like(high_ref)
 
-    @pl.loop(0, CONDS)
+    @pl.loop(0, STEP)
     def _(c):
-        cre = cond_ref[c, 0:ROWS].astype(F32)
-        cim = cond_ref[c, ROWS : 2 * ROWS].astype(F32)
-        both = unpack_tail(cond_ref[c, 2 * ROWS :].astype(F32))
-        ctail = jnp.concatenate([both, both[:, 32:], both[:, :32]], axis=1)
-        for i in range(4):
-            vre, vim = val_main[i, 0], val_main[i, 1]
-            dre = vre * cre + vim * cim
-            dim = vre * cim - vim * cre
-            tail = val_tail[i] * ctail
-            density = jnp.concatenate([dre, dim, tail], axis=1).astype(BF)
-            along = lax.dot_general(
-                table_ref[...], density, (((1,), (1,)), ((), ())), preferred_element_type=F32
-            )
-            for part in range(2):
-                start = part * PAIRS + (step * CONDS + c) * 4 + i
-                piece = along[part * KROWS : (part + 1) * KROWS]
-                low_ref[pl.ds(start, KROWS, stride=128), :] = piece[:, :128]
-                high_ref[pl.ds(start, KROWS, stride=128), 0 : ROWS - 128] = piece[:, 128:]
+        for which in range(2):
+            src = own_ref.at[c] if which == 0 else sib_ref.at[c, 0]
+            core = where_ref[2] if which == 0 else 1 - where_ref[2]
+            first = ((step * STEP + c) * 2 + core) * 4
+            cre = src[0:ROWS].astype(F32)
+            cim = src[ROWS : 2 * ROWS].astype(F32)
+            both = unpack_tail(src[2 * ROWS :].astype(F32))
+            ctail = jnp.concatenate([both, both[:, 32:], both[:, :32]], axis=1)
+            for i in range(0, 4, 2):
+                density = []
+                for j in (i, i + 1):
+                    vre, vim = val_main[j, 0], val_main[j, 1]
+                    density += [vre * cre + vim * cim, vre * cim - vim * cre, val_tail[j] * ctail]
+                density = jnp.concatenate(density, axis=1).astype(BF)
+                along = lax.dot_general(
+                    table_ref[...], density, (((1,), (1,)), ((), ())), preferred_element_type=F32
+                )
+                for j in range(2):
+                    for part in range(2):
+                        start = part * PAIRS + first + i + j
+                        at = (2 * j + part) * KROWS
+                        piece = along[at : at + KROWS]
+                        low_ref[pl.ds(start, KROWS, stride=128), :] = piece[:, :128]
+                        high_ref[pl.ds(start, KROWS, stride=128), 0 : ROWS - 128] = piece[:, 128:]
 
     @pl.when(step == pl.num_programs(0) - 1)
     def _():
@@ -191,18 +239,23 @@
                 out_ref[x * 128 + PAIRS : (x + 1) * 128, lanes] = (c[PAIRS:] - s[:PAIRS]).astype(BF)
 
 
-def z_transform(chip, val_wire, second, cond_wire, ytab):
+def z_transform(where, val_wire, second, own, ytab):
+    single = z_table()
+    table = np.zeros((4 * KROWS, 768), single.dtype)
+    table[: 2 * KROWS, :384] = single
+    table[2 * KROWS :, 384:] = single
     return pl.pallas_call(
         z_kernel,
         out_shape=jax.ShapeDtypeStruct((256, 512), BF),
         grid_spec=pltpu.PrefetchScalarGridSpec(
             num_scalar_prefetch=1,
-            grid=(PARTS // CONDS,),
+            grid=(CHIPS // STEP,),
             in_specs=[
-                pl.BlockSpec((2, WIRE, 128), lambda c, o: (o[0], 0, 0)),
-                pl.BlockSpec((2, WIRE, 128), lambda c, o: (0, 0, 0)),
-                pl.BlockSpec((CONDS, WIRE, 128), lambda c, o: (c, 0, 0)),
-                pl.BlockSpec((2 * KROWS, 384), lambda c, o: (0, 0)),
+                pl.BlockSpec((1, 2, WIRE, 128), lambda c, o: (o[0], 0, 0, 0)),
+                pl.BlockSpec((1, 2, WIRE, 128), lambda c, o: (o[1], 0, 0, 0)),
+                pl.BlockSpec((STEP, WIRE, 128), lambda c, o: (c, 0, 0)),
+                pl.BlockSpec((STEP, 1, WIRE, 128), lambda c, o: (c, 2, 0, 0)),
+                pl.BlockSpec((4 * KROWS, 768), lambda c, o: (0, 0)),
                 pl.BlockSpec((4, 256, 256), lambda c, o: (0, 0, 0)),
             ],
             out_specs=pl.BlockSpec((256, 512), lambda c, o: (0, 0)),
@@ -215,7 +268,7 @@
         ),
         compiler_params=pltpu.CompilerParams(vmem_limit_bytes=40 * 2**20),
         name="ztransform",
-    )(chip, val_wire, second, cond_wire, jnp.asarray(z_table()), ytab)
+    )(where, val_wire, second, own, val_wire, jnp.asarray(table), ytab)
 
 
 def g_kernel(parity_ref, plane_ref, index_ref, phase_ref, out_ref):
@@ -263,40 +316,43 @@
     x_local = valence.shape[2]
     n_grid = lax.axis_size("grid")
 
-    rows_all = x_local * LENGTH
-    cond_wire = pack_cond(conduction.reshape(2, rows_all, LENGTH), cond_band)
-    cond_wire, core = lax.optimization_barrier((cond_wire, band_pos & 1))
-    cond_wire = lax.all_to_all(cond_wire, "band", 0, 0, tiled=True)
+    core = band_pos & 1
+    siblings = [(b, b ^ 1) for b in range(PARTS)]
+    same_core = [[b for b in range(PARTS) if b % 2 == k] for k in range(2)]
+
+    conduction = pltpu.with_memory_space_constraint(conduction.reshape(2, CHIPS, 2, ROWS, LENGTH), pltpu.HBM)
+    keep, give = pack_cond(conduction, core[None], cond_band)
+    cond_sib = lax.ppermute(give, "band", siblings)
+    keep, core_late = lax.optimization_barrier((keep, core))
+    cond_own = lax.all_to_all(keep, "band", 0, 0, axis_index_groups=same_core, tiled=True)
 
     first, second = owners[0], owners[1]
-    bands = valence.reshape(2, 2, rows_all, LENGTH)
-    sibling = pack_val(bands, (1 - core)[None])
-    sibling = lax.ppermute(sibling, "band", [(b, b ^ 1) for b in range(PARTS)])
+    bands = pltpu.with_memory_space_constraint(valence.reshape(2, 2, CHIPS, 2, ROWS, LENGTH), pltpu.HBM)
+    val_sib = lax.ppermute(pack_give(bands, core_late[None]), "band", siblings)
     here = (first >> 1) == (band_pos >> 1)
     own = jnp.where(here, first == band_pos, second == band_pos)
-    val_wire = pack_val(bands, core[None], own.astype(jnp.int32)[None], sibling)
-    val_wire = lax.all_to_all(val_wire, "band", 0, 0, tiled=True)
-    cond_wire, val_wire = lax.optimization_barrier((cond_wire, val_wire))
+    wire = pack_choice(bands, core[None], own.astype(jnp.int32)[None], val_sib, cond_sib)
+    cond_own, wire = lax.optimization_barrier((cond_own, wire))
+    wire = lax.all_to_all(wire, "band", 0, 0, axis_index_groups=same_core, tiled=True)
 
     ytab = plane_tables(band_pos & 3)
-    chip = (first >> 1)[None]
+    where = jnp.stack([first >> 1, second >> 1, core])
 
     def exchange_again(operands):
-        bands, sibling, val_wire, cond_wire, ytab = operands
-        again = pack_val(bands, core[None], (second == band_pos).astype(jnp.int32)[None], sibling)
-        again = lax.all_to_all(again, "band", 0, 0, tiled=True)
-        again = lax.dynamic_slice_in_dim(again, (second >> 1) * 2, 2, 0)
-        return z_transform(chip, val_wire, again, cond_wire, ytab)
+        bands, val_sib, wire, cond_own, ytab = operands
+        again = pack_choice(bands, core[None], (second == band_pos).astype(jnp.int32)[None], val_sib)
+        again = lax.all_to_all(again, "band", 0, 0, axis_index_groups=same_core, tiled=True)
+        return z_transform(where, wire, again, cond_own, ytab)
 
     def from_first(operands):
-        _, _, val_wire, cond_wire, ytab = operands
-        again = lax.dynamic_slice_in_dim(val_wire, (second >> 1) * 2, 2, 0)
-        return z_transform(chip, val_wire, again, cond_wire, ytab)
+        _, _, wire, cond_own, ytab = operands
+        return z_transform(where, wire, wire, cond_own, ytab)
 
     both = (first != second) & ((first >> 1) == (second >> 1))
-    plane = lax.cond(both, exchange_again, from_first, (bands, sibling, val_wire, cond_wire, ytab))
-
-    numbers = cond_wire[:, WIRE - 1, 127].astype(jnp.int32)
+    plane = lax.cond(both, exchange_again, from_first, (bands, val_sib, wire, cond_own, ytab))
+
+    last = jnp.stack([cond_own[:, WIRE - 1, 127], wire[:, 2, WIRE - 1, 127]], axis=1)
+    numbers = jnp.where(core == 0, last, last[:, ::-1]).reshape(PARTS).astype(jnp.int32)
     order = jnp.arange(cond_energy.shape[0], dtype=jnp.int32)
     levels = jnp.sum(jnp.where(numbers[:, None] == order[None, :], cond_energy[None, :], 0.0), axis=1)
     val_index = (owners[:, None] * 2 + jnp.arange(2, dtype=jnp.int32)[None, :]).reshape(4)
@@ -315,19 +371,17 @@
     phase = jnp.stack(waves).astype(BF).astype(F32) * norm
     phase = phase.reshape(4, PARTS, GCHUNK).transpose(1, 0, 2).reshape(PARTS // 2, 2, 4, GCHUNK)
 
-    core = band_pos & 1
     away = g_elements((1 - core)[None], plane, index, phase, BF)
-    come = lax.ppermute(away, "band", [(b, b ^ 1) for b in range(PARTS)])
+    come = lax.ppermute(away, "band", siblings)
     keep = g_elements(core[None], plane, index, phase, F32)
     parts = (keep + come.astype(F32)).astype(BF)
-    same_core = [[b for b in range(PARTS) if b % 2 == k] for k in range(2)]
     parts = lax.all_to_all(parts, "band", 0, 0, axis_index_groups=same_core, tiled=True)
     block = jnp.sum(parts.astype(F32), axis=0)
-    zh_flip = [(g, g ^ 1) for g in range(n_grid)]
-    y_flip = [(g, g ^ 2) for g in range(n_grid)]
-    y_rest = [(g, 6 - (g & 6) + (g & 1)) for g in range(n_grid)]
-    for perm in (zh_flip, y_flip, y_rest):
-        block = block + lax.ppermute(block.astype(BF), "grid", perm).astype(F32)
+    block = block + lax.ppermute(block.astype(BF), "grid", [(g, g ^ 1) for g in range(n_grid)]).astype(F32)
+    narrow = block.astype(BF)
+    for turn in (2, 4, 6):
+        step = [(g, (g + turn) % n_grid) for g in range(n_grid)]
+        block = block + lax.ppermute(narrow, "grid", step).astype(F32)
 
     straight, crossed = [], []
     for b in range(PARTS):

time: 135 us -> 138 us (1.022)
  local copies, waits for them, and re-layouts: 3.05 us -> 5.09 us
  waiting for transfers between devices: 56 us -> 57.6 us
    all_to_all x2, waiting for transfers between devices: 37.2 us -> 40.1 us  [the longest x1 38.6 us: shards(): lax.all_to_all(wire, 'band', 0, 0, axis_index_groups=same_core, tiled=True)]
    ppermute x5 -> x7, starting transfers between devices: 8.27 us -> 11.2 us  [the longest x3 5.05 us: shards(): block = block + lax.ppermute(narrow, 'grid', step).astype(F32)]
    slice x0 -> x2, local copies, waits for them, and re-layouts: none -> 1.86 us  [the longest x1 0.93 us: shards(): cond_own[:, WIRE - 1, 127]]
    ppermute x1, starting transfers between devices: 10.4 us -> 8.75 us  [shards(): other = lax.ppermute(block, ('band', 'grid'), crossed)]
    ppermute x5 -> x7, waiting for transfers between devices: 5.63 us -> 3.97 us  [the longest x3 2.2 us: shards(): block = block + lax.ppermute(narrow, 'grid', step).astype(F32)]
  transfers between devices with their start and end apart: 10 -> 12, of which waited for: 9 -> 8; matrix products, arithmetic and copies ran while one was open for 5% -> 5% of each run, Pallas kernels for 3% -> 3%
where the time goes in v1:
time: 138 us; the launch traced here: 137 us
  waiting for transfers between devices  57.6 us (42%)
  starting transfers between devices  41.5 us (30%)
  Pallas kernels  22.7 us (16%)
  local copies, waits for them, and re-layouts  5.09 us (4%)
  between operations  4.85 us (4%)
  other arithmetic  4.77 us (3%)
    all_to_all x1, waiting for transfers between devices, shards(): lax.all_to_all(wire, 'band', 0, 0, axis_index_groups=same_core, tiled=True)  38.6 us
    pallas_call x1, Pallas kernels, z_transform(): pl.pallas_call(z_kernel, out_shape=jax.ShapeDtypeStruct((256, 512), BF),...  10.4 us
    ppermute x1, starting transfers between devices, shards(): other = lax.ppermute(block, ('band', 'grid'), crossed)  8.75 us
    all_to_all x1, starting transfers between devices, shards(): lax.all_to_all(parts, 'band', 0, 0, axis_index_groups=same_core, tiled=True)  7.18 us
    all_to_all x1, starting transfers between devices, shards(): lax.all_to_all(wire, 'band', 0, 0, axis_index_groups=same_core, tiled=True)  7.1 us
    all_to_all x1, waiting for transfers between devices, shards(): lax.all_to_all(parts, 'band', 0, 0, axis_index_groups=same_core, tiled=True)  6.51 us
    all_to_all x1, starting transfers between devices, shards(): lax.all_to_all(keep, 'band', 0, 0, axis_index_groups=same_core, tiled=True)  5.12 us
    ppermute x3, starting transfers between devices, shards(): block = block + lax.ppermute(narrow, 'grid', step).astype(F32)  5.05 us
  transfers between devices with their start and end apart: 12, of which 8 were waited for; matrix products, arithmetic and copies ran while one was open for 5% of the time, Pallas kernels for 3%

profile of v1, /device:TPU:39, one launch (start us, length us, event | category | flops | bytes accessed | tf_op | source)
XLA Modules:
  0.0 137.4 jit_solution(6537754948952147667)
XLA Ops:
  0.7 3.4 %packcond.1 = (bf16[8,504,128]{2,1,0:T(8,128)(2,1)}, bf16[8,504,128]{2,1,0:T(8,128)(2,1)}) custom-call(s32[1]{0:T(128)} %bitcast.2.core_ref.parity_ref, s32[1]{0:T(128)S(6)} %copy.34.number_ref, bf16[2,8,2,200,160]{4,3,2,1,0:T(8,128)(2,1)} %bitcast.39, bf16[2,8,2,200,160]{4,3,2,1,0:T(8,128)(2,1)} %bitcast.40), custom_call_target="tpu_custom_call" | custom-call | bytes 6000000 | tf_op jit(solution)/shard_map/packcond/pallas_call | solution.py:78
  4.0 3.4 %packgive.1 = bf16[8,2,504,128]{3,2,1,0:T(8,128)(2,1)} custom-call(s32[1]{0:T(128)} %bitcast.10.core_ref, bf16[2,2,8,2,200,160]{5,4,3,2,1,0:T(8,128)(2,1)} %bitcast.36), custom_call_target="tpu_custom_call" | custom-call | bytes 6000000 | tf_op jit(solution)/shard_map/packgive/pallas_call | solution.py:113
  8.1 5.1 %all-to-all-start.1 = ((bf16[8,504,128]{2,1,0:T(8,128)(2,1)}), bf16[8,504,128]{2,1,0:T(8,128)(2,1)S(1)}, u32[]{:S(2)}, u32[]{:S(2)}) async-start(bf16[8,504,128]{2,1,0:T(8,128)(2,1)} %get-tuple-element.60), calls=%async_computation.1 | async-start | bytes 2064384 | tf_op jit(solution)/shard_map/all_to_all | solution.py:327
  19.3 1.0 cosine_convert_fusion.1
  20.4 3.8 %packchoice.3 = bf16[8,3,504,128]{3,2,1,0:T(8,128)(2,1)} custom-call(s32[1]{0:T(128)} %bitcast.2.core_ref.parity_ref, s32[1]{0:T(128)} %bitcast.8.own_ref, bf16[2,2,8,2,200,160]{5,4,3,2,1,0:T(8,128)(2,1)} %bitcast.37, bf16[8,2,504,128]{3,2,1,0:T(8,128)(2,1)} %collective-permute-done.other_ref, bf16[8,504,128]{2,1,0:T(8,128)(2,1)S(1)} %collective-permute-done.1.refs_0_), custom_call_target="tpu_custom_call" | custom-call | bytes 10000000 | tf_op jit(solution)/shard_map/packchoice/pallas_call | solution.py:151
  24.2 1.5 %all-to-all-done.1 = bf16[8,504,128]{2,1,0:T(8,128)(2,1)S(1)} async-done(((bf16[8,504,128]{2,1,0:T(8,128)(2,1)}), bf16[8,504,128]{2,1,0:T(8,128)(2,1)S(1)}, u32[]{:S(2)}, u32[]{:S(2)}) %all-to-all-start.1) | async-done | bytes 1032224 | tf_op jit(solution)/shard_map/all_to_all | solution.py:327
  25.7 7.1 %all-to-all-start.2 = ((bf16[8,3,504,128]{3,2,1,0:T(8,128)(2,1)}), bf16[8,3,504,128]{3,2,1,0:T(8,128)(2,1)}, u32[]{:S(2)}, u32[]{:S(2)}) async-start(bf16[8,3,504,128]{3,2,1,0:T(8,128)(2,1)} %packchoice.3), calls=%async_computation.2 | async-start | bytes 6193152 | tf_op jit(solution)/shard_map/all_to_all | solution.py:336
  33.9 38.6 %all-to-all-done.2 = bf16[8,3,504,128]{3,2,1,0:T(8,128)(2,1)} async-done(((bf16[8,3,504,128]{3,2,1,0:T(8,128)(2,1)}), bf16[8,3,504,128]{3,2,1,0:T(8,128)(2,1)}, u32[]{:S(2)}, u32[]{:S(2)}) %all-to-all-start.2) | async-done | bytes 3096608 | tf_op jit(solution)/shard_map/all_to_all | solution.py:336
  72.6 10.7 %conditional.1 = (bf16[256,512]{1,0:T(8,128)(2,1)S(1)}) conditional(s32[]{:T(128)} %convert_element_type.67, (s32[3]{0:T(128)S(1)}, bf16[8,3,504,128]{3,2,1,0:T(8,128)(2,1)}, bf16[8,504,128]{2,1,0:T(8,128)(2,1)S(1)}, bf16[96,768]{1,0:T(8,128)(2,1)S(1)}, bf16[4,256,256]{1,0,2:T(4,128)(2,1)S(1)}) %tuple.33, (s32[]{:T(128)}, s32[]{:T(128)}, s32[]{:T(128)}, ...), branch_computations={%region_0.1_spmd, %region_1.2_spmd} | conditional | flops 2 | bytes 23467758 | solution.py:352
  72.9 10.4 %ztransform.2 = bf16[256,512]{1,0:T(8,128)(2,1)S(1)} custom-call(s32[3]{0:T(128)S(1)} %get-tuple-element.38.where_ref, bf16[8,3,504,128]{3,2,1,0:T(8,128)(2,1)} %get-tuple-element.39.v0_ref.v1_ref.sib_ref, bf16[8,3,504,128]{3,2,1,0:T(8,128)(2,1)} %get-tuple-element.39.v0_ref.v1_ref.sib_ref, bf16[8,504,128]{2,1,0:T(8,128)(2,1)S(1)} %get-tuple-element.40.own_ref, ...), custom_call_target="tpu_custom_call" | custom-call | tf_op jit(solution)/shard_map/cond/branch_0_fun/ztransform/pallas_call | solution.py:247
  84.2 2.7 %collective-permute-start.2 = (bf16[8,128,256]{2,1,0:T(8,128)(2,1)S(1)}, bf16[8,128,256]{2,1,0:T(8,128)(2,1)S(1)}, u32[]{:S(2)}, u32[]{:S(2)}) collective-permute-start(bf16[8,128,256]{2,1,0:T(8,128)(2,1)S(1)} %gelements.3), channel_id=1, source_target_pairs={{0,8},{8,0},{16,24},{24,16},{32,40},{40,32},{48,56},{56,48},{64,72... | collective-permute-start | bytes 1572872 | tf_op jit(solution)/shard_map/ppermute | solution.py:375
  90.3 7.2 %all-to-all-start.3 = ((bf16[8,128,256]{2,1,0:T(8,128)(2,1)}), bf16[8,128,256]{2,1,0:T(8,128)(2,1)S(1)}, u32[]{:S(2)}, u32[]{:S(2)}) async-start(bf16[8,128,256]{2,1,0:T(8,128)(2,1)} %add_convert_fusion), calls=%async_computation.3 | async-start | bytes 1048576 | tf_op jit(solution)/shard_map/all_to_all | solution.py:378
  98.8 6.5 %all-to-all-done.3 = bf16[8,128,256]{2,1,0:T(8,128)(2,1)S(1)} async-done(((bf16[8,128,256]{2,1,0:T(8,128)(2,1)}), bf16[8,128,256]{2,1,0:T(8,128)(2,1)S(1)}, u32[]{:S(2)}, u32[]{:S(2)}) %all-to-all-start.3) | async-done | bytes 524320 | tf_op jit(solution)/shard_map/all_to_all | solution.py:378
  105.4 2.8 %collective-permute-start.3 = (bf16[128,256]{1,0:T(8,128)(2,1)S(1)}, bf16[128,256]{1,0:T(8,128)(2,1)S(1)}, u32[]{:S(2)}, u32[]{:S(2)}) collective-permute-start(bf16[128,256]{1,0:T(8,128)(2,1)S(1)} %convert_element_type.74), channel_id=1, source_target_pairs={{0,1},{1,0},{2,3},{3,2},{4,5},{5,4},{6,7},{7,6},{8,9},{9,8},{10,11... | collective-permute-start | bytes 196616 | tf_op jit(solution)/shard_map/ppermute | solution.py:380
  108.3 1.8 %collective-permute-done.3 = bf16[128,256]{1,0:T(8,128)(2,1)S(1)} collective-permute-done((bf16[128,256]{1,0:T(8,128)(2,1)S(1)}, bf16[128,256]{1,0:T(8,128)(2,1)S(1)}, u32[]{:S(2)}, u32[]{:S(2)}) %collective-permute-start.3) | collective-permute-done | bytes 65568 | tf_op jit(solution)/shard_map/ppermute | solution.py:380
  110.1 1.4 collective-permute-start.4
  111.4 2.6 %collective-permute-start.5 = (bf16[128,256]{1,0:T(8,128)(2,1)S(1)}, bf16[128,256]{1,0:T(8,128)(2,1)S(1)}, u32[]{:S(2)}, u32[]{:S(2)}) collective-permute-start(bf16[128,256]{1,0:T(8,128)(2,1)S(1)} %fusion.3), channel_id=1, source_target_pairs={{0,4},{1,5},{2,6},{3,7},{4,0},{5,1},{6,2},{7,3},{8,12},{9,13},{10,... | collective-permute-start | bytes 196616 | tf_op jit(solution)/shard_map/ppermute | solution.py:384
  114.1 1.1 collective-permute-start.6
  115.2 1.2 collective-permute-done.5
  117.5 8.7 %collective-permute-start.7 = (bf16[128,256]{1,0:T(8,128)(2,1)S(1)}, bf16[128,256]{1,0:T(8,128)(2,1)S(1)}, u32[]{:S(2)}, u32[]{:S(2)}) collective-permute-start(bf16[128,256]{1,0:T(8,128)(2,1)S(1)} %get-tuple-element.96), channel_id=1, source_target_pairs={{0,8},{1,24},{2,40},{3,56},{4,72},{5,88},{6,104},{7,120},{8,0},{9,... | collective-permute-start | bytes 196616 | tf_op jit(solution)/shard_map/ppermute | solution.py:393
  126.2 2.2 %collective-permute-start.8 = (bf16[128,256]{1,0:T(8,128)(2,1)S(1)}, bf16[128,256]{1,0:T(8,128)(2,1)S(1)}, u32[]{:S(2)}, u32[]{:S(2)}) collective-permute-start(bf16[128,256]{1,0:T(8,128)(2,1)S(1)} %get-tuple-element.96), channel_id=1, source_target_pairs={{0,0},{1,16},{2,32},{3,48},{4,64},{5,80},{6,96},{7,112},{8,8},{9,2... | collective-permute-start | bytes 196616 | tf_op jit(solution)/shard_map/ppermute | solution.py:392
  128.5 2.0 %collective-permute-done.7 = bf16[128,256]{1,0:T(8,128)(2,1)S(1)} collective-permute-done((bf16[128,256]{1,0:T(8,128)(2,1)S(1)}, bf16[128,256]{1,0:T(8,128)(2,1)S(1)}, u32[]{:S(2)}, u32[]{:S(2)}) %collective-permute-start.7) | collective-permute-done | bytes 65568 | tf_op jit(solution)/shard_map/ppermute | solution.py:393
  130.6 4.9 %collective-permute-done.8 = bf16[128,256]{1,0:T(8,128)(2,1)S(1)} collective-permute-done((bf16[128,256]{1,0:T(8,128)(2,1)S(1)}, bf16[128,256]{1,0:T(8,128)(2,1)S(1)}, u32[]{:S(2)}, u32[]{:S(2)}) %collective-permute-start.8) | collective-permute-done | bytes 65568 | tf_op jit(solution)/shard_map/ppermute | solution.py:392
  136.4 1.0 pad_maximum_fusion
  (59 shorter events, 12.1 us)
Async XLA Ops:
  0.0 86.9 %copy-start = (f32[32]{0:T(128)S(1)}, f32[32]{0:T(128)}, u32[]{:S(2)}) copy-start(f32[32]{0:T(128)} %param.14) | copy-start | bytes 388
  4.0 10.0 %copy-start.6 = (s32[2]{0:T(128)S(1)}, s32[2]{0:T(128)}, u32[]{:S(2)}) copy-start(s32[2]{0:T(128)} %param.17) | copy-start | bytes 28
  7.4 11.9 %copy-start.5 = (s32[3,4096]{1,0:T(4,128)S(1)}, s32[3,4096]{1,0:T(4,128)}, u32[]{:S(2)}) copy-start(s32[3,4096]{1,0:T(4,128)} %param.18) | copy-start | bytes 147460
  7.4 12.9 %collective-permute-start = (bf16[8,2,504,128]{3,2,1,0:T(8,128)(2,1)}, bf16[8,2,504,128]{3,2,1,0:T(8,128)(2,1)}, u32[]{:S(2)}, u32[]{:S(2)}) collective-permute-start(bf16[8,2,504,128]{3,2,1,0:T(8,128)(2,1)} %packgive.1), channel_id=1, source_target_pairs={{0,8},{8,0},{16,24},{24,16},{32,40},{40,32},{48,56},{56,48},{64,72... | collective-permute-start | bytes 6193160 | tf_op jit(solution)/shard_map/ppermute | solution.py:331
  8.1 12.2 %collective-permute-start.1 = (bf16[8,504,128]{2,1,0:T(8,128)(2,1)}, bf16[8,504,128]{2,1,0:T(8,128)(2,1)S(1)}, u32[]{:S(2)}, u32[]{:S(2)}) collective-permute-start(bf16[8,504,128]{2,1,0:T(8,128)(2,1)} %get-tuple-element.62), channel_id=1, source_target_pairs={{0,8},{8,0},{16,24},{24,16},{32,40},{40,32},{48,56},{56,48},{64,72... | collective-permute-start | bytes 3096584 | tf_op jit(solution)/shard_map/ppermute | solution.py:325
  8.1 17.6 %all-to-all-start.1 = ((bf16[8,504,128]{2,1,0:T(8,128)(2,1)}), bf16[8,504,128]{2,1,0:T(8,128)(2,1)S(1)}, u32[]{:S(2)}, u32[]{:S(2)}) async-start(bf16[8,504,128]{2,1,0:T(8,128)(2,1)} %get-tuple-element.60), calls=%async_computation.1 | async-start | bytes 2064384 | tf_op jit(solution)/shard_map/all_to_all | solution.py:327
  24.2 48.4 %copy-start.4 = (bf16[96,768]{1,0:T(8,128)(2,1)S(1)}, bf16[96,768]{1,0:T(8,128)(2,1)}, u32[]{:S(2)}) copy-start(bf16[96,768]{1,0:T(8,128)(2,1)} %constant.77.clone) | copy-start | bytes 442372
  25.7 46.8 %copy-start.1 = (bf16[8,504,128]{2,1,0:T(8,128)(2,1)}, bf16[8,504,128]{2,1,0:T(8,128)(2,1)S(1)}, u32[]{:S(2)}) copy-start(bf16[8,504,128]{2,1,0:T(8,128)(2,1)S(1)} %all-to-all-done.1) | copy-start | bytes 3096580
  25.7 46.8 %all-to-all-start.2 = ((bf16[8,3,504,128]{3,2,1,0:T(8,128)(2,1)}), bf16[8,3,504,128]{3,2,1,0:T(8,128)(2,1)}, u32[]{:S(2)}, u32[]{:S(2)}) async-start(bf16[8,3,504,128]{3,2,1,0:T(8,128)(2,1)} %packchoice.3), calls=%async_computation.2 | async-start | bytes 6193152 | tf_op jit(solution)/shard_map/all_to_all | solution.py:336
  84.2 5.1 %collective-permute-start.2 = (bf16[8,128,256]{2,1,0:T(8,128)(2,1)S(1)}, bf16[8,128,256]{2,1,0:T(8,128)(2,1)S(1)}, u32[]{:S(2)}, u32[]{:S(2)}) collective-permute-start(bf16[8,128,256]{2,1,0:T(8,128)(2,1)S(1)} %gelements.3), channel_id=1, source_target_pairs={{0,8},{8,0},{16,24},{24,16},{32,40},{40,32},{48,56},{56,48},{64,72... | collective-permute-start | bytes 1572872 | tf_op jit(solution)/shard_map/ppermute | solution.py:375
  89.3 9.3 %copy-start.7 = (f32[16]{0:T(128)S(1)}, f32[16]{0:T(128)}, u32[]{:S(2)}) copy-start(f32[16]{0:T(128)} %param.15) | copy-start | bytes 196
  90.3 15.0 %all-to-all-start.3 = ((bf16[8,128,256]{2,1,0:T(8,128)(2,1)}), bf16[8,128,256]{2,1,0:T(8,128)(2,1)S(1)}, u32[]{:S(2)}, u32[]{:S(2)}) async-start(bf16[8,128,256]{2,1,0:T(8,128)(2,1)} %add_convert_fusion), calls=%async_computation.3 | async-start | bytes 1048576 | tf_op jit(solution)/shard_map/all_to_all | solution.py:378
  105.4 4.7 %collective-permute-start.3 = (bf16[128,256]{1,0:T(8,128)(2,1)S(1)}, bf16[128,256]{1,0:T(8,128)(2,1)S(1)}, u32[]{:S(2)}, u32[]{:S(2)}) collective-permute-start(bf16[128,256]{1,0:T(8,128)(2,1)S(1)} %convert_element_type.74), channel_id=1, source_target_pairs={{0,1},{1,0},{2,3},{3,2},{4,5},{5,4},{6,7},{7,6},{8,9},{9,8},{10,11... | collective-permute-start | bytes 196616 | tf_op jit(solution)/shard_map/ppermute | solution.py:380
  110.1 5.1 %collective-permute-start.4 = (bf16[128,256]{1,0:T(8,128)(2,1)S(1)}, bf16[128,256]{1,0:T(8,128)(2,1)S(1)}, u32[]{:S(2)}, u32[]{:S(2)}) collective-permute-start(bf16[128,256]{1,0:T(8,128)(2,1)S(1)} %fusion.3), channel_id=1, source_target_pairs={{0,2},{1,3},{2,4},{3,5},{4,6},{5,7},{6,0},{7,1},{8,10},{9,11},{10,... | collective-permute-start | bytes 196616 | tf_op jit(solution)/shard_map/ppermute | solution.py:384
  111.4 5.0 %collective-permute-start.5 = (bf16[128,256]{1,0:T(8,128)(2,1)S(1)}, bf16[128,256]{1,0:T(8,128)(2,1)S(1)}, u32[]{:S(2)}, u32[]{:S(2)}) collective-permute-start(bf16[128,256]{1,0:T(8,128)(2,1)S(1)} %fusion.3), channel_id=1, source_target_pairs={{0,4},{1,5},{2,6},{3,7},{4,0},{5,1},{6,2},{7,3},{8,12},{9,13},{10,... | collective-permute-start | bytes 196616 | tf_op jit(solution)/shard_map/ppermute | solution.py:384
  114.1 3.3 %collective-permute-start.6 = (bf16[128,256]{1,0:T(8,128)(2,1)S(1)}, bf16[128,256]{1,0:T(8,128)(2,1)S(1)}, u32[]{:S(2)}, u32[]{:S(2)}) collective-permute-start(bf16[128,256]{1,0:T(8,128)(2,1)S(1)} %fusion.3), channel_id=1, source_target_pairs={{0,6},{1,7},{2,0},{3,1},{4,2},{5,3},{6,4},{7,5},{8,14},{9,15},{10,... | collective-permute-start | bytes 196616 | tf_op jit(solution)/shard_map/ppermute | solution.py:384
  117.5 13.1 %collective-permute-start.7 = (bf16[128,256]{1,0:T(8,128)(2,1)S(1)}, bf16[128,256]{1,0:T(8,128)(2,1)S(1)}, u32[]{:S(2)}, u32[]{:S(2)}) collective-permute-start(bf16[128,256]{1,0:T(8,128)(2,1)S(1)} %get-tuple-element.96), channel_id=1, source_target_pairs={{0,8},{1,24},{2,40},{3,56},{4,72},{5,88},{6,104},{7,120},{8,0},{9,... | collective-permute-start | bytes 196616 | tf_op jit(solution)/shard_map/ppermute | solution.py:393
  126.2 9.2 %collective-permute-start.8 = (bf16[128,256]{1,0:T(8,128)(2,1)S(1)}, bf16[128,256]{1,0:T(8,128)(2,1)S(1)}, u32[]{:S(2)}, u32[]{:S(2)}) collective-permute-start(bf16[128,256]{1,0:T(8,128)(2,1)S(1)} %get-tuple-element.96), channel_id=1, source_target_pairs={{0,0},{1,16},{2,32},{3,48},{4,64},{5,80},{6,96},{7,112},{8,8},{9,2... | collective-permute-start | bytes 196616 | tf_op jit(solution)/shard_map/ppermute | solution.py:392

commit v2 on v0

--- a/solution.py
+++ b/solution.py
@@ -152,20 +152,23 @@
         cim = cond_ref[c, ROWS : 2 * ROWS].astype(F32)
         both = unpack_tail(cond_ref[c, 2 * ROWS :].astype(F32))
         ctail = jnp.concatenate([both, both[:, 32:], both[:, :32]], axis=1)
-        for i in range(4):
-            vre, vim = val_main[i, 0], val_main[i, 1]
-            dre = vre * cre + vim * cim
-            dim = vre * cim - vim * cre
-            tail = val_tail[i] * ctail
-            density = jnp.concatenate([dre, dim, tail], axis=1).astype(BF)
+        first = (step * CONDS + c) * 4
+        for i in range(0, 4, 2):
+            density = []
+            for j in (i, i + 1):
+                vre, vim = val_main[j, 0], val_main[j, 1]
+                density += [vre * cre + vim * cim, vre * cim - vim * cre, val_tail[j] * ctail]
+            density = jnp.concatenate(density, axis=1).astype(BF)
             along = lax.dot_general(
                 table_ref[...], density, (((1,), (1,)), ((), ())), preferred_element_type=F32
             )
-            for part in range(2):
-                start = part * PAIRS + (step * CONDS + c) * 4 + i
-                piece = along[part * KROWS : (part + 1) * KROWS]
-                low_ref[pl.ds(start, KROWS, stride=128), :] = piece[:, :128]
-                high_ref[pl.ds(start, KROWS, stride=128), 0 : ROWS - 128] = piece[:, 128:]
+            for j in range(2):
+                for part in range(2):
+                    start = part * PAIRS + first + i + j
+                    at = (2 * j + part) * KROWS
+                    piece = along[at : at + KROWS]
+                    low_ref[pl.ds(start, KROWS, stride=128), :] = piece[:, :128]
+                    high_ref[pl.ds(start, KROWS, stride=128), 0 : ROWS - 128] = piece[:, 128:]
 
     @pl.when(step == pl.num_programs(0) - 1)
     def _():
@@ -192,6 +195,10 @@
 
 
 def z_transform(chip, val_wire, second, cond_wire, ytab):
+    single = z_table()
+    table = np.zeros((4 * KROWS, 768), single.dtype)
+    table[: 2 * KROWS, :384] = single
+    table[2 * KROWS :, 384:] = single
     return pl.pallas_call(
         z_kernel,
         out_shape=jax.ShapeDtypeStruct((256, 512), BF),
@@ -202,7 +209,7 @@
                 pl.BlockSpec((2, WIRE, 128), lambda c, o: (o[0], 0, 0)),
                 pl.BlockSpec((2, WIRE, 128), lambda c, o: (0, 0, 0)),
                 pl.BlockSpec((CONDS, WIRE, 128), lambda c, o: (c, 0, 0)),
-                pl.BlockSpec((2 * KROWS, 384), lambda c, o: (0, 0)),
+                pl.BlockSpec((4 * KROWS, 768), lambda c, o: (0, 0)),
                 pl.BlockSpec((4, 256, 256), lambda c, o: (0, 0, 0)),
             ],
             out_specs=pl.BlockSpec((256, 512), lambda c, o: (0, 0)),
@@ -215,7 +222,7 @@
         ),
         compiler_params=pltpu.CompilerParams(vmem_limit_bytes=40 * 2**20),
         name="ztransform",
-    )(chip, val_wire, second, cond_wire, jnp.asarray(z_table()), ytab)
+    )(chip, val_wire, second, cond_wire, jnp.asarray(table), ytab)
 
 
 def g_kernel(parity_ref, plane_ref, index_ref, phase_ref, out_ref):
@@ -316,35 +323,32 @@
     phase = phase.reshape(4, PARTS, GCHUNK).transpose(1, 0, 2).reshape(PARTS // 2, 2, 4, GCHUNK)
 
     core = band_pos & 1
+    siblings = [(b, b ^ 1) for b in range(PARTS)]
     away = g_elements((1 - core)[None], plane, index, phase, BF)
-    come = lax.ppermute(away, "band", [(b, b ^ 1) for b in range(PARTS)])
+    come = lax.ppermute(away, "band", siblings)
     keep = g_elements(core[None], plane, index, phase, F32)
     parts = (keep + come.astype(F32)).astype(BF)
-    same_core = [[b for b in range(PARTS) if b % 2 == k] for k in range(2)]
-    parts = lax.all_to_all(parts, "band", 0, 0, axis_index_groups=same_core, tiled=True)
+    parts = lax.all_to_all(parts, "grid", 0, 0, tiled=True)
     block = jnp.sum(parts.astype(F32), axis=0)
-    zh_flip = [(g, g ^ 1) for g in range(n_grid)]
-    y_flip = [(g, g ^ 2) for g in range(n_grid)]
-    y_rest = [(g, 6 - (g & 6) + (g & 1)) for g in range(n_grid)]
-    for perm in (zh_flip, y_flip, y_rest):
-        block = block + lax.ppermute(block.astype(BF), "grid", perm).astype(F32)
-
-    straight, crossed = [], []
+    block = block + lax.ppermute(block.astype(BF), "band", [(b, b ^ 2) for b in range(PARTS)]).astype(F32)
+    narrow = block.astype(BF)
+    for turn in (4, 8, 12):
+        step = [(b, (b + turn) % PARTS) for b in range(PARTS)]
+        block = block + lax.ppermute(narrow, "band", step).astype(F32)
+
+    narrow = block.astype(BF)
+    far = []
     for b in range(PARTS):
         for g in range(n_grid):
-            straight.append((b * n_grid + g, (2 * g + b % 2) * n_grid + b // 2))
-            crossed.append((b * n_grid + g, (2 * g + 1 - b % 2) * n_grid + b // 2))
-    block = block.astype(BF)
-    same = lax.ppermute(block, ("band", "grid"), straight)
-    other = lax.ppermute(block, ("band", "grid"), crossed)
-    odd = (band_pos & 1) == 1
-    left = jnp.where(odd, other, same)
-    right = jnp.where(odd, same, other)
+            far.append((b * n_grid + g, (2 * g + b % 2) * n_grid + b // 2))
+    column = lax.ppermute(narrow, ("band", "grid"), far).astype(F32)
+    other = lax.ppermute(narrow, "band", siblings)
+    left = jnp.where(core == 1, other, narrow)
+    right = jnp.where(core == 1, narrow, other)
     rows = jnp.concatenate([left, right], axis=1).astype(F32)
-    block = block.astype(F32)
 
     w2 = jnp.concatenate([weight, weight])[:, None]
-    for_real = block * w2
+    for_real = column * w2
     for_imag = jnp.concatenate([-for_real[PAIRS:], for_real[:PAIRS]], axis=0)
     high = lax.Precision.HIGHEST
     chi_re = jnp.einsum("pr,pc->rc", rows, for_real, precision=high)

time: 135 us -> 134 us (level)
  the two profiles are of different devices: /device:TPU:39 before, /device:TPU:38 now
where the time goes in v2:
time: 134 us; the launch traced here: 133 us
  waiting for transfers between devices  59.7 us (45%)
  starting transfers between devices  32.6 us (24%)
  Pallas kernels  25.7 us (19%)
  other arithmetic  5.91 us (4%)
  between operations  4.54 us (3%)
  local copies, waits for them, and re-layouts  2.98 us (2%)
    all_to_all x1, waiting for transfers between devices, shards(): val_wire = lax.all_to_all(val_wire, 'band', 0, 0, tiled=True)  21.9 us
    all_to_all x1, waiting for transfers between devices, shards(): cond_wire = lax.all_to_all(cond_wire, 'band', 0, 0, tiled=True)  15.1 us
    pallas_call x1, Pallas kernels, z_transform(): pl.pallas_call(z_kernel, out_shape=jax.ShapeDtypeStruct((256, 512), BF),...  12.1 us
    all_to_all x1, waiting for transfers between devices, shards(): parts = lax.all_to_all(parts, 'grid', 0, 0, tiled=True)  9.25 us
    all_to_all x1, starting transfers between devices, shards(): val_wire = lax.all_to_all(val_wire, 'band', 0, 0, tiled=True)  7.86 us
    ppermute x1, waiting for transfers between devices, shards(): column = lax.ppermute(narrow, ('band', 'grid'), far).astype(F32)  7.27 us
    all_to_all x1, starting transfers between devices, shards(): parts = lax.all_to_all(parts, 'grid', 0, 0, tiled=True)  6.89 us
    pallas_call x2, Pallas kernels, pack_val(): pl.pallas_call(kernel, out_shape=jax.ShapeDtypeStruct((PARTS, WIRE, 128),...  6.51 us
  transfers between devices with their start and end apart: 11, of which 8 were waited for; matrix products, arithmetic and copies ran while one was open for 5% of the time, Pallas kernels for 4%

profile of v2, /device:TPU:38, one launch (start us, length us, event | category | flops | bytes accessed | tf_op | source)
XLA Modules:
  0.0 132.9 jit_solution(5021044127819508342)
XLA Ops:
  0.7 3.5 %packcond.1 = bf16[16,504,128]{2,1,0:T(8,128)(2,1)} custom-call(s32[1]{0:T(128)S(6)} %copy.31.number_ref, bf16[2,3200,160]{2,1,0:T(8,128)(2,1)} %bitcast.37), custom_call_target="tpu_custom_call" | custom-call | bytes 6000000 | tf_op jit(solution)/shard_map/packcond/pallas_call | solution.py:75
  4.2 2.4 %packval.4 = bf16[16,504,128]{2,1,0:T(8,128)(2,1)S(1)} custom-call(s32[1]{0:T(128)} %bitcast.9.band_ref, bf16[2,2,3200,160]{3,2,1,0:T(8,128)(2,1)} %bitcast.34), custom_call_target="tpu_custom_call" | custom-call | bytes 8000000 | tf_op jit(solution)/shard_map/packval/pallas_call | solution.py:111
  6.8 5.8 %all-to-all-start.1 = ((bf16[16,504,128]{2,1,0:T(8,128)(2,1)}), bf16[16,504,128]{2,1,0:T(8,128)(2,1)}, u32[]{:S(2)}, u32[]{:S(2)}) async-start(bf16[16,504,128]{2,1,0:T(8,128)(2,1)} %packcond.1), calls=%async_computation.1 | async-start | bytes 4128768 | tf_op jit(solution)/shard_map/all_to_all | solution.py:276
  15.9 1.0 cosine_convert_fusion.1
  17.7 4.1 %packval.5 = bf16[16,504,128]{2,1,0:T(8,128)(2,1)} custom-call(s32[1]{0:T(128)} %bitcast.6.band_ref, s32[1]{0:T(128)} %bitcast.7.own_ref, bf16[2,2,3200,160]{3,2,1,0:T(8,128)(2,1)} %bitcast.35, bf16[16,504,128]{2,1,0:T(8,128)(2,1)} %collective-permute-done.other_ref), custom_call_target="tpu_custom_call" | custom-call | bytes 8000000 | tf_op jit(solution)/shard_map/packval/pallas_call | solution.py:111
  21.8 15.1 %all-to-all-done.1 = bf16[16,504,128]{2,1,0:T(8,128)(2,1)} async-done(((bf16[16,504,128]{2,1,0:T(8,128)(2,1)}), bf16[16,504,128]{2,1,0:T(8,128)(2,1)}, u32[]{:S(2)}, u32[]{:S(2)}) %all-to-all-start.1) | async-done | bytes 2064416 | tf_op jit(solution)/shard_map/all_to_all | solution.py:276
  37.0 7.9 %all-to-all-start.2 = ((bf16[16,504,128]{2,1,0:T(8,128)(2,1)}), bf16[16,504,128]{2,1,0:T(8,128)(2,1)S(1)}, u32[]{:S(2)}, u32[]{:S(2)}) async-start(bf16[16,504,128]{2,1,0:T(8,128)(2,1)} %packval.5), calls=%async_computation.2 | async-start | bytes 4128768 | tf_op jit(solution)/shard_map/all_to_all | solution.py:285
  47.2 21.9 %all-to-all-done.2 = bf16[16,504,128]{2,1,0:T(8,128)(2,1)S(1)} async-done(((bf16[16,504,128]{2,1,0:T(8,128)(2,1)}), bf16[16,504,128]{2,1,0:T(8,128)(2,1)S(1)}, u32[]{:S(2)}, u32[]{:S(2)}) %all-to-all-start.2) | async-done | bytes 2064416 | tf_op jit(solution)/shard_map/all_to_all | solution.py:285
  69.1 13.0 %conditional.1 = (bf16[256,512]{1,0:T(8,128)(2,1)}) conditional(s32[]{:T(128)} %convert_element_type.67, (s32[]{:T(128)}, bf16[16,504,128]{2,1,0:T(8,128)(2,1)S(1)}, s32[1]{0:T(128)}, bf16[16,504,128]{2,1,0:T(8,128)(2,1)}, bf16[96,768]{1,0:T(8,128)(2,1)}, /*index=5*/bf16[4,256,256]{1,0,2:T(4,128)(2,1)S(1)}) %tuple.15, (s32[]{:T(128)}, s32[]{:T(128)}, ...), branch_computations={%region_0.1_spmd, %region_1.2_spmd} | conditional | flops 7 | bytes 16347792 | solution.py:304
  70.1 12.1 %ztransform.2 = bf16[256,512]{1,0:T(8,128)(2,1)} custom-call(s32[1]{0:T(128)} %get-tuple-element.40.chip_ref, bf16[16,504,128]{2,1,0:T(8,128)(2,1)S(1)} %get-tuple-element.41.v0_ref, bf16[2,504,128]{2,1,0:T(8,128)(2,1)S(1)} %constant_dynamic-slice_fusion.v1_ref, bf16[16,504,128]{2,1,0:T(8,128)(2,1)} %get-tuple-element.43.cond_ref, ...), custom_call_target="tpu_custom_call" | custom-call | tf_op jit(solution)/shard_map/cond/branch_0_fun/ztransform/pallas_call | solution.py:202
  82.1 1.8 %gelements.3 = bf16[8,128,256]{2,1,0:T(8,128)(2,1)S(1)} custom-call(s32[1]{0:T(128)} %bitcast.21.parity_ref, bf16[256,512]{1,0:T(8,128)(2,1)} %get-tuple-element.110.plane_ref, s32[8,2,1,256]{3,2,1,0:T(1,128)S(1)} %bitcast.32, f32[8,2,4,256]{3,2,1,0:T(4,128)S(1)} %bitcast.30), custom_call_target="tpu_custom_call" | custom-call | flops 2000000000 | bytes 12000000 | tf_op jit(solution)/shard_map/gelements/pallas_call | solution.py:248
  84.1 1.8 %gelements.2 = f32[8,128,256]{2,1,0:T(8,128)S(1)} custom-call(s32[1]{0:T(128)} %bitcast.2.parity_ref, bf16[256,512]{1,0:T(8,128)(2,1)} %get-tuple-element.110.plane_ref, s32[8,2,1,256]{3,2,1,0:T(1,128)S(1)} %bitcast.33, f32[8,2,4,256]{3,2,1,0:T(4,128)S(1)} %bitcast.31), custom_call_target="tpu_custom_call" | custom-call | flops 2000000000 | bytes 12000000 | tf_op jit(solution)/shard_map/gelements/pallas_call | solution.py:248
  86.9 6.9 %all-to-all-start.3 = ((bf16[8,128,256]{2,1,0:T(8,128)(2,1)}), bf16[8,128,256]{2,1,0:T(8,128)(2,1)S(1)}, u32[]{:S(2)}, u32[]{:S(2)}) async-start(bf16[8,128,256]{2,1,0:T(8,128)(2,1)} %add_convert_fusion), calls=%async_computation.3 | async-start | bytes 1048576 | tf_op jit(solution)/shard_map/all_to_all | solution.py:331
  94.6 1.2 convert_reduce_fusion.1
  95.8 9.2 %all-to-all-done.3 = bf16[8,128,256]{2,1,0:T(8,128)(2,1)S(1)} async-done(((bf16[8,128,256]{2,1,0:T(8,128)(2,1)}), bf16[8,128,256]{2,1,0:T(8,128)(2,1)S(1)}, u32[]{:S(2)}, u32[]{:S(2)}) %all-to-all-start.3) | async-done | bytes 524320 | tf_op jit(solution)/shard_map/all_to_all | solution.py:331
  105.1 2.3 %collective-permute-start.2 = (bf16[128,256]{1,0:T(8,128)(2,1)S(1)}, bf16[128,256]{1,0:T(8,128)(2,1)S(1)}, u32[]{:S(2)}, u32[]{:S(2)}) collective-permute-start(bf16[128,256]{1,0:T(8,128)(2,1)S(1)} %convert_element_type.74), channel_id=1, source_target_pairs={{0,16},{8,24},{16,0},{24,8},{32,48},{40,56},{48,32},{56,40},{64,80... | collective-permute-start | bytes 196616 | tf_op jit(solution)/shard_map/ppermute | solution.py:333
  107.6 2.1 %collective-permute-done.2 = bf16[128,256]{1,0:T(8,128)(2,1)S(1)} collective-permute-done((bf16[128,256]{1,0:T(8,128)(2,1)S(1)}, bf16[128,256]{1,0:T(8,128)(2,1)S(1)}, u32[]{:S(2)}, u32[]{:S(2)}) %collective-permute-start.2) | collective-permute-done | bytes 65568 | tf_op jit(solution)/shard_map/ppermute | solution.py:333
  109.7 3.1 %collective-permute-start.5 = (bf16[128,256]{1,0:T(8,128)(2,1)S(1)}, bf16[128,256]{1,0:T(8,128)(2,1)S(1)}, u32[]{:S(2)}, u32[]{:S(2)}) collective-permute-start(bf16[128,256]{1,0:T(8,128)(2,1)S(1)} %fusion.3), channel_id=1, source_target_pairs={{0,96},{8,104},{16,112},{24,120},{32,0},{40,8},{48,16},{56,24},{64... | collective-permute-start | bytes 196616 | tf_op jit(solution)/shard_map/ppermute | solution.py:337
  112.7 2.7 %collective-permute-start.4 = (bf16[128,256]{1,0:T(8,128)(2,1)S(1)}, bf16[128,256]{1,0:T(8,128)(2,1)S(1)}, u32[]{:S(2)}, u32[]{:S(2)}) collective-permute-start(bf16[128,256]{1,0:T(8,128)(2,1)S(1)} %fusion.3), channel_id=1, source_target_pairs={{0,64},{8,72},{16,80},{24,88},{32,96},{40,104},{48,112},{56,120},{... | collective-permute-start | bytes 196616 | tf_op jit(solution)/shard_map/ppermute | solution.py:337
  116.3 2.2 %collective-permute-done.4 = bf16[128,256]{1,0:T(8,128)(2,1)S(1)} collective-permute-done((bf16[128,256]{1,0:T(8,128)(2,1)S(1)}, bf16[128,256]{1,0:T(8,128)(2,1)S(1)}, u32[]{:S(2)}, u32[]{:S(2)}) %collective-permute-start.4) | collective-permute-done | bytes 65568 | tf_op jit(solution)/shard_map/ppermute | solution.py:337
  118.5 1.2 collective-permute-done.3
  119.8 3.7 %collective-permute-start.7 = (bf16[128,256]{1,0:T(8,128)(2,1)S(1)}, bf16[128,256]{1,0:T(8,128)(2,1)S(1)}, u32[]{:S(2)}, u32[]{:S(2)}) collective-permute-start(bf16[128,256]{1,0:T(8,128)(2,1)S(1)} %add_convert_fusion.1), channel_id=1, source_target_pairs={{0,0},{1,16},{2,32},{3,48},{4,64},{5,80},{6,96},{7,112},{8,8},{9,2... | collective-permute-start | bytes 196616 | tf_op jit(solution)/shard_map/ppermute | solution.py:344
  123.6 7.3 %collective-permute-done.7 = bf16[128,256]{1,0:T(8,128)(2,1)S(1)} collective-permute-done((bf16[128,256]{1,0:T(8,128)(2,1)S(1)}, bf16[128,256]{1,0:T(8,128)(2,1)S(1)}, u32[]{:S(2)}, u32[]{:S(2)}) %collective-permute-start.7) | collective-permute-done | bytes 65568 | tf_op jit(solution)/shard_map/ppermute | solution.py:344
  131.9 1.0 pad_maximum_fusion
  (48 shorter events, 7.5 us)
Async XLA Ops:
  0.0 93.9 %copy-start = (f32[32]{0:T(128)S(1)}, f32[32]{0:T(128)}, u32[]{:S(2)}) copy-start(f32[32]{0:T(128)} %param.14) | copy-start | bytes 388
  6.6 5.9 %copy-start.3 = (s32[2]{0:T(128)S(1)}, s32[2]{0:T(128)}, u32[]{:S(2)}) copy-start(s32[2]{0:T(128)} %param.17) | copy-start | bytes 28
  6.7 9.2 %copy-start.2 = (s32[3,4096]{1,0:T(4,128)S(1)}, s32[3,4096]{1,0:T(4,128)}, u32[]{:S(2)}) copy-start(s32[3,4096]{1,0:T(4,128)} %param.18) | copy-start | bytes 147460
  6.7 11.1 %collective-permute-start = (bf16[16,504,128]{2,1,0:T(8,128)(2,1)S(1)}, bf16[16,504,128]{2,1,0:T(8,128)(2,1)}, u32[]{:S(2)}, u32[]{:S(2)}) collective-permute-start(bf16[16,504,128]{2,1,0:T(8,128)(2,1)S(1)} %packval.4), channel_id=1, source_target_pairs={{0,8},{8,0},{16,24},{24,16},{32,40},{40,32},{48,56},{56,48},{64,72... | collective-permute-start | bytes 6193160 | tf_op jit(solution)/shard_map/ppermute | solution.py:281
  6.8 30.2 %all-to-all-start.1 = ((bf16[16,504,128]{2,1,0:T(8,128)(2,1)}), bf16[16,504,128]{2,1,0:T(8,128)(2,1)}, u32[]{:S(2)}, u32[]{:S(2)}) async-start(bf16[16,504,128]{2,1,0:T(8,128)(2,1)} %packcond.1), calls=%async_computation.1 | async-start | bytes 4128768 | tf_op jit(solution)/shard_map/all_to_all | solution.py:276
  37.0 32.2 %all-to-all-start.2 = ((bf16[16,504,128]{2,1,0:T(8,128)(2,1)}), bf16[16,504,128]{2,1,0:T(8,128)(2,1)S(1)}, u32[]{:S(2)}, u32[]{:S(2)}) async-start(bf16[16,504,128]{2,1,0:T(8,128)(2,1)} %packval.5), calls=%async_computation.2 | async-start | bytes 4128768 | tf_op jit(solution)/shard_map/all_to_all | solution.py:285
  83.9 2.0 %collective-permute-start.1 = (bf16[8,128,256]{2,1,0:T(8,128)(2,1)S(1)}, bf16[8,128,256]{2,1,0:T(8,128)(2,1)S(1)}, u32[]{:S(2)}, u32[]{:S(2)}) collective-permute-start(bf16[8,128,256]{2,1,0:T(8,128)(2,1)S(1)} %gelements.3), channel_id=1, source_target_pairs={{0,8},{8,0},{16,24},{24,16},{32,40},{40,32},{48,56},{56,48},{64,72... | collective-permute-start | bytes 1572872 | tf_op jit(solution)/shard_map/ppermute | solution.py:328
  85.9 21.5 %copy-start.4 = (f32[16]{0:T(128)S(1)}, f32[16]{0:T(128)}, u32[]{:S(2)}) copy-start(f32[16]{0:T(128)} %param.15) | copy-start | bytes 196
  86.9 18.2 %all-to-all-start.3 = ((bf16[8,128,256]{2,1,0:T(8,128)(2,1)}), bf16[8,128,256]{2,1,0:T(8,128)(2,1)S(1)}, u32[]{:S(2)}, u32[]{:S(2)}) async-start(bf16[8,128,256]{2,1,0:T(8,128)(2,1)} %add_convert_fusion), calls=%async_computation.3 | async-start | bytes 1048576 | tf_op jit(solution)/shard_map/all_to_all | solution.py:331
  105.1 4.5 %collective-permute-start.2 = (bf16[128,256]{1,0:T(8,128)(2,1)S(1)}, bf16[128,256]{1,0:T(8,128)(2,1)S(1)}, u32[]{:S(2)}, u32[]{:S(2)}) collective-permute-start(bf16[128,256]{1,0:T(8,128)(2,1)S(1)} %convert_element_type.74), channel_id=1, source_target_pairs={{0,16},{8,24},{16,0},{24,8},{32,48},{40,56},{48,32},{56,40},{64,80... | collective-permute-start | bytes 196616 | tf_op jit(solution)/shard_map/ppermute | solution.py:333
  109.7 6.7 %collective-permute-start.5 = (bf16[128,256]{1,0:T(8,128)(2,1)S(1)}, bf16[128,256]{1,0:T(8,128)(2,1)S(1)}, u32[]{:S(2)}, u32[]{:S(2)}) collective-permute-start(bf16[128,256]{1,0:T(8,128)(2,1)S(1)} %fusion.3), channel_id=1, source_target_pairs={{0,96},{8,104},{16,112},{24,120},{32,0},{40,8},{48,16},{56,24},{64... | collective-permute-start | bytes 196616 | tf_op jit(solution)/shard_map/ppermute | solution.py:337
  112.7 5.8 %collective-permute-start.4 = (bf16[128,256]{1,0:T(8,128)(2,1)S(1)}, bf16[128,256]{1,0:T(8,128)(2,1)S(1)}, u32[]{:S(2)}, u32[]{:S(2)}) collective-permute-start(bf16[128,256]{1,0:T(8,128)(2,1)S(1)} %fusion.3), channel_id=1, source_target_pairs={{0,64},{8,72},{16,80},{24,88},{32,96},{40,104},{48,112},{56,120},{... | collective-permute-start | bytes 196616 | tf_op jit(solution)/shard_map/ppermute | solution.py:337
  115.4 4.3 %collective-permute-start.3 = (bf16[128,256]{1,0:T(8,128)(2,1)S(1)}, bf16[128,256]{1,0:T(8,128)(2,1)S(1)}, u32[]{:S(2)}, u32[]{:S(2)}) collective-permute-start(bf16[128,256]{1,0:T(8,128)(2,1)S(1)} %fusion.3), channel_id=1, source_target_pairs={{0,32},{8,40},{16,48},{24,56},{32,64},{40,72},{48,80},{56,88},{64,... | collective-permute-start | bytes 196616 | tf_op jit(solution)/shard_map/ppermute | solution.py:337
  119.8 11.1 %collective-permute-start.7 = (bf16[128,256]{1,0:T(8,128)(2,1)S(1)}, bf16[128,256]{1,0:T(8,128)(2,1)S(1)}, u32[]{:S(2)}, u32[]{:S(2)}) collective-permute-start(bf16[128,256]{1,0:T(8,128)(2,1)S(1)} %add_convert_fusion.1), channel_id=1, source_target_pairs={{0,0},{1,16},{2,32},{3,48},{4,64},{5,80},{6,96},{7,112},{8,8},{9,2... | collective-permute-start | bytes 196616 | tf_op jit(solution)/shard_map/ppermute | solution.py:344
  123.5 7.4 %collective-permute-start.6 = (bf16[128,256]{1,0:T(8,128)(2,1)S(1)}, bf16[128,256]{1,0:T(8,128)(2,1)S(1)}, u32[]{:S(2)}, u32[]{:S(2)}) collective-permute-start(bf16[128,256]{1,0:T(8,128)(2,1)S(1)} %add_convert_fusion.1), channel_id=1, source_target_pairs={{0,8},{8,0},{16,24},{24,16},{32,40},{40,32},{48,56},{56,48},{64,72... | collective-permute-start | bytes 196616 | tf_op jit(solution)/shard_map/ppermute | solution.py:345

commit v3 on v2

--- a/solution.py
+++ b/solution.py
@@ -55,6 +55,10 @@
     return out.reshape(4, 256, 128).astype(jnp.bfloat16)
 
 
+def in_hbm(array):
+    return pltpu.with_memory_space_constraint(array, pltpu.HBM)
+
+
 def pack_band(src, out, fill):
     real, imag = src[0], src[1]
     out[0:ROWS] = real[:, :128]
@@ -74,7 +78,7 @@
 def pack_cond(conduction, number):
     return pl.pallas_call(
         pack_cond_kernel,
-        out_shape=jax.ShapeDtypeStruct((PARTS, WIRE, 128), BF),
+        out_shape=pltpu.HBM((PARTS, WIRE, 128), BF),
         grid_spec=pltpu.PrefetchScalarGridSpec(
             num_scalar_prefetch=1,
             grid=(PARTS // PACK,),
@@ -82,6 +86,7 @@
             out_specs=pl.BlockSpec((PACK, WIRE, 128), lambda t, n: (t, 0, 0)),
         ),
         cost_estimate=pl.CostEstimate(flops=0, transcendentals=0, bytes_accessed=6_000_000),
+        compiler_params=pltpu.CompilerParams(vmem_limit_bytes=14 * 2**20),
         name="packcond",
     )(number, conduction)
 
@@ -91,36 +96,55 @@
         pack_band(val_ref.at[0, :, pl.ds(t * ROWS, ROWS)], out_ref.at[t], 0.0)
 
 
-def pack_choice_kernel(band_ref, own_ref, val_ref, other_ref, out_ref):
+def pack_choice_kernel(band_ref, own_ref, val_ref, *refs):
+    out_ref = refs[-1]
+
     @pl.when(own_ref[0] == 1)
     def _():
         pack_val_kernel(band_ref, val_ref, out_ref)
 
-    @pl.when(own_ref[0] == 0)
-    def _():
-        out_ref[...] = other_ref[...]
-
-
-def pack_val(valence, band, own=None, other=None):
-    wire_spec = pl.BlockSpec((PACK, WIRE, 128), lambda t, *_: (t, 0, 0))
-    scalars, arrays, specs, kernel = (band,), (valence,), [], pack_val_kernel
-    specs.append(pl.BlockSpec((1, 2, PACK * ROWS, LENGTH), lambda t, k, *_: (k[0], 0, t, 0)))
-    if other is not None:
-        scalars, arrays, kernel = (band, own), (valence, other), pack_choice_kernel
-        specs.append(wire_spec)
-    return pl.pallas_call(
-        kernel,
-        out_shape=jax.ShapeDtypeStruct((PARTS, WIRE, 128), BF),
-        grid_spec=pltpu.PrefetchScalarGridSpec(
-            num_scalar_prefetch=len(scalars),
+    for t in range(PARTS // PACK):
+
+        @pl.when((own_ref[0] == 0) & (pl.program_id(0) == t))
+        def _():
+            out_ref[...] = refs[t][...]
+
+
+WIRE_BLOCK = (PACK, WIRE, 128)
+VAL_BLOCK = (1, 2, PACK * ROWS, LENGTH)
+
+
+def pack_give(valence, band, t):
+    return pl.pallas_call(
+        pack_val_kernel,
+        out_shape=jax.ShapeDtypeStruct(WIRE_BLOCK, BF),
+        grid_spec=pltpu.PrefetchScalarGridSpec(
+            num_scalar_prefetch=1,
+            grid=(1,),
+            in_specs=[pl.BlockSpec(VAL_BLOCK, lambda i, k: (k[0], 0, t, 0))],
+            out_specs=pl.BlockSpec(WIRE_BLOCK, lambda i, k: (0, 0, 0)),
+        ),
+        cost_estimate=pl.CostEstimate(flops=0, transcendentals=0, bytes_accessed=3_000_000),
+        compiler_params=pltpu.CompilerParams(vmem_limit_bytes=14 * 2**20),
+        name="packgive",
+    )(band, valence)
+
+
+def pack_choice(valence, band, own, others):
+    return pl.pallas_call(
+        pack_choice_kernel,
+        out_shape=pltpu.HBM((PARTS, WIRE, 128), BF),
+        grid_spec=pltpu.PrefetchScalarGridSpec(
+            num_scalar_prefetch=2,
             grid=(PARTS // PACK,),
-            in_specs=specs,
-            out_specs=wire_spec,
+            in_specs=[pl.BlockSpec(VAL_BLOCK, lambda t, k, o: (k[0], 0, t, 0))]
+            + [pl.BlockSpec(WIRE_BLOCK, lambda t, k, o: (0, 0, 0)) for _ in others],
+            out_specs=pl.BlockSpec(WIRE_BLOCK, lambda t, k, o: (t, 0, 0)),
         ),
         cost_estimate=pl.CostEstimate(flops=0, transcendentals=0, bytes_accessed=8_000_000),
-        compiler_params=pltpu.CompilerParams(vmem_limit_bytes=40 * 2**20),
-        name="packval",
-    )(*scalars, *arrays)
+        compiler_params=pltpu.CompilerParams(vmem_limit_bytes=16 * 2**20),
+        name="packchoice",
+    )(band, own, valence, *others)
 
 
 def unpack_tail(tail):
@@ -133,18 +157,26 @@
     return jnp.pad(jnp.tile(tab, (1, 1, SLOTS)), ((0, 0), (0, 0), (0, 256 - SLOTS * SIDE)))
 
 
-def z_kernel(chip_ref, v0_ref, v1_ref, cond_ref, table_ref, ytab_ref, out_ref, val_main, val_tail, low_ref, high_ref):
+def z_kernel(where_ref, v0_ref, v1_ref, again_ref, cond_ref, table_ref, ytab_ref, out_ref, val_main, val_tail, low_ref, high_ref):
     step = pl.program_id(0)
+
+    def take(i, src):
+        val_main[i, 0] = src[0:ROWS].astype(F32)
+        val_main[i, 1] = src[ROWS : 2 * ROWS].astype(F32)
+        both = unpack_tail(src[2 * ROWS :].astype(F32))
+        val_tail[i] = jnp.concatenate([both, both], axis=1)
 
     @pl.when(step == 0)
     def _():
-        for i in range(4):
-            src = (v0_ref if i < 2 else v1_ref).at[i % 2]
-            val_main[i, 0] = src[0:ROWS].astype(F32)
-            val_main[i, 1] = src[ROWS : 2 * ROWS].astype(F32)
-            both = unpack_tail(src[2 * ROWS :].astype(F32))
-            val_tail[i] = jnp.concatenate([both, both], axis=1)
+        for j in range(2):
+            take(j, v0_ref.at[j])
+            take(2 + j, v1_ref.at[j])
         high_ref[...] = jnp.zeros_like(high_ref)
+
+    @pl.when((step == 0) & (where_ref[2] == 1))
+    def _():
+        for j in range(2):
+            take(2 + j, again_ref.at[j])
 
     @pl.loop(0, CONDS)
     def _(c):
@@ -194,7 +226,7 @@
                 out_ref[x * 128 + PAIRS : (x + 1) * 128, lanes] = (c[PAIRS:] - s[:PAIRS]).astype(BF)
 
 
-def z_transform(chip, val_wire, second, cond_wire, ytab):
+def z_transform(where, val_wire, again, cond_wire, ytab):
     single = z_table()
     table = np.zeros((4 * KROWS, 768), single.dtype)
     table[: 2 * KROWS, :384] = single
@@ -207,6 +239,7 @@
             grid=(PARTS // CONDS,),
             in_specs=[
                 pl.BlockSpec((2, WIRE, 128), lambda c, o: (o[0], 0, 0)),
+                pl.BlockSpec((2, WIRE, 128), lambda c, o: (o[1], 0, 0)),
                 pl.BlockSpec((2, WIRE, 128), lambda c, o: (0, 0, 0)),
                 pl.BlockSpec((CONDS, WIRE, 128), lambda c, o: (c, 0, 0)),
                 pl.BlockSpec((4 * KROWS, 768), lambda c, o: (0, 0)),
@@ -220,9 +253,9 @@
                 pltpu.VMEM((KROWS * 128, 128), F32),
             ],
         ),
-        compiler_params=pltpu.CompilerParams(vmem_limit_bytes=40 * 2**20),
+        compiler_params=pltpu.CompilerParams(vmem_limit_bytes=20 * 2**20),
         name="ztransform",
-    )(chip, val_wire, second, cond_wire, jnp.asarray(table), ytab)
+    )(where, val_wire, val_wire, again, cond_wire, jnp.asarray(table), ytab)
 
 
 def g_kernel(parity_ref, plane_ref, index_ref, phase_ref, out_ref):
@@ -258,10 +291,43 @@
             ],
             out_specs=pl.BlockSpec((chips, 128, GCHUNK), lambda i, k: (0, 0, 0)),
         ),
-        compiler_params=pltpu.CompilerParams(vmem_limit_bytes=40 * 2**20),
+        compiler_params=pltpu.CompilerParams(vmem_limit_bytes=10 * 2**20),
         cost_estimate=pl.CostEstimate(flops=2 * 10**9, transcendentals=0, bytes_accessed=12_000_000),
         name="gelements",
     )(parity, plane, index, phase)
+
+
+def chi_kernel(core_ref, mine_ref, other_ref, column_ref, weight_ref, out_ref):
+    real = column_ref[...].astype(F32) * weight_ref[...]
+    imag = jnp.concatenate([-real[PAIRS:], real[:PAIRS]], axis=0)
+    sides = []
+    for side in (real, imag):
+        top = side.astype(BF)
+        sides.append((top, (side - top.astype(F32)).astype(BF)))
+    for half, rows in ((core_ref[0], mine_ref[...]), (1 - core_ref[0], other_ref[...])):
+        at = pl.ds(pl.multiple_of(half * GCHUNK, GCHUNK), GCHUNK)
+        for part in range(2):
+            total = None
+            for piece in sides[part]:
+                term = lax.dot_general(rows, piece, (((0,), (0,)), ((), ())), preferred_element_type=F32)
+                total = term if total is None else total + term
+            out_ref[part, at, :] = total
+
+
+def chi_block(core, mine, other, column, weight):
+    spec = pl.BlockSpec((128, GCHUNK), lambda i, k: (0, 0))
+    return pl.pallas_call(
+        chi_kernel,
+        out_shape=jax.ShapeDtypeStruct((2, 2 * GCHUNK, GCHUNK), F32),
+        grid_spec=pltpu.PrefetchScalarGridSpec(
+            num_scalar_prefetch=1,
+            grid=(1,),
+            in_specs=[spec, spec, spec, pl.BlockSpec((128, 1), lambda i, k: (0, 0))],
+            out_specs=pl.BlockSpec((2, 2 * GCHUNK, GCHUNK), lambda i, k: (0, 0, 0)),
+        ),
+        compiler_params=pltpu.CompilerParams(vmem_limit_bytes=8 * 2**20),
+        name="chi",
+    )(core, mine, other, column, weight)
 
 
 def shards(valence, conduction, val_energy, cond_energy, cond_band, owners, gvectors):
@@ -271,37 +337,38 @@
     n_grid = lax.axis_size("grid")
 
     rows_all = x_local * LENGTH
-    cond_wire = pack_cond(conduction.reshape(2, rows_all, LENGTH), cond_band)
+    cond_wire = pack_cond(in_hbm(conduction.reshape(2, rows_all, LENGTH)), cond_band)
     cond_wire, core = lax.optimization_barrier((cond_wire, band_pos & 1))
     cond_wire = lax.all_to_all(cond_wire, "band", 0, 0, tiled=True)
 
     first, second = owners[0], owners[1]
-    bands = valence.reshape(2, 2, rows_all, LENGTH)
-    sibling = pack_val(bands, (1 - core)[None])
-    sibling = lax.ppermute(sibling, "band", [(b, b ^ 1) for b in range(PARTS)])
+    bands = in_hbm(valence.reshape(2, 2, rows_all, LENGTH))
+    siblings = [(b, b ^ 1) for b in range(PARTS)]
+    sibling = [
+        lax.ppermute(pack_give(bands, (1 - core)[None], t), "band", siblings) for t in range(PARTS // PACK)
+    ]
     here = (first >> 1) == (band_pos >> 1)
     own = jnp.where(here, first == band_pos, second == band_pos)
-    val_wire = pack_val(bands, core[None], own.astype(jnp.int32)[None], sibling)
+    val_wire = pack_choice(bands, core[None], own.astype(jnp.int32)[None], sibling)
     val_wire = lax.all_to_all(val_wire, "band", 0, 0, tiled=True)
     cond_wire, val_wire = lax.optimization_barrier((cond_wire, val_wire))
 
     ytab = plane_tables(band_pos & 3)
-    chip = (first >> 1)[None]
 
     def exchange_again(operands):
-        bands, sibling, val_wire, cond_wire, ytab = operands
-        again = pack_val(bands, core[None], (second == band_pos).astype(jnp.int32)[None], sibling)
+        bands, sibling = operands
+        again = pack_choice(bands, core[None], (second == band_pos).astype(jnp.int32)[None], sibling)
         again = lax.all_to_all(again, "band", 0, 0, tiled=True)
-        again = lax.dynamic_slice_in_dim(again, (second >> 1) * 2, 2, 0)
-        return z_transform(chip, val_wire, again, cond_wire, ytab)
-
-    def from_first(operands):
-        _, _, val_wire, cond_wire, ytab = operands
-        again = lax.dynamic_slice_in_dim(val_wire, (second >> 1) * 2, 2, 0)
-        return z_transform(chip, val_wire, again, cond_wire, ytab)
+        return lax.dynamic_slice_in_dim(again, (second >> 1) * 2, 2, 0)
+
+    def nothing_more(operands):
+        return jnp.zeros((2, WIRE, 128), BF)
 
     both = (first != second) & ((first >> 1) == (second >> 1))
-    plane = lax.cond(both, exchange_again, from_first, (bands, sibling, val_wire, cond_wire, ytab))
+    val_wire, both = lax.optimization_barrier((val_wire, both))
+    again = lax.cond(both, exchange_again, nothing_more, (bands, sibling))
+    where = jnp.stack([first >> 1, second >> 1, both.astype(jnp.int32)])
+    plane = z_transform(where, val_wire, again, in_hbm(cond_wire), ytab)
 
     numbers = cond_wire[:, WIRE - 1, 127].astype(jnp.int32)
     order = jnp.arange(cond_energy.shape[0], dtype=jnp.int32)
@@ -323,7 +390,6 @@
     phase = phase.reshape(4, PARTS, GCHUNK).transpose(1, 0, 2).reshape(PARTS // 2, 2, 4, GCHUNK)
 
     core = band_pos & 1
-    siblings = [(b, b ^ 1) for b in range(PARTS)]
     away = g_elements((1 - core)[None], plane, index, phase, BF)
     come = lax.ppermute(away, "band", siblings)
     keep = g_elements(core[None], plane, index, phase, F32)
@@ -341,19 +407,9 @@
     for b in range(PARTS):
         for g in range(n_grid):
             far.append((b * n_grid + g, (2 * g + b % 2) * n_grid + b // 2))
-    column = lax.ppermute(narrow, ("band", "grid"), far).astype(F32)
+    column = lax.ppermute(narrow, ("band", "grid"), far)
     other = lax.ppermute(narrow, "band", siblings)
-    left = jnp.where(core == 1, other, narrow)
-    right = jnp.where(core == 1, narrow, other)
-    rows = jnp.concatenate([left, right], axis=1).astype(F32)
-
-    w2 = jnp.concatenate([weight, weight])[:, None]
-    for_real = column * w2
-    for_imag = jnp.concatenate([-for_real[PAIRS:], for_real[:PAIRS]], axis=0)
-    high = lax.Precision.HIGHEST
-    chi_re = jnp.einsum("pr,pc->rc", rows, for_real, precision=high)
-    chi_im = jnp.einsum("pr,pc->rc", rows, for_imag, precision=high)
-    return jnp.stack([chi_re, chi_im])
+    return chi_block(core[None], narrow, other, column, jnp.concatenate([weight, weight])[:, None])
 
 
 def solution(mesh):

time: 134 us -> 130 us (0.970)
  waiting for transfers between devices: 59.7 us -> 57.2 us
    all_to_all x1, waiting for transfers between devices: 15.1 us -> 11.1 us  [shards(): cond_wire = lax.all_to_all(cond_wire, 'band', 0, 0, tiled=True)]
    pallas_call x3 -> x5, Pallas kernels: 10.1 us -> 12.5 us  [the longest x2 3.8 us: pack_give(): pl.pallas_call(pack_val_kernel, out_shape=jax.ShapeDtypeStruct(WIRE_BLOCK...]
    pallas_call x2, Pallas kernels: 3.6 us -> 1.74 us  [g_elements(): pl.pallas_call(g_kernel, out_shape=jax.ShapeDtypeStruct((chips, 128, GCHU...]
    ppermute x2 -> x3, waiting for transfers between devices: 7.27 us -> 8.21 us  [the longest x1 8.21 us: shards(): column = lax.ppermute(narrow, ('band', 'grid'), far)]
    ppermute x2 -> x3, starting transfers between devices: 3.78 us -> 4.26 us  [the longest x1 3.59 us: shards(): column = lax.ppermute(narrow, ('band', 'grid'), far)]
  transfers between devices with their start and end apart: 11 -> 12, of which waited for: 8 -> 9; matrix products, arithmetic and copies ran while one was open for 5% -> 5% of each run, Pallas kernels for 4% -> 6%
where the time goes in v3:
time: 130 us; the launch traced here: 129 us
  waiting for transfers between devices  57.2 us (44%)
  starting transfers between devices  33 us (25%)
  Pallas kernels  26.2 us (20%)
  other arithmetic  4.84 us (4%)
  between operations  4.42 us (3%)
  local copies, waits for them, and re-layouts  3.8 us (3%)
    all_to_all x1, waiting for transfers between devices, shards(): val_wire = lax.all_to_all(val_wire, 'band', 0, 0, tiled=True)  21.7 us
    pallas_call x1, Pallas kernels, z_transform(): pl.pallas_call(z_kernel, out_shape=jax.ShapeDtypeStruct((256, 512), BF),...  12 us
    all_to_all x1, waiting for transfers between devices, shards(): cond_wire = lax.all_to_all(cond_wire, 'band', 0, 0, tiled=True)  11.1 us
    all_to_all x1, waiting for transfers between devices, shards(): parts = lax.all_to_all(parts, 'grid', 0, 0, tiled=True)  9.16 us
    ppermute x1, waiting for transfers between devices, shards(): column = lax.ppermute(narrow, ('band', 'grid'), far)  8.21 us
    all_to_all x1, starting transfers between devices, shards(): val_wire = lax.all_to_all(val_wire, 'band', 0, 0, tiled=True)  7.86 us
    all_to_all x1, starting transfers between devices, shards(): parts = lax.all_to_all(parts, 'grid', 0, 0, tiled=True)  6.89 us
    ppermute x3, starting transfers between devices, shards(): block = block + lax.ppermute(narrow, 'band', step).astype(F32)  5.75 us
  transfers between devices with their start and end apart: 12, of which 9 were waited for; matrix products, arithmetic and copies ran while one was open for 5% of the time, Pallas kernels for 6%

profile of v3, /device:TPU:38, one launch (start us, length us, event | category | flops | bytes accessed | tf_op | source)
XLA Modules:
  0.0 129.5 jit_solution(13069671541957607827)
XLA Ops:
  0.7 3.5 %packcond.1 = bf16[16,504,128]{2,1,0:T(8,128)(2,1)} custom-call(s32[1]{0:T(128)S(6)} %copy.31.number_ref, bf16[2,3200,160]{2,1,0:T(8,128)(2,1)} %bitcast.38), custom_call_target="tpu_custom_call" | custom-call | bytes 6000000 | tf_op jit(solution)/shard_map/packcond/pallas_call | solution.py:79
  4.2 5.7 %all-to-all-start.1 = ((bf16[16,504,128]{2,1,0:T(8,128)(2,1)}), bf16[16,504,128]{2,1,0:T(8,128)(2,1)}, u32[]{:S(2)}, u32[]{:S(2)}) async-start(bf16[16,504,128]{2,1,0:T(8,128)(2,1)} %packcond.1), calls=%async_computation.1 | async-start | bytes 4128768 | tf_op jit(solution)/shard_map/all_to_all | solution.py:342
  9.9 1.9 %packgive.2 = bf16[8,504,128]{2,1,0:T(8,128)(2,1)S(1)} custom-call(s32[1]{0:T(128)} %bitcast.11.band_ref, bf16[2,2,3200,160]{3,2,1,0:T(8,128)(2,1)} %bitcast.34), custom_call_target="tpu_custom_call" | custom-call | bytes 3000000 | tf_op jit(solution)/shard_map/packgive/pallas_call | solution.py:118
  12.1 1.9 %packgive.3 = bf16[8,504,128]{2,1,0:T(8,128)(2,1)S(1)} custom-call(s32[1]{0:T(128)} %bitcast.11.band_ref, bf16[2,2,3200,160]{3,2,1,0:T(8,128)(2,1)} %bitcast.35), custom_call_target="tpu_custom_call" | custom-call | bytes 3000000 | tf_op jit(solution)/shard_map/packgive/pallas_call | solution.py:118
  14.4 1.0 cosine_convert_fusion.1
  19.5 3.7 %packchoice.3 = bf16[16,504,128]{2,1,0:T(8,128)(2,1)} custom-call(s32[1]{0:T(128)} %bitcast.8.band_ref, s32[1]{0:T(128)} %bitcast.9.own_ref, bf16[2,2,3200,160]{3,2,1,0:T(8,128)(2,1)} %bitcast.36, bf16[8,504,128]{2,1,0:T(8,128)(2,1)S(1)} %collective-permute-done.refs_0_, bf16[8,504,128]{2,1,0:T(8,128)(2,1)} %collective-permute-done.1.refs_1_), custom_call_target="tpu_custom_call" | custom-call | bytes 8000000 | tf_op jit(solution)/shard_map/packchoice/pallas_call | solution.py:134
  23.2 11.1 %all-to-all-done.1.cond_ref = bf16[16,504,128]{2,1,0:T(8,128)(2,1)} async-done(((bf16[16,504,128]{2,1,0:T(8,128)(2,1)}), bf16[16,504,128]{2,1,0:T(8,128)(2,1)}, u32[]{:S(2)}, u32[]{:S(2)}) %all-to-all-start.1) | async-done | bytes 2064416 | tf_op jit(solution)/shard_map/all_to_all | solution.py:342
  34.3 7.9 %all-to-all-start.2 = ((bf16[16,504,128]{2,1,0:T(8,128)(2,1)}), bf16[16,504,128]{2,1,0:T(8,128)(2,1)S(1)}, u32[]{:S(2)}, u32[]{:S(2)}) async-start(bf16[16,504,128]{2,1,0:T(8,128)(2,1)} %packchoice.3), calls=%async_computation.2 | async-start | bytes 4128768 | tf_op jit(solution)/shard_map/all_to_all | solution.py:353
  44.8 21.7 %all-to-all-done.2.v0_ref.v1_ref = bf16[16,504,128]{2,1,0:T(8,128)(2,1)S(1)} async-done(((bf16[16,504,128]{2,1,0:T(8,128)(2,1)}), bf16[16,504,128]{2,1,0:T(8,128)(2,1)S(1)}, u32[]{:S(2)}, u32[]{:S(2)}) %all-to-all-start.2) | async-done | bytes 2064416 | tf_op jit(solution)/shard_map/all_to_all | solution.py:353
  67.4 12.0 %ztransform.1.plane_ref = bf16[256,512]{1,0:T(8,128)(2,1)S(1)} custom-call(s32[3]{0:T(128)S(1)} %pad_add_fusion.where_ref, bf16[16,504,128]{2,1,0:T(8,128)(2,1)S(1)} %all-to-all-done.2.v0_ref.v1_ref, bf16[16,504,128]{2,1,0:T(8,128)(2,1)S(1)} %all-to-all-done.2.v0_ref.v1_ref, bf16[2,504,128]{2,1,0:T(8,128)(2,1)S(1)} %get-tuple-element.48.again_ref, ...), custom_call_target="tpu_custom_call" | custom-call | tf_op jit(solution)/shard_map/ztransform/pallas_call | solution.py:234
  81.3 1.0 collective-permute-done.2
  82.3 0.9 add_convert_fusion
  83.2 6.9 %all-to-all-start.3 = ((bf16[8,128,256]{2,1,0:T(8,128)(2,1)}), bf16[8,128,256]{2,1,0:T(8,128)(2,1)S(1)}, u32[]{:S(2)}, u32[]{:S(2)}) async-start(bf16[8,128,256]{2,1,0:T(8,128)(2,1)} %add_convert_fusion), calls=%async_computation.3 | async-start | bytes 1048576 | tf_op jit(solution)/shard_map/all_to_all | solution.py:397
  90.9 1.2 convert_reduce_fusion.1
  92.1 9.2 %all-to-all-done.3 = bf16[8,128,256]{2,1,0:T(8,128)(2,1)S(1)} async-done(((bf16[8,128,256]{2,1,0:T(8,128)(2,1)}), bf16[8,128,256]{2,1,0:T(8,128)(2,1)S(1)}, u32[]{:S(2)}, u32[]{:S(2)}) %all-to-all-start.3) | async-done | bytes 524320 | tf_op jit(solution)/shard_map/all_to_all | solution.py:397
  101.4 2.3 %collective-permute-start.3 = (bf16[128,256]{1,0:T(8,128)(2,1)S(1)}, bf16[128,256]{1,0:T(8,128)(2,1)S(1)}, u32[]{:S(2)}, u32[]{:S(2)}) collective-permute-start(bf16[128,256]{1,0:T(8,128)(2,1)S(1)} %convert_element_type.71), channel_id=1, source_target_pairs={{0,16},{8,24},{16,0},{24,8},{32,48},{40,56},{48,32},{56,40},{64,80... | collective-permute-start | bytes 196616 | tf_op jit(solution)/shard_map/ppermute | solution.py:399
  103.9 2.1 %collective-permute-done.3 = bf16[128,256]{1,0:T(8,128)(2,1)S(1)} collective-permute-done((bf16[128,256]{1,0:T(8,128)(2,1)S(1)}, bf16[128,256]{1,0:T(8,128)(2,1)S(1)}, u32[]{:S(2)}, u32[]{:S(2)}) %collective-permute-start.3) | collective-permute-done | bytes 65568 | tf_op jit(solution)/shard_map/ppermute | solution.py:399
  105.9 3.0 %collective-permute-start.6 = (bf16[128,256]{1,0:T(8,128)(2,1)S(1)}, bf16[128,256]{1,0:T(8,128)(2,1)S(1)}, u32[]{:S(2)}, u32[]{:S(2)}) collective-permute-start(bf16[128,256]{1,0:T(8,128)(2,1)S(1)} %fusion), channel_id=1, source_target_pairs={{0,96},{8,104},{16,112},{24,120},{32,0},{40,8},{48,16},{56,24},{64... | collective-permute-start | bytes 196616 | tf_op jit(solution)/shard_map/ppermute | solution.py:403
  108.9 2.7 %collective-permute-start.5 = (bf16[128,256]{1,0:T(8,128)(2,1)S(1)}, bf16[128,256]{1,0:T(8,128)(2,1)S(1)}, u32[]{:S(2)}, u32[]{:S(2)}) collective-permute-start(bf16[128,256]{1,0:T(8,128)(2,1)S(1)} %fusion), channel_id=1, source_target_pairs={{0,64},{8,72},{16,80},{24,88},{32,96},{40,104},{48,112},{56,120},{... | collective-permute-start | bytes 196616 | tf_op jit(solution)/shard_map/ppermute | solution.py:403
  112.5 2.2 %collective-permute-done.5 = bf16[128,256]{1,0:T(8,128)(2,1)S(1)} collective-permute-done((bf16[128,256]{1,0:T(8,128)(2,1)S(1)}, bf16[128,256]{1,0:T(8,128)(2,1)S(1)}, u32[]{:S(2)}, u32[]{:S(2)}) %collective-permute-start.5) | collective-permute-done | bytes 65568 | tf_op jit(solution)/shard_map/ppermute | solution.py:403
  114.7 1.2 collective-permute-done.4
  116.0 3.6 %collective-permute-start.8 = (bf16[128,256]{1,0:T(8,128)(2,1)S(1)}, bf16[128,256]{1,0:T(8,128)(2,1)S(1)}, u32[]{:S(2)}, u32[]{:S(2)}) collective-permute-start(bf16[128,256]{1,0:T(8,128)(2,1)S(1)} %add_convert_fusion.1.mine_ref), channel_id=1, source_target_pairs={{0,0},{1,16},{2,32},{3,48},{4,64},{5,80},{6,96},{7,112},{8,8},{9,2... | collective-permute-start | bytes 196616 | tf_op jit(solution)/shard_map/ppermute | solution.py:410
  119.8 8.2 %collective-permute-done.8.column_ref = bf16[128,256]{1,0:T(8,128)(2,1)S(1)} collective-permute-done((bf16[128,256]{1,0:T(8,128)(2,1)S(1)}, bf16[128,256]{1,0:T(8,128)(2,1)S(1)}, u32[]{:S(2)}, u32[]{:S(2)}) %collective-permute-start.8) | collective-permute-done | bytes 65568 | tf_op jit(solution)/shard_map/ppermute | solution.py:410
  128.0 1.5 %chi.1 = f32[2,512,256]{2,1,0:T(8,128)} custom-call(s32[1]{0:T(128)} %bitcast.2.parity_ref.core_ref, bf16[128,256]{1,0:T(8,128)(2,1)S(1)} %add_convert_fusion.1.mine_ref, bf16[128,256]{1,0:T(8,128)(2,1)S(1)} %collective-permute-done.7.other_ref, bf16[128,256]{1,0:T(8,128)(2,1)S(1)} %collective-permute-done.8.column_ref, f32[128,1]{1,0:T(8,128)S(1)} %copy.28.weight_ref), custom_call_target="tpu_custom_call" | custom-call | tf_op jit(solution)/shard_map/chi/pallas_call | solution.py:319
  (52 shorter events, 8.9 us)
Async XLA Ops:
  0.0 90.3 %copy-start = (f32[32]{0:T(128)S(1)}, f32[32]{0:T(128)}, u32[]{:S(2)}) copy-start(f32[32]{0:T(128)} %param.13) | copy-start | bytes 388
  4.2 30.1 %all-to-all-start.1 = ((bf16[16,504,128]{2,1,0:T(8,128)(2,1)}), bf16[16,504,128]{2,1,0:T(8,128)(2,1)}, u32[]{:S(2)}, u32[]{:S(2)}) async-start(bf16[16,504,128]{2,1,0:T(8,128)(2,1)} %packcond.1), calls=%async_computation.1 | async-start | bytes 4128768 | tf_op jit(solution)/shard_map/all_to_all | solution.py:342
  11.8 2.6 %copy-start.3 = (s32[3,4096]{1,0:T(4,128)S(1)}, s32[3,4096]{1,0:T(4,128)}, u32[]{:S(2)}) copy-start(s32[3,4096]{1,0:T(4,128)} %param.17) | copy-start | bytes 147460
  11.8 3.6 %copy-start.4 = (s32[2]{0:T(128)S(1)}, s32[2]{0:T(128)}, u32[]{:S(2)}) copy-start(s32[2]{0:T(128)} %param.16) | copy-start | bytes 28
  11.8 7.7 %collective-permute-start = (bf16[8,504,128]{2,1,0:T(8,128)(2,1)S(1)}, bf16[8,504,128]{2,1,0:T(8,128)(2,1)S(1)}, u32[]{:S(2)}, u32[]{:S(2)}) collective-permute-start(bf16[8,504,128]{2,1,0:T(8,128)(2,1)S(1)} %packgive.2), channel_id=1, source_target_pairs={{0,8},{8,0},{16,24},{24,16},{32,40},{40,32},{48,56},{56,48},{64,72... | collective-permute-start | bytes 3096584 | tf_op jit(solution)/shard_map/ppermute | solution.py:348
  14.0 5.6 %collective-permute-start.1 = (bf16[8,504,128]{2,1,0:T(8,128)(2,1)S(1)}, bf16[8,504,128]{2,1,0:T(8,128)(2,1)}, u32[]{:S(2)}, u32[]{:S(2)}) collective-permute-start(bf16[8,504,128]{2,1,0:T(8,128)(2,1)S(1)} %packgive.3), channel_id=1, source_target_pairs={{0,8},{8,0},{16,24},{24,16},{32,40},{40,32},{48,56},{56,48},{64,72... | collective-permute-start | bytes 3096584 | tf_op jit(solution)/shard_map/ppermute | solution.py:348
  19.5 3.7 %copy-start.2 = (bf16[8,504,128]{2,1,0:T(8,128)(2,1)}, bf16[8,504,128]{2,1,0:T(8,128)(2,1)S(1)}, u32[]{:S(2)}) copy-start(bf16[8,504,128]{2,1,0:T(8,128)(2,1)S(1)} %collective-permute-done.refs_0_) | copy-start | bytes 3096580
  34.3 32.2 %all-to-all-start.2 = ((bf16[16,504,128]{2,1,0:T(8,128)(2,1)}), bf16[16,504,128]{2,1,0:T(8,128)(2,1)S(1)}, u32[]{:S(2)}, u32[]{:S(2)}) async-start(bf16[16,504,128]{2,1,0:T(8,128)(2,1)} %packchoice.3), calls=%async_computation.2 | async-start | bytes 4128768 | tf_op jit(solution)/shard_map/all_to_all | solution.py:353
  66.5 0.9 copy-start.1
  80.3 2.0 %collective-permute-start.2 = (bf16[8,128,256]{2,1,0:T(8,128)(2,1)S(1)}, bf16[8,128,256]{2,1,0:T(8,128)(2,1)S(1)}, u32[]{:S(2)}, u32[]{:S(2)}) collective-permute-start(bf16[8,128,256]{2,1,0:T(8,128)(2,1)S(1)} %gelements.3), channel_id=1, source_target_pairs={{0,8},{8,0},{16,24},{24,16},{32,40},{40,32},{48,56},{56,48},{64,72... | collective-permute-start | bytes 1572872 | tf_op jit(solution)/shard_map/ppermute | solution.py:394
  81.3 22.4 %copy-start.5 = (f32[16]{0:T(128)S(1)}, f32[16]{0:T(128)}, u32[]{:S(2)}) copy-start(f32[16]{0:T(128)} %param.14) | copy-start | bytes 196
  83.2 18.1 %all-to-all-start.3 = ((bf16[8,128,256]{2,1,0:T(8,128)(2,1)}), bf16[8,128,256]{2,1,0:T(8,128)(2,1)S(1)}, u32[]{:S(2)}, u32[]{:S(2)}) async-start(bf16[8,128,256]{2,1,0:T(8,128)(2,1)} %add_convert_fusion), calls=%async_computation.3 | async-start | bytes 1048576 | tf_op jit(solution)/shard_map/all_to_all | solution.py:397
  101.4 4.5 %collective-permute-start.3 = (bf16[128,256]{1,0:T(8,128)(2,1)S(1)}, bf16[128,256]{1,0:T(8,128)(2,1)S(1)}, u32[]{:S(2)}, u32[]{:S(2)}) collective-permute-start(bf16[128,256]{1,0:T(8,128)(2,1)S(1)} %convert_element_type.71), channel_id=1, source_target_pairs={{0,16},{8,24},{16,0},{24,8},{32,48},{40,56},{48,32},{56,40},{64,80... | collective-permute-start | bytes 196616 | tf_op jit(solution)/shard_map/ppermute | solution.py:399
  105.9 6.5 %collective-permute-start.6 = (bf16[128,256]{1,0:T(8,128)(2,1)S(1)}, bf16[128,256]{1,0:T(8,128)(2,1)S(1)}, u32[]{:S(2)}, u32[]{:S(2)}) collective-permute-start(bf16[128,256]{1,0:T(8,128)(2,1)S(1)} %fusion), channel_id=1, source_target_pairs={{0,96},{8,104},{16,112},{24,120},{32,0},{40,8},{48,16},{56,24},{64... | collective-permute-start | bytes 196616 | tf_op jit(solution)/shard_map/ppermute | solution.py:403
  108.9 5.8 %collective-permute-start.5 = (bf16[128,256]{1,0:T(8,128)(2,1)S(1)}, bf16[128,256]{1,0:T(8,128)(2,1)S(1)}, u32[]{:S(2)}, u32[]{:S(2)}) collective-permute-start(bf16[128,256]{1,0:T(8,128)(2,1)S(1)} %fusion), channel_id=1, source_target_pairs={{0,64},{8,72},{16,80},{24,88},{32,96},{40,104},{48,112},{56,120},{... | collective-permute-start | bytes 196616 | tf_op jit(solution)/shard_map/ppermute | solution.py:403
  111.6 4.3 %collective-permute-start.4 = (bf16[128,256]{1,0:T(8,128)(2,1)S(1)}, bf16[128,256]{1,0:T(8,128)(2,1)S(1)}, u32[]{:S(2)}, u32[]{:S(2)}) collective-permute-start(bf16[128,256]{1,0:T(8,128)(2,1)S(1)} %fusion), channel_id=1, source_target_pairs={{0,32},{8,40},{16,48},{24,56},{32,64},{40,72},{48,80},{56,88},{64,... | collective-permute-start | bytes 196616 | tf_op jit(solution)/shard_map/ppermute | solution.py:403
  115.9 3.9 %collective-permute-start.7 = (bf16[128,256]{1,0:T(8,128)(2,1)S(1)}, bf16[128,256]{1,0:T(8,128)(2,1)S(1)}, u32[]{:S(2)}, u32[]{:S(2)}) collective-permute-start(bf16[128,256]{1,0:T(8,128)(2,1)S(1)} %add_convert_fusion.1.mine_ref), channel_id=1, source_target_pairs={{0,8},{8,0},{16,24},{24,16},{32,40},{40,32},{48,56},{56,48},{64,72... | collective-permute-start | bytes 196616 | tf_op jit(solution)/shard_map/ppermute | solution.py:411
  116.0 12.0 %collective-permute-start.8 = (bf16[128,256]{1,0:T(8,128)(2,1)S(1)}, bf16[128,256]{1,0:T(8,128)(2,1)S(1)}, u32[]{:S(2)}, u32[]{:S(2)}) collective-permute-start(bf16[128,256]{1,0:T(8,128)(2,1)S(1)} %add_convert_fusion.1.mine_ref), channel_id=1, source_target_pairs={{0,0},{1,16},{2,32},{3,48},{4,64},{5,80},{6,96},{7,112},{8,8},{9,2... | collective-permute-start | bytes 196616 | tf_op jit(solution)/shard_map/ppermute | solution.py:410

commit v4 on v3

--- a/solution.py
+++ b/solution.py
@@ -18,6 +18,7 @@
 WIRE = 2 * ROWS + TAIL
 PAIRS = 64
 PACK = 8
+CHIPS = 8
 CONDS = 4
 SLOTS = 12
 KROWS = 24
@@ -91,60 +92,67 @@
     )(number, conduction)
 
 
-def pack_val_kernel(band_ref, val_ref, out_ref):
-    for t in range(PACK):
-        pack_band(val_ref.at[0, :, pl.ds(t * ROWS, ROWS)], out_ref.at[t], 0.0)
-
-
-def pack_choice_kernel(band_ref, own_ref, val_ref, *refs):
-    out_ref = refs[-1]
-
-    @pl.when(own_ref[0] == 1)
+def pack_give_kernel(place_ref, val_ref, out_ref):
+    for s in range(CHIPS // 2):
+        for band in range(2):
+            pack_band(val_ref.at[band, :, s ^ (place_ref[1] & 3), 0], out_ref.at[s, band], 0.0)
+
+
+def pack_give(valence, place, half):
+    block = (2, 2, CHIPS // 2, 1, ROWS, LENGTH)
+    return pl.pallas_call(
+        pack_give_kernel,
+        out_shape=jax.ShapeDtypeStruct((CHIPS // 2, 2, WIRE, 128), BF),
+        grid_spec=pltpu.PrefetchScalarGridSpec(
+            num_scalar_prefetch=1,
+            grid=(1,),
+            in_specs=[pl.BlockSpec(block, lambda i, p: (0, 0, half ^ (p[1] >> 2), 1 - p[0], 0, 0))],
+            out_specs=pl.BlockSpec((CHIPS // 2, 2, WIRE, 128), lambda i, p: (0, 0, 0, 0)),
+        ),
+        cost_estimate=pl.CostEstimate(flops=0, transcendentals=0, bytes_accessed=3_000_000),
+        compiler_params=pltpu.CompilerParams(vmem_limit_bytes=16 * 2**20),
+        name="packgive",
+    )(place, valence)
+
+
+def pack_choice_kernel(place_ref, val_ref, *refs):
+    others, outs = refs[:2], refs[2:]
+
+    @pl.when(place_ref[2] == 1)
     def _():
-        pack_val_kernel(band_ref, val_ref, out_ref)
-
-    for t in range(PARTS // PACK):
-
-        @pl.when((own_ref[0] == 0) & (pl.program_id(0) == t))
-        def _():
-            out_ref[...] = refs[t][...]
-
-
-WIRE_BLOCK = (PACK, WIRE, 128)
-VAL_BLOCK = (1, 2, PACK * ROWS, LENGTH)
-
-
-def pack_give(valence, band, t):
-    return pl.pallas_call(
-        pack_val_kernel,
-        out_shape=jax.ShapeDtypeStruct(WIRE_BLOCK, BF),
+        for s in range(CHIPS):
+            for band in range(2):
+                pack_band(val_ref.at[band, :, s ^ place_ref[1], 0], outs[s].at[band], 0.0)
+
+    @pl.when(place_ref[2] == 0)
+    def _():
+        for s in range(CHIPS):
+            outs[s][...] = others[s // 4][s % 4]
+
+
+def pack_choice(valence, place, others):
+    piece = (2, WIRE, 128)
+    return pl.pallas_call(
+        pack_choice_kernel,
+        out_shape=[jax.ShapeDtypeStruct(piece, BF)] * CHIPS,
         grid_spec=pltpu.PrefetchScalarGridSpec(
             num_scalar_prefetch=1,
             grid=(1,),
-            in_specs=[pl.BlockSpec(VAL_BLOCK, lambda i, k: (k[0], 0, t, 0))],
-            out_specs=pl.BlockSpec(WIRE_BLOCK, lambda i, k: (0, 0, 0)),
-        ),
-        cost_estimate=pl.CostEstimate(flops=0, transcendentals=0, bytes_accessed=3_000_000),
-        compiler_params=pltpu.CompilerParams(vmem_limit_bytes=14 * 2**20),
-        name="packgive",
-    )(band, valence)
-
-
-def pack_choice(valence, band, own, others):
-    return pl.pallas_call(
-        pack_choice_kernel,
-        out_shape=pltpu.HBM((PARTS, WIRE, 128), BF),
-        grid_spec=pltpu.PrefetchScalarGridSpec(
-            num_scalar_prefetch=2,
-            grid=(PARTS // PACK,),
-            in_specs=[pl.BlockSpec(VAL_BLOCK, lambda t, k, o: (k[0], 0, t, 0))]
-            + [pl.BlockSpec(WIRE_BLOCK, lambda t, k, o: (0, 0, 0)) for _ in others],
-            out_specs=pl.BlockSpec(WIRE_BLOCK, lambda t, k, o: (t, 0, 0)),
+            in_specs=[pl.BlockSpec((2, 2, CHIPS, 1, ROWS, LENGTH), lambda i, p: (0, 0, 0, p[0], 0, 0))]
+            + [pl.BlockSpec((CHIPS // 2, 2, WIRE, 128), lambda i, p: (0, 0, 0, 0))] * 2,
+            out_specs=[pl.BlockSpec(piece, lambda i, p: (0, 0, 0))] * CHIPS,
         ),
         cost_estimate=pl.CostEstimate(flops=0, transcendentals=0, bytes_accessed=8_000_000),
-        compiler_params=pltpu.CompilerParams(vmem_limit_bytes=16 * 2**20),
+        compiler_params=pltpu.CompilerParams(vmem_limit_bytes=28 * 2**20),
         name="packchoice",
-    )(band, own, valence, *others)
+    )(place, valence, *others)
+
+
+def send_to_chips(pieces):
+    got = [pieces[0]]
+    for s in range(1, CHIPS):
+        got.append(lax.ppermute(pieces[s], "band", [(b, b ^ (2 * s)) for b in range(PARTS)]))
+    return got
 
 
 def unpack_tail(tail):
@@ -157,28 +165,33 @@
     return jnp.pad(jnp.tile(tab, (1, 1, SLOTS)), ((0, 0), (0, 0), (0, 256 - SLOTS * SIDE)))
 
 
-def z_kernel(where_ref, v0_ref, v1_ref, again_ref, cond_ref, table_ref, ytab_ref, out_ref, val_main, val_tail, low_ref, high_ref):
+def z_kernel(where_ref, *refs):
+    val_refs, again_ref = refs[:CHIPS], refs[CHIPS]
+    cond_ref, table_ref, ytab_ref, out_ref, raw_ref, val_main, val_tail, low_ref, high_ref = refs[CHIPS + 1 :]
     step = pl.program_id(0)
 
-    def take(i, src):
-        val_main[i, 0] = src[0:ROWS].astype(F32)
-        val_main[i, 1] = src[ROWS : 2 * ROWS].astype(F32)
-        both = unpack_tail(src[2 * ROWS :].astype(F32))
-        val_tail[i] = jnp.concatenate([both, both], axis=1)
+    for s in range(CHIPS):
+        for r in range(2):
+
+            @pl.when((step == 0) & (where_ref[r] == s))
+            def _():
+                raw_ref[r] = val_refs[s][...]
+
+    @pl.when((step == 0) & (where_ref[2] == 1))
+    def _():
+        raw_ref[1] = again_ref[...]
 
     @pl.when(step == 0)
     def _():
-        for j in range(2):
-            take(j, v0_ref.at[j])
-            take(2 + j, v1_ref.at[j])
+        for i in range(4):
+            src = raw_ref.at[i // 2, i % 2]
+            val_main[i, 0] = src[0:ROWS].astype(F32)
+            val_main[i, 1] = src[ROWS : 2 * ROWS].astype(F32)
+            both = unpack_tail(src[2 * ROWS :].astype(F32))
+            val_tail[i] = jnp.concatenate([both, both], axis=1)
         high_ref[...] = jnp.zeros_like(high_ref)
 
-    @pl.when((step == 0) & (where_ref[2] == 1))
-    def _():
-        for j in range(2):
-            take(2 + j, again_ref.at[j])
-
-    @pl.loop(0, CONDS)
+    @pl.loop(0, CONDS, unroll=CONDS)
     def _(c):
         cre = cond_ref[c, 0:ROWS].astype(F32)
         cim = cond_ref[c, ROWS : 2 * ROWS].astype(F32)
@@ -226,7 +239,7 @@
                 out_ref[x * 128 + PAIRS : (x + 1) * 128, lanes] = (c[PAIRS:] - s[:PAIRS]).astype(BF)
 
 
-def z_transform(where, val_wire, again, cond_wire, ytab):
+def z_transform(where, val_pieces, again, cond_wire, ytab):
     single = z_table()
     table = np.zeros((4 * KROWS, 768), single.dtype)
     table[: 2 * KROWS, :384] = single
@@ -238,24 +251,23 @@
             num_scalar_prefetch=1,
             grid=(PARTS // CONDS,),
             in_specs=[
-                pl.BlockSpec((2, WIRE, 128), lambda c, o: (o[0], 0, 0)),
-                pl.BlockSpec((2, WIRE, 128), lambda c, o: (o[1], 0, 0)),
-                pl.BlockSpec((2, WIRE, 128), lambda c, o: (0, 0, 0)),
+                *[pl.BlockSpec((2, WIRE, 128), lambda c, o: (0, 0, 0))] * (CHIPS + 1),
                 pl.BlockSpec((CONDS, WIRE, 128), lambda c, o: (c, 0, 0)),
                 pl.BlockSpec((4 * KROWS, 768), lambda c, o: (0, 0)),
                 pl.BlockSpec((4, 256, 256), lambda c, o: (0, 0, 0)),
             ],
             out_specs=pl.BlockSpec((256, 512), lambda c, o: (0, 0)),
             scratch_shapes=[
+                pltpu.VMEM((2, 2, WIRE, 128), BF),
                 pltpu.VMEM((4, 2, ROWS, 128), F32),
                 pltpu.VMEM((4, ROWS, 128), F32),
                 pltpu.VMEM((KROWS * 128, 128), F32),
                 pltpu.VMEM((KROWS * 128, 128), F32),
             ],
         ),
-        compiler_params=pltpu.CompilerParams(vmem_limit_bytes=20 * 2**20),
+        compiler_params=pltpu.CompilerParams(vmem_limit_bytes=28 * 2**20),
         name="ztransform",
-    )(where, val_wire, val_wire, again, cond_wire, jnp.asarray(table), ytab)
+    )(where, *val_pieces, again, cond_wire, in_hbm(jnp.asarray(table)), ytab)
 
 
 def g_kernel(parity_ref, plane_ref, index_ref, phase_ref, out_ref):
@@ -342,33 +354,34 @@
     cond_wire = lax.all_to_all(cond_wire, "band", 0, 0, tiled=True)
 
     first, second = owners[0], owners[1]
-    bands = in_hbm(valence.reshape(2, 2, rows_all, LENGTH))
+    chip = band_pos >> 1
     siblings = [(b, b ^ 1) for b in range(PARTS)]
-    sibling = [
-        lax.ppermute(pack_give(bands, (1 - core)[None], t), "band", siblings) for t in range(PARTS // PACK)
-    ]
-    here = (first >> 1) == (band_pos >> 1)
+    bands = in_hbm(valence.reshape(2, 2, CHIPS, 2, ROWS, LENGTH))
+    place = jnp.stack([core, chip])
+    sibling = [lax.ppermute(pack_give(bands, place, half), "band", siblings) for half in range(2)]
+    here = (first >> 1) == chip
     own = jnp.where(here, first == band_pos, second == band_pos)
-    val_wire = pack_choice(bands, core[None], own.astype(jnp.int32)[None], sibling)
-    val_wire = lax.all_to_all(val_wire, "band", 0, 0, tiled=True)
-    cond_wire, val_wire = lax.optimization_barrier((cond_wire, val_wire))
-
+    place = jnp.stack([core, chip, own.astype(jnp.int32)])
+    pieces = send_to_chips(pack_choice(bands, place, sibling))
     ytab = plane_tables(band_pos & 3)
 
     def exchange_again(operands):
         bands, sibling = operands
-        again = pack_choice(bands, core[None], (second == band_pos).astype(jnp.int32)[None], sibling)
-        again = lax.all_to_all(again, "band", 0, 0, tiled=True)
-        return lax.dynamic_slice_in_dim(again, (second >> 1) * 2, 2, 0)
+        place = jnp.stack([core, chip, (second == band_pos).astype(jnp.int32)])
+        again = send_to_chips(pack_choice(bands, place, sibling))
+        found = again[0]
+        for s in range(1, CHIPS):
+            found = jnp.where((second >> 1) == chip ^ s, again[s], found)
+        return found
 
     def nothing_more(operands):
         return jnp.zeros((2, WIRE, 128), BF)
 
     both = (first != second) & ((first >> 1) == (second >> 1))
-    val_wire, both = lax.optimization_barrier((val_wire, both))
+    cond_wire, both, pieces = lax.optimization_barrier((cond_wire, both, pieces))
     again = lax.cond(both, exchange_again, nothing_more, (bands, sibling))
-    where = jnp.stack([first >> 1, second >> 1, both.astype(jnp.int32)])
-    plane = z_transform(where, val_wire, again, in_hbm(cond_wire), ytab)
+    where = jnp.stack([(first >> 1) ^ chip, (second >> 1) ^ chip, both.astype(jnp.int32)])
+    plane = z_transform(where, pieces, again, in_hbm(cond_wire), ytab)
 
     numbers = cond_wire[:, WIRE - 1, 127].astype(jnp.int32)
     order = jnp.arange(cond_energy.shape[0], dtype=jnp.int32)
@@ -406,7 +419,10 @@
     far = []
     for b in range(PARTS):
         for g in range(n_grid):
-            far.append((b * n_grid + g, (2 * g + b % 2) * n_grid + b // 2))
+            x, zl, y, zh = b >> 2, (b >> 1) & 1, g >> 1, g & 1
+            to_x, to_zl, to_y, to_zh = y, zh, (2 * y + 2 - x) % 4, zl
+            to_b = to_x * 4 + to_zl * 2 + (b & 1)
+            far.append((b * n_grid + g, to_b * n_grid + to_y * 2 + to_zh))
     column = lax.ppermute(narrow, ("band", "grid"), far)
     other = lax.ppermute(narrow, "band", siblings)
     return chi_block(core[None], narrow, other, column, jnp.concatenate([weight, weight])[:, None])

time: 130 us -> 124 us (0.954); the launches traced: 129 us -> 121 us
  waiting for transfers between devices: 57.2 us -> 47.3 us
  local copies, waits for them, and re-layouts: 3.8 us -> 5.63 us
    ppermute x2 -> x9, waiting for transfers between devices: 0.01 us -> 26 us  [the longest x7 26 us: send_to_chips(): lax.ppermute(pieces[s], 'band', [(b, b ^ 2 * s) for b in range(PARTS)])]
    all_to_all x1 -> x0, waiting for transfers between devices: 21.7 us -> none  [shards(): val_wire = lax.all_to_all(val_wire, 'band', 0, 0, tiled=True)]
    all_to_all x1, waiting for transfers between devices: 11.1 us -> 0.01 us  [shards(): cond_wire = lax.all_to_all(cond_wire, 'band', 0, 0, tiled=True)]
    ppermute x2 -> x9, starting transfers between devices: 0.67 us -> 11.3 us  [the longest x7 10.6 us: send_to_chips(): lax.ppermute(pieces[s], 'band', [(b, b ^ 2 * s) for b in range(PARTS)])]
    all_to_all x1 -> x0, starting transfers between devices: 7.86 us -> none  [shards(): val_wire = lax.all_to_all(val_wire, 'band', 0, 0, tiled=True)]
    ppermute x1, waiting for transfers between devices: 8.21 us -> 5.14 us  [shards(): column = lax.ppermute(narrow, ('band', 'grid'), far)]
    ppermute x3, starting transfers between devices: 5.75 us -> 3.3 us  [shards(): block = block + lax.ppermute(narrow, 'band', step).astype(F32)]
    pallas_call x1, Pallas kernels: 12 us -> 10.3 us  [z_transform(): pl.pallas_call(z_kernel, out_shape=jax.ShapeDtypeStruct((256, 512), BF),...]
  transfers between devices with their start and end apart: 12 -> 18, of which waited for: 9 -> 12; matrix products, arithmetic and copies ran while one was open for 5% -> 7% of each run, Pallas kernels for 6% -> 8%
where the time goes in v4:
time: 124 us; the launch traced here: 121 us
  waiting for transfers between devices  47.3 us (38%)
  starting transfers between devices  32.8 us (26%)
  Pallas kernels  25.9 us (21%)
  local copies, waits for them, and re-layouts  5.63 us (5%)
  other arithmetic  5 us (4%)
  between operations  4.71 us (4%)
    ppermute x7, waiting for transfers between devices, send_to_chips(): lax.ppermute(pieces[s], 'band', [(b, b ^ 2 * s) for b in range(PARTS)])  26 us
    ppermute x7, starting transfers between devices, send_to_chips(): lax.ppermute(pieces[s], 'band', [(b, b ^ 2 * s) for b in range(PARTS)])  10.6 us
    pallas_call x1, Pallas kernels, z_transform(): pl.pallas_call(z_kernel, out_shape=jax.ShapeDtypeStruct((256, 512), BF),...  10.3 us
    all_to_all x1, waiting for transfers between devices, shards(): parts = lax.all_to_all(parts, 'grid', 0, 0, tiled=True)  9.16 us
    all_to_all x1, starting transfers between devices, shards(): parts = lax.all_to_all(parts, 'grid', 0, 0, tiled=True)  6.88 us
    all_to_all x1, starting transfers between devices, shards(): cond_wire = lax.all_to_all(cond_wire, 'band', 0, 0, tiled=True)  5.7 us
    ppermute x1, waiting for transfers between devices, shards(): column = lax.ppermute(narrow, ('band', 'grid'), far)  5.14 us
    pallas_call x2, Pallas kernels, pack_give(): pl.pallas_call(pack_give_kernel, out_shape=jax.ShapeDtypeStruct((CHIPS //...  4.92 us
  transfers between devices with their start and end apart: 18, of which 12 were waited for; matrix products, arithmetic and copies ran while one was open for 7% of the time, Pallas kernels for 8%

profile of v4, /device:TPU:38, one launch (start us, length us, event | category | flops | bytes accessed | tf_op | source)
XLA Modules:
  0.0 121.3 jit_solution(13946035642198432275)
XLA Ops:
  0.7 3.5 %packcond.1 = bf16[16,504,128]{2,1,0:T(8,128)(2,1)} custom-call(s32[1]{0:T(128)S(6)} %copy.31.number_ref, bf16[2,3200,160]{2,1,0:T(8,128)(2,1)} %bitcast.39), custom_call_target="tpu_custom_call" | custom-call | bytes 6000000 | tf_op jit(solution)/shard_map/packcond/pallas_call | solution.py:80
  4.2 5.7 %all-to-all-start = ((bf16[16,504,128]{2,1,0:T(8,128)(2,1)}), bf16[16,504,128]{2,1,0:T(8,128)(2,1)}, u32[]{:S(2)}, u32[]{:S(2)}) async-start(bf16[16,504,128]{2,1,0:T(8,128)(2,1)} %packcond.1), calls=%async_computation | async-start | bytes 4128768 | tf_op jit(solution)/shard_map/all_to_all | solution.py:354
  9.9 2.5 %packgive.2 = bf16[4,2,504,128]{3,2,1,0:T(8,128)(2,1)S(1)} custom-call(s32[2]{0:T(128)S(1)} %pad_add_fusion.2.place_ref, bf16[2,2,8,2,200,160]{5,4,3,2,1,0:T(8,128)(2,1)} %bitcast.35), custom_call_target="tpu_custom_call" | custom-call | bytes 3000000 | tf_op jit(solution)/shard_map/packgive/pallas_call | solution.py:103
  12.7 2.5 %packgive.3 = bf16[4,2,504,128]{3,2,1,0:T(8,128)(2,1)S(1)} custom-call(s32[2]{0:T(128)S(1)} %pad_add_fusion.2.place_ref, bf16[2,2,8,2,200,160]{5,4,3,2,1,0:T(8,128)(2,1)} %bitcast.36), custom_call_target="tpu_custom_call" | custom-call | bytes 3000000 | tf_op jit(solution)/shard_map/packgive/pallas_call | solution.py:103
  19.4 4.0 %packchoice.3 = (bf16[2,504,128]{2,1,0:T(8,128)(2,1)S(1)}, bf16[2,504,128]{2,1,0:T(8,128)(2,1)S(1)}, bf16[2,504,128]{2,1,0:T(8,128)(2,1)S(1)}, bf16[2,504,128]{2...) custom-call(s32[3]{0:T(128)S(1)} %pad_add_fusion.1.place_ref, ...), custom_call_target="tpu_custom_call" | custom-call | bytes 8000000 | tf_op jit(solution)/shard_map/packchoice/pallas_call | solution.py:135
  28.4 2.1 %collective-permute-start.11 = (bf16[2,504,128]{2,1,0:T(8,128)(2,1)}, bf16[2,504,128]{2,1,0:T(8,128)(2,1)S(1)}, u32[]{:S(2)}, u32[]{:S(2)}) collective-permute-start(bf16[2,504,128]{2,1,0:T(8,128)(2,1)} %get-tuple-element.62), channel_id=1, source_target_pairs={{0,48},{8,56},{16,32},{24,40},{32,16},{40,24},{48,0},{56,8},{64,11... | collective-permute-start | bytes 774152 | tf_op jit(solution)/shard_map/ppermute | solution.py:154
  32.0 2.1 %collective-permute-start.13 = (bf16[2,504,128]{2,1,0:T(8,128)(2,1)S(1)}, bf16[2,504,128]{2,1,0:T(8,128)(2,1)S(1)}, u32[]{:S(2)}, u32[]{:S(2)}) collective-permute-start(bf16[2,504,128]{2,1,0:T(8,128)(2,1)S(1)} %get-tuple-element.64), channel_id=1, source_target_pairs={{0,80},{8,88},{16,64},{24,72},{32,112},{40,120},{48,96},{56,104},{... | collective-permute-start | bytes 774152 | tf_op jit(solution)/shard_map/ppermute | solution.py:154
  34.0 5.9 %collective-permute-done.9.refs_1_ = bf16[2,504,128]{2,1,0:T(8,128)(2,1)S(1)} collective-permute-done((bf16[2,504,128]{2,1,0:T(8,128)(2,1)S(1)}, bf16[2,504,128]{2,1,0:T(8,128)(2,1)S(1)}, u32[]{:S(2)}, u32[]{:S(2)}) %collective-permute-start.9) | collective-permute-done | bytes 258080 | tf_op jit(solution)/shard_map/ppermute | solution.py:154
  41.2 2.3 %collective-permute-start.15 = (bf16[2,504,128]{2,1,0:T(8,128)(2,1)S(1)}, bf16[2,504,128]{2,1,0:T(8,128)(2,1)S(1)}, u32[]{:S(2)}, u32[]{:S(2)}) collective-permute-start(bf16[2,504,128]{2,1,0:T(8,128)(2,1)S(1)} %get-tuple-element.66), channel_id=1, source_target_pairs={{0,112},{8,120},{16,96},{24,104},{32,80},{40,88},{48,64},{56,72},{... | collective-permute-start | bytes 774152 | tf_op jit(solution)/shard_map/ppermute | solution.py:154
  46.0 1.8 %collective-permute-done.11.refs_3_ = bf16[2,504,128]{2,1,0:T(8,128)(2,1)S(1)} collective-permute-done((bf16[2,504,128]{2,1,0:T(8,128)(2,1)}, bf16[2,504,128]{2,1,0:T(8,128)(2,1)S(1)}, u32[]{:S(2)}, u32[]{:S(2)}) %collective-permute-start.11) | collective-permute-done | bytes 258080 | tf_op jit(solution)/shard_map/ppermute | solution.py:154
  47.9 5.6 %collective-permute-done.12.refs_4_ = bf16[2,504,128]{2,1,0:T(8,128)(2,1)S(1)} collective-permute-done((bf16[2,504,128]{2,1,0:T(8,128)(2,1)}, bf16[2,504,128]{2,1,0:T(8,128)(2,1)S(1)}, u32[]{:S(2)}, u32[]{:S(2)}) %collective-permute-start.12) | collective-permute-done | bytes 258080 | tf_op jit(solution)/shard_map/ppermute | solution.py:154
  53.5 3.5 %collective-permute-done.13.refs_5_ = bf16[2,504,128]{2,1,0:T(8,128)(2,1)S(1)} collective-permute-done((bf16[2,504,128]{2,1,0:T(8,128)(2,1)S(1)}, bf16[2,504,128]{2,1,0:T(8,128)(2,1)S(1)}, u32[]{:S(2)}, u32[]{:S(2)}) %collective-permute-start.13) | collective-permute-done | bytes 258080 | tf_op jit(solution)/shard_map/ppermute | solution.py:154
  57.0 4.3 %collective-permute-done.14.refs_6_ = bf16[2,504,128]{2,1,0:T(8,128)(2,1)S(1)} collective-permute-done((bf16[2,504,128]{2,1,0:T(8,128)(2,1)S(1)}, bf16[2,504,128]{2,1,0:T(8,128)(2,1)S(1)}, u32[]{:S(2)}, u32[]{:S(2)}) %collective-permute-start.14) | collective-permute-done | bytes 258080 | tf_op jit(solution)/shard_map/ppermute | solution.py:154
  61.3 4.9 %collective-permute-done.15.refs_7_ = bf16[2,504,128]{2,1,0:T(8,128)(2,1)S(1)} collective-permute-done((bf16[2,504,128]{2,1,0:T(8,128)(2,1)S(1)}, bf16[2,504,128]{2,1,0:T(8,128)(2,1)S(1)}, u32[]{:S(2)}, u32[]{:S(2)}) %collective-permute-start.15) | collective-permute-done | bytes 258080 | tf_op jit(solution)/shard_map/ppermute | solution.py:154
  67.0 10.3 %ztransform.1.plane_ref = bf16[256,512]{1,0:T(8,128)(2,1)S(1)} custom-call(s32[3]{0:T(128)S(1)} %pad_add_fusion.3.where_ref, bf16[2,504,128]{2,1,0:T(8,128)(2,1)S(1)} %get-tuple-element.68.refs_0_, bf16[2,504,128]{2,1,0:T(8,128)(2,1)S(1)} %collective-permute-done.9.refs_1_, bf16[2,504,128]{2,1,0:T(8,128)(2,1)S(1)} %collective-permute-done.10.refs_2_, ...), custom_call_target="tpu_custom_call" | custom-call | tf_op jit(solution)/shard_map/ztransform/pallas_call | solution.py:247
  81.1 6.9 %all-to-all-start.1 = ((bf16[8,128,256]{2,1,0:T(8,128)(2,1)}), bf16[8,128,256]{2,1,0:T(8,128)(2,1)S(1)}, u32[]{:S(2)}, u32[]{:S(2)}) async-start(bf16[8,128,256]{2,1,0:T(8,128)(2,1)} %add_convert_fusion), calls=%async_computation.1 | async-start | bytes 1048576 | tf_op jit(solution)/shard_map/all_to_all | solution.py:410
  90.0 9.2 %all-to-all-done.1 = bf16[8,128,256]{2,1,0:T(8,128)(2,1)S(1)} async-done(((bf16[8,128,256]{2,1,0:T(8,128)(2,1)}), bf16[8,128,256]{2,1,0:T(8,128)(2,1)S(1)}, u32[]{:S(2)}, u32[]{:S(2)}) %all-to-all-start.1) | async-done | bytes 524320 | tf_op jit(solution)/shard_map/all_to_all | solution.py:410
  99.2 1.8 %collective-permute-start.17 = (bf16[128,256]{1,0:T(8,128)(2,1)S(1)}, bf16[128,256]{1,0:T(8,128)(2,1)S(1)}, u32[]{:S(2)}, u32[]{:S(2)}) collective-permute-start(bf16[128,256]{1,0:T(8,128)(2,1)S(1)} %convert_element_type.71), channel_id=1, source_target_pairs={{0,16},{8,24},{16,0},{24,8},{32,48},{40,56},{48,32},{56,40},{64,80... | collective-permute-start | bytes 196616 | tf_op jit(solution)/shard_map/ppermute | solution.py:412
  101.2 2.4 %collective-permute-done.17 = bf16[128,256]{1,0:T(8,128)(2,1)S(1)} collective-permute-done((bf16[128,256]{1,0:T(8,128)(2,1)S(1)}, bf16[128,256]{1,0:T(8,128)(2,1)S(1)}, u32[]{:S(2)}, u32[]{:S(2)}) %collective-permute-start.17) | collective-permute-done | bytes 65568 | tf_op jit(solution)/shard_map/ppermute | solution.py:412
  103.7 1.7 %collective-permute-start.19 = (bf16[128,256]{1,0:T(8,128)(2,1)S(1)}, bf16[128,256]{1,0:T(8,128)(2,1)S(1)}, u32[]{:S(2)}, u32[]{:S(2)}) collective-permute-start(bf16[128,256]{1,0:T(8,128)(2,1)S(1)} %fusion), channel_id=1, source_target_pairs={{0,64},{8,72},{16,80},{24,88},{32,96},{40,104},{48,112},{56,120},{... | collective-permute-start | bytes 196616 | tf_op jit(solution)/shard_map/ppermute | solution.py:416
  105.4 1.5 %collective-permute-start.18 = (bf16[128,256]{1,0:T(8,128)(2,1)S(1)}, bf16[128,256]{1,0:T(8,128)(2,1)S(1)}, u32[]{:S(2)}, u32[]{:S(2)}) collective-permute-start(bf16[128,256]{1,0:T(8,128)(2,1)S(1)} %fusion), channel_id=1, source_target_pairs={{0,32},{8,40},{16,48},{24,56},{32,64},{40,72},{48,80},{56,88},{64,... | collective-permute-start | bytes 196616 | tf_op jit(solution)/shard_map/ppermute | solution.py:416
  107.1 2.8 %collective-permute-done.20 = bf16[128,256]{1,0:T(8,128)(2,1)S(1)} collective-permute-done((bf16[128,256]{1,0:T(8,128)(2,1)S(1)}, bf16[128,256]{1,0:T(8,128)(2,1)S(1)}, u32[]{:S(2)}, u32[]{:S(2)}) %collective-permute-start.20) | collective-permute-done | bytes 65568 | tf_op jit(solution)/shard_map/ppermute | solution.py:416
  110.8 3.7 %collective-permute-start.22 = (bf16[128,256]{1,0:T(8,128)(2,1)S(1)}, bf16[128,256]{1,0:T(8,128)(2,1)S(1)}, u32[]{:S(2)}, u32[]{:S(2)}) collective-permute-start(bf16[128,256]{1,0:T(8,128)(2,1)S(1)} %add_convert_fusion.1.mine_ref), channel_id=1, source_target_pairs={{0,4},{1,20},{2,32},{3,48},{4,68},{5,84},{6,96},{7,112},{8,12},{9,... | collective-permute-start | bytes 196616 | tf_op jit(solution)/shard_map/ppermute | solution.py:426
  114.7 5.1 %collective-permute-done.22.column_ref = bf16[128,256]{1,0:T(8,128)(2,1)S(1)} collective-permute-done((bf16[128,256]{1,0:T(8,128)(2,1)S(1)}, bf16[128,256]{1,0:T(8,128)(2,1)S(1)}, u32[]{:S(2)}, u32[]{:S(2)}) %collective-permute-start.22) | collective-permute-done | bytes 65568 | tf_op jit(solution)/shard_map/ppermute | solution.py:426
  (62 shorter events, 21.5 us)
Async XLA Ops:
  0.0 88.1 %copy-start = (f32[32]{0:T(128)S(1)}, f32[32]{0:T(128)}, u32[]{:S(2)}) copy-start(f32[32]{0:T(128)} %param.13) | copy-start | bytes 388
  4.2 62.0 %all-to-all-start = ((bf16[16,504,128]{2,1,0:T(8,128)(2,1)}), bf16[16,504,128]{2,1,0:T(8,128)(2,1)}, u32[]{:S(2)}, u32[]{:S(2)}) async-start(bf16[16,504,128]{2,1,0:T(8,128)(2,1)} %packcond.1), calls=%async_computation | async-start | bytes 4128768 | tf_op jit(solution)/shard_map/all_to_all | solution.py:354
  12.4 3.2 %copy-start.3 = (s32[3,4096]{1,0:T(4,128)S(1)}, s32[3,4096]{1,0:T(4,128)}, u32[]{:S(2)}) copy-start(s32[3,4096]{1,0:T(4,128)} %param.17) | copy-start | bytes 147460
  12.4 4.2 %copy-start.4 = (s32[2]{0:T(128)S(1)}, s32[2]{0:T(128)}, u32[]{:S(2)}) copy-start(s32[2]{0:T(128)} %param.16) | copy-start | bytes 28
  12.4 7.0 %collective-permute-start.7 = (bf16[4,2,504,128]{3,2,1,0:T(8,128)(2,1)S(1)}, bf16[4,2,504,128]{3,2,1,0:T(8,128)(2,1)}, u32[]{:S(2)}, u32[]{:S(2)}) collective-permute-start(bf16[4,2,504,128]{3,2,1,0:T(8,128)(2,1)S(1)} %packgive.2), channel_id=1, source_target_pairs={{0,8},{8,0},{16,24},{24,16},{32,40},{40,32},{48,56},{56,48},{64,72... | collective-permute-start | bytes 3096584 | tf_op jit(solution)/shard_map/ppermute | solution.py:361
  15.1 4.3 %collective-permute-start.8 = (bf16[4,2,504,128]{3,2,1,0:T(8,128)(2,1)S(1)}, bf16[4,2,504,128]{3,2,1,0:T(8,128)(2,1)}, u32[]{:S(2)}, u32[]{:S(2)}) collective-permute-start(bf16[4,2,504,128]{3,2,1,0:T(8,128)(2,1)S(1)} %packgive.3), channel_id=1, source_target_pairs={{0,8},{8,0},{16,24},{24,16},{32,40},{40,32},{48,56},{56,48},{64,72... | collective-permute-start | bytes 3096584 | tf_op jit(solution)/shard_map/ppermute | solution.py:361
  23.4 16.5 %collective-permute-start.9 = (bf16[2,504,128]{2,1,0:T(8,128)(2,1)S(1)}, bf16[2,504,128]{2,1,0:T(8,128)(2,1)S(1)}, u32[]{:S(2)}, u32[]{:S(2)}) collective-permute-start(bf16[2,504,128]{2,1,0:T(8,128)(2,1)S(1)} %get-tuple-element.60), channel_id=1, source_target_pairs={{0,16},{8,24},{16,0},{24,8},{32,48},{40,56},{48,32},{56,40},{64,80... | collective-permute-start | bytes 774152 | tf_op jit(solution)/shard_map/ppermute | solution.py:154
  24.0 17.2 %collective-permute-start.10 = (bf16[2,504,128]{2,1,0:T(8,128)(2,1)S(1)}, bf16[2,504,128]{2,1,0:T(8,128)(2,1)S(1)}, u32[]{:S(2)}, u32[]{:S(2)}) collective-permute-start(bf16[2,504,128]{2,1,0:T(8,128)(2,1)S(1)} %get-tuple-element.61), channel_id=1, source_target_pairs={{0,32},{8,40},{16,48},{24,56},{32,0},{40,8},{48,16},{56,24},{64,96... | collective-permute-start | bytes 774152 | tf_op jit(solution)/shard_map/ppermute | solution.py:154
  28.4 19.5 %collective-permute-start.11 = (bf16[2,504,128]{2,1,0:T(8,128)(2,1)}, bf16[2,504,128]{2,1,0:T(8,128)(2,1)S(1)}, u32[]{:S(2)}, u32[]{:S(2)}) collective-permute-start(bf16[2,504,128]{2,1,0:T(8,128)(2,1)} %get-tuple-element.62), channel_id=1, source_target_pairs={{0,48},{8,56},{16,32},{24,40},{32,16},{40,24},{48,0},{56,8},{64,11... | collective-permute-start | bytes 774152 | tf_op jit(solution)/shard_map/ppermute | solution.py:154
  30.5 23.0 %collective-permute-start.12 = (bf16[2,504,128]{2,1,0:T(8,128)(2,1)}, bf16[2,504,128]{2,1,0:T(8,128)(2,1)S(1)}, u32[]{:S(2)}, u32[]{:S(2)}) collective-permute-start(bf16[2,504,128]{2,1,0:T(8,128)(2,1)} %get-tuple-element.63), channel_id=1, source_target_pairs={{0,64},{8,72},{16,80},{24,88},{32,96},{40,104},{48,112},{56,120},{... | collective-permute-start | bytes 774152 | tf_op jit(solution)/shard_map/ppermute | solution.py:154
  32.0 25.0 %collective-permute-start.13 = (bf16[2,504,128]{2,1,0:T(8,128)(2,1)S(1)}, bf16[2,504,128]{2,1,0:T(8,128)(2,1)S(1)}, u32[]{:S(2)}, u32[]{:S(2)}) collective-permute-start(bf16[2,504,128]{2,1,0:T(8,128)(2,1)S(1)} %get-tuple-element.64), channel_id=1, source_target_pairs={{0,80},{8,88},{16,64},{24,72},{32,112},{40,120},{48,96},{56,104},{... | collective-permute-start | bytes 774152 | tf_op jit(solution)/shard_map/ppermute | solution.py:154
  39.9 21.4 %collective-permute-start.14 = (bf16[2,504,128]{2,1,0:T(8,128)(2,1)S(1)}, bf16[2,504,128]{2,1,0:T(8,128)(2,1)S(1)}, u32[]{:S(2)}, u32[]{:S(2)}) collective-permute-start(bf16[2,504,128]{2,1,0:T(8,128)(2,1)S(1)} %get-tuple-element.65), channel_id=1, source_target_pairs={{0,96},{8,104},{16,112},{24,120},{32,64},{40,72},{48,80},{56,88},{... | collective-permute-start | bytes 774152 | tf_op jit(solution)/shard_map/ppermute | solution.py:154
  41.2 25.0 %collective-permute-start.15 = (bf16[2,504,128]{2,1,0:T(8,128)(2,1)S(1)}, bf16[2,504,128]{2,1,0:T(8,128)(2,1)S(1)}, u32[]{:S(2)}, u32[]{:S(2)}) collective-permute-start(bf16[2,504,128]{2,1,0:T(8,128)(2,1)S(1)} %get-tuple-element.66), channel_id=1, source_target_pairs={{0,112},{8,120},{16,96},{24,104},{32,80},{40,88},{48,64},{56,72},{... | collective-permute-start | bytes 774152 | tf_op jit(solution)/shard_map/ppermute | solution.py:154
  78.1 2.0 %collective-permute-start.16 = (bf16[8,128,256]{2,1,0:T(8,128)(2,1)S(1)}, bf16[8,128,256]{2,1,0:T(8,128)(2,1)S(1)}, u32[]{:S(2)}, u32[]{:S(2)}) collective-permute-start(bf16[8,128,256]{2,1,0:T(8,128)(2,1)S(1)} %gelements.3), channel_id=1, source_target_pairs={{0,8},{8,0},{16,24},{24,16},{32,40},{40,32},{48,56},{56,48},{64,72... | collective-permute-start | bytes 1572872 | tf_op jit(solution)/shard_map/ppermute | solution.py:407
  79.1 21.9 %copy-start.5 = (f32[16]{0:T(128)S(1)}, f32[16]{0:T(128)}, u32[]{:S(2)}) copy-start(f32[16]{0:T(128)} %param.14) | copy-start | bytes 196
  81.1 18.1 %all-to-all-start.1 = ((bf16[8,128,256]{2,1,0:T(8,128)(2,1)}), bf16[8,128,256]{2,1,0:T(8,128)(2,1)S(1)}, u32[]{:S(2)}, u32[]{:S(2)}) async-start(bf16[8,128,256]{2,1,0:T(8,128)(2,1)} %add_convert_fusion), calls=%async_computation.1 | async-start | bytes 1048576 | tf_op jit(solution)/shard_map/all_to_all | solution.py:410
  99.2 4.3 %collective-permute-start.17 = (bf16[128,256]{1,0:T(8,128)(2,1)S(1)}, bf16[128,256]{1,0:T(8,128)(2,1)S(1)}, u32[]{:S(2)}, u32[]{:S(2)}) collective-permute-start(bf16[128,256]{1,0:T(8,128)(2,1)S(1)} %convert_element_type.71), channel_id=1, source_target_pairs={{0,16},{8,24},{16,0},{24,8},{32,48},{40,56},{48,32},{56,40},{64,80... | collective-permute-start | bytes 196616 | tf_op jit(solution)/shard_map/ppermute | solution.py:412
  103.6 6.2 %collective-permute-start.20 = (bf16[128,256]{1,0:T(8,128)(2,1)S(1)}, bf16[128,256]{1,0:T(8,128)(2,1)S(1)}, u32[]{:S(2)}, u32[]{:S(2)}) collective-permute-start(bf16[128,256]{1,0:T(8,128)(2,1)S(1)} %fusion), channel_id=1, source_target_pairs={{0,96},{8,104},{16,112},{24,120},{32,0},{40,8},{48,16},{56,24},{64... | collective-permute-start | bytes 196616 | tf_op jit(solution)/shard_map/ppermute | solution.py:416
  103.7 6.2 %collective-permute-start.19 = (bf16[128,256]{1,0:T(8,128)(2,1)S(1)}, bf16[128,256]{1,0:T(8,128)(2,1)S(1)}, u32[]{:S(2)}, u32[]{:S(2)}) collective-permute-start(bf16[128,256]{1,0:T(8,128)(2,1)S(1)} %fusion), channel_id=1, source_target_pairs={{0,64},{8,72},{16,80},{24,88},{32,96},{40,104},{48,112},{56,120},{... | collective-permute-start | bytes 196616 | tf_op jit(solution)/shard_map/ppermute | solution.py:416
  105.4 5.3 %collective-permute-start.18 = (bf16[128,256]{1,0:T(8,128)(2,1)S(1)}, bf16[128,256]{1,0:T(8,128)(2,1)S(1)}, u32[]{:S(2)}, u32[]{:S(2)}) collective-permute-start(bf16[128,256]{1,0:T(8,128)(2,1)S(1)} %fusion), channel_id=1, source_target_pairs={{0,32},{8,40},{16,48},{24,56},{32,64},{40,72},{48,80},{56,88},{64,... | collective-permute-start | bytes 196616 | tf_op jit(solution)/shard_map/ppermute | solution.py:416
  110.7 4.0 %collective-permute-start.21 = (bf16[128,256]{1,0:T(8,128)(2,1)S(1)}, bf16[128,256]{1,0:T(8,128)(2,1)S(1)}, u32[]{:S(2)}, u32[]{:S(2)}) collective-permute-start(bf16[128,256]{1,0:T(8,128)(2,1)S(1)} %add_convert_fusion.1.mine_ref), channel_id=1, source_target_pairs={{0,8},{8,0},{16,24},{24,16},{32,40},{40,32},{48,56},{56,48},{64,72... | collective-permute-start | bytes 196616 | tf_op jit(solution)/shard_map/ppermute | solution.py:427
  110.8 9.0 %collective-permute-start.22 = (bf16[128,256]{1,0:T(8,128)(2,1)S(1)}, bf16[128,256]{1,0:T(8,128)(2,1)S(1)}, u32[]{:S(2)}, u32[]{:S(2)}) collective-permute-start(bf16[128,256]{1,0:T(8,128)(2,1)S(1)} %add_convert_fusion.1.mine_ref), channel_id=1, source_target_pairs={{0,4},{1,20},{2,32},{3,48},{4,68},{5,84},{6,96},{7,112},{8,12},{9,... | collective-permute-start | bytes 196616 | tf_op jit(solution)/shard_map/ppermute | solution.py:426

commit v5 on v4

--- a/solution.py
+++ b/solution.py
@@ -19,6 +19,7 @@
 PAIRS = 64
 PACK = 8
 CHIPS = 8
+GIVE = 4
 CONDS = 4
 SLOTS = 12
 KROWS = 24
@@ -93,21 +94,21 @@
 
 
 def pack_give_kernel(place_ref, val_ref, out_ref):
-    for s in range(CHIPS // 2):
+    for s in range(GIVE):
         for band in range(2):
-            pack_band(val_ref.at[band, :, s ^ (place_ref[1] & 3), 0], out_ref.at[s, band], 0.0)
-
-
-def pack_give(valence, place, half):
-    block = (2, 2, CHIPS // 2, 1, ROWS, LENGTH)
+            pack_band(val_ref.at[band, :, s ^ (place_ref[1] & (GIVE - 1)), 0], out_ref.at[s, band], 0.0)
+
+
+def pack_give(valence, place, t):
+    block = (2, 2, GIVE, 1, ROWS, LENGTH)
     return pl.pallas_call(
         pack_give_kernel,
-        out_shape=jax.ShapeDtypeStruct((CHIPS // 2, 2, WIRE, 128), BF),
+        out_shape=jax.ShapeDtypeStruct((GIVE, 2, WIRE, 128), BF),
         grid_spec=pltpu.PrefetchScalarGridSpec(
             num_scalar_prefetch=1,
             grid=(1,),
-            in_specs=[pl.BlockSpec(block, lambda i, p: (0, 0, half ^ (p[1] >> 2), 1 - p[0], 0, 0))],
-            out_specs=pl.BlockSpec((CHIPS // 2, 2, WIRE, 128), lambda i, p: (0, 0, 0, 0)),
+            in_specs=[pl.BlockSpec(block, lambda i, p: (0, 0, t ^ (p[1] // GIVE), 1 - p[0], 0, 0))],
+            out_specs=pl.BlockSpec((GIVE, 2, WIRE, 128), lambda i, p: (0, 0, 0, 0)),
         ),
         cost_estimate=pl.CostEstimate(flops=0, transcendentals=0, bytes_accessed=3_000_000),
         compiler_params=pltpu.CompilerParams(vmem_limit_bytes=16 * 2**20),
@@ -116,7 +117,7 @@
 
 
 def pack_choice_kernel(place_ref, val_ref, *refs):
-    others, outs = refs[:2], refs[2:]
+    others, outs = refs[: CHIPS // GIVE], refs[CHIPS // GIVE :]
 
     @pl.when(place_ref[2] == 1)
     def _():
@@ -127,7 +128,7 @@
     @pl.when(place_ref[2] == 0)
     def _():
         for s in range(CHIPS):
-            outs[s][...] = others[s // 4][s % 4]
+            outs[s][...] = others[s // GIVE][s % GIVE]
 
 
 def pack_choice(valence, place, others):
@@ -139,7 +140,7 @@
             num_scalar_prefetch=1,
             grid=(1,),
             in_specs=[pl.BlockSpec((2, 2, CHIPS, 1, ROWS, LENGTH), lambda i, p: (0, 0, 0, p[0], 0, 0))]
-            + [pl.BlockSpec((CHIPS // 2, 2, WIRE, 128), lambda i, p: (0, 0, 0, 0))] * 2,
+            + [pl.BlockSpec((GIVE, 2, WIRE, 128), lambda i, p: (0, 0, 0, 0))] * (CHIPS // GIVE),
             out_specs=[pl.BlockSpec(piece, lambda i, p: (0, 0, 0))] * CHIPS,
         ),
         cost_estimate=pl.CostEstimate(flops=0, transcendentals=0, bytes_accessed=8_000_000),
@@ -272,20 +273,21 @@
 
 def g_kernel(parity_ref, plane_ref, index_ref, phase_ref, out_ref):
     row = lax.broadcasted_iota(jnp.int32, (512, GCHUNK), 0)
-    for chunk in range(out_ref.shape[0]):
+    for s in range(out_ref.shape[0]):
+        chunk = s ^ parity_ref[1]
         pick = jnp.where(row == index_ref[chunk, 0], 1.0, 0.0).astype(BF)
         at = jnp.dot(plane_ref[...], pick, preferred_element_type=F32)
         real = jnp.zeros((PAIRS, GCHUNK), F32)
         imag = jnp.zeros((PAIRS, GCHUNK), F32)
         for x in range(2):
-            c = phase_ref[chunk, 0, 2 * x : 2 * x + 1]
-            s = phase_ref[chunk, 0, 2 * x + 1 : 2 * x + 2]
+            cos = phase_ref[chunk, 0, 2 * x : 2 * x + 1]
+            sin = phase_ref[chunk, 0, 2 * x + 1 : 2 * x + 2]
             re = at[x * 128 : x * 128 + PAIRS]
             im = at[x * 128 + PAIRS : (x + 1) * 128]
-            real = real + re * c + im * s
-            imag = imag + im * c - re * s
-        out_ref[chunk, :PAIRS] = real.astype(out_ref.dtype)
-        out_ref[chunk, PAIRS:] = imag.astype(out_ref.dtype)
+            real = real + re * cos + im * sin
+            imag = imag + im * cos - re * sin
+        out_ref[s, :PAIRS] = real.astype(out_ref.dtype)
+        out_ref[s, PAIRS:] = imag.astype(out_ref.dtype)
 
 
 def g_elements(parity, plane, index, phase, dtype):
@@ -307,6 +309,25 @@
         cost_estimate=pl.CostEstimate(flops=2 * 10**9, transcendentals=0, bytes_accessed=12_000_000),
         name="gelements",
     )(parity, plane, index, phase)
+
+
+def merge_kernel(keep_ref, come_ref, *out_refs):
+    for s, out_ref in enumerate(out_refs):
+        out_ref[...] = (keep_ref[s] + come_ref[s].astype(F32)).astype(BF)
+
+
+def merge(keep, come):
+    blocks = keep.shape[0]
+    whole = pl.BlockSpec((blocks, 128, GCHUNK), lambda i: (0, 0, 0))
+    return pl.pallas_call(
+        merge_kernel,
+        out_shape=[jax.ShapeDtypeStruct((128, GCHUNK), BF)] * blocks,
+        grid=(1,),
+        in_specs=[whole, whole],
+        out_specs=[pl.BlockSpec((128, GCHUNK), lambda i: (0, 0))] * blocks,
+        compiler_params=pltpu.CompilerParams(vmem_limit_bytes=10 * 2**20),
+        name="merge",
+    )(keep, come)
 
 
 def chi_kernel(core_ref, mine_ref, other_ref, column_ref, weight_ref, out_ref):
@@ -358,7 +379,7 @@
     siblings = [(b, b ^ 1) for b in range(PARTS)]
     bands = in_hbm(valence.reshape(2, 2, CHIPS, 2, ROWS, LENGTH))
     place = jnp.stack([core, chip])
-    sibling = [lax.ppermute(pack_give(bands, place, half), "band", siblings) for half in range(2)]
+    sibling = [lax.ppermute(pack_give(bands, place, t), "band", siblings) for t in range(CHIPS // GIVE)]
     here = (first >> 1) == chip
     own = jnp.where(here, first == band_pos, second == band_pos)
     place = jnp.stack([core, chip, own.astype(jnp.int32)])
@@ -403,12 +424,13 @@
     phase = phase.reshape(4, PARTS, GCHUNK).transpose(1, 0, 2).reshape(PARTS // 2, 2, 4, GCHUNK)
 
     core = band_pos & 1
-    away = g_elements((1 - core)[None], plane, index, phase, BF)
+    away = g_elements(jnp.stack([1 - core, grid_pos]), plane, index, phase, BF)
     come = lax.ppermute(away, "band", siblings)
-    keep = g_elements(core[None], plane, index, phase, F32)
-    parts = (keep + come.astype(F32)).astype(BF)
-    parts = lax.all_to_all(parts, "grid", 0, 0, tiled=True)
-    block = jnp.sum(parts.astype(F32), axis=0)
+    keep = g_elements(jnp.stack([core, grid_pos]), plane, index, phase, F32)
+    parts = merge(keep, come)
+    block = parts[0].astype(F32)
+    for s in range(1, n_grid):
+        block = block + lax.ppermute(parts[s], "grid", [(g, g ^ s) for g in range(n_grid)]).astype(F32)
     block = block + lax.ppermute(block.astype(BF), "band", [(b, b ^ 2) for b in range(PARTS)]).astype(F32)
     narrow = block.astype(BF)
     for turn in (4, 8, 12):

time: 124 us -> 133 us (1.073); the launches traced: 121 us -> 132 us
  waiting for transfers between devices: 47.3 us -> 56 us
    ppermute x2 -> x9, starting transfers between devices: 0.67 us -> 14.9 us  [the longest x7 14.3 us: shards(): lax.ppermute(parts[s], 'grid', [(g, g ^ s) for g in range(n_grid)])]
    all_to_all x1 -> x0, waiting for transfers between devices: 9.16 us -> none  [shards(): parts = lax.all_to_all(parts, 'grid', 0, 0, tiled=True)]
    all_to_all x1 -> x0, starting transfers between devices: 6.88 us -> none  [shards(): parts = lax.all_to_all(parts, 'grid', 0, 0, tiled=True)]
    ppermute x2 -> x9, waiting for transfers between devices: 0.01 us -> 6.49 us  [the longest x7 6.48 us: shards(): lax.ppermute(parts[s], 'grid', [(g, g ^ s) for g in range(n_grid)])]
    ppermute x7, waiting for transfers between devices: 26 us -> 31.5 us  [send_to_chips(): lax.ppermute(pieces[s], 'band', [(b, b ^ 2 * s) for b in range(PARTS)])]
    ppermute x1, starting transfers between devices: 3.68 us -> 0.07 us  [shards(): column = lax.ppermute(narrow, ('band', 'grid'), far)]
    ppermute x1, waiting for transfers between devices: 5.14 us -> 7.49 us  [shards(): column = lax.ppermute(narrow, ('band', 'grid'), far)]
    ppermute x7, starting transfers between devices: 10.6 us -> 8.81 us  [send_to_chips(): lax.ppermute(pieces[s], 'band', [(b, b ^ 2 * s) for b in range(PARTS)])]
  transfers between devices with their start and end apart: 18 -> 24, of which waited for: 12 -> 16; matrix products, arithmetic and copies ran while one was open for 7% -> 7% of each run, Pallas kernels for 8% -> 6%
where the time goes in v5:
time: 133 us; the launch traced here: 132 us
  waiting for transfers between devices  56 us (42%)
  starting transfers between devices  32.8 us (25%)
  Pallas kernels  27.2 us (20%)
  local copies, waits for them, and re-layouts  6.54 us (5%)
  other arithmetic  4.81 us (4%)
  between operations  4.75 us (4%)
    ppermute x7, waiting for transfers between devices, send_to_chips(): lax.ppermute(pieces[s], 'band', [(b, b ^ 2 * s) for b in range(PARTS)])  31.5 us
    ppermute x7, starting transfers between devices, shards(): lax.ppermute(parts[s], 'grid', [(g, g ^ s) for g in range(n_grid)])  14.3 us
    pallas_call x1, Pallas kernels, z_transform(): pl.pallas_call(z_kernel, out_shape=jax.ShapeDtypeStruct((256, 512), BF),...  10.3 us
    ppermute x7, starting transfers between devices, send_to_chips(): lax.ppermute(pieces[s], 'band', [(b, b ^ 2 * s) for b in range(PARTS)])  8.81 us
    ppermute x1, waiting for transfers between devices, shards(): column = lax.ppermute(narrow, ('band', 'grid'), far)  7.49 us
    ppermute x7, waiting for transfers between devices, shards(): lax.ppermute(parts[s], 'grid', [(g, g ^ s) for g in range(n_grid)])  6.48 us
    all_to_all x1, starting transfers between devices, shards(): cond_wire = lax.all_to_all(cond_wire, 'band', 0, 0, tiled=True)  5.69 us
    ppermute x3, waiting for transfers between devices, shards(): block = block + lax.ppermute(narrow, 'band', step).astype(F32)  5.3 us
  transfers between devices with their start and end apart: 24, of which 16 were waited for; matrix products, arithmetic and copies ran while one was open for 7% of the time, Pallas kernels for 6%

profile of v5, /device:TPU:38, one launch (start us, length us, event | category | flops | bytes accessed | tf_op | source)
XLA Modules:
  0.0 132.1 jit_solution(4766181405042946458)
XLA Ops:
  0.7 3.5 %packcond.1 = bf16[16,504,128]{2,1,0:T(8,128)(2,1)} custom-call(s32[1]{0:T(128)S(6)} %copy.31.number_ref, bf16[2,3200,160]{2,1,0:T(8,128)(2,1)} %bitcast.40), custom_call_target="tpu_custom_call" | custom-call | bytes 6000000 | tf_op jit(solution)/shard_map/packcond/pallas_call | solution.py:81
  4.3 2.5 %packgive.2 = bf16[4,2,504,128]{3,2,1,0:T(8,128)(2,1)S(1)} custom-call(s32[2]{0:T(128)S(1)} %pad_add_fusion.3.place_ref, bf16[2,2,8,2,200,160]{5,4,3,2,1,0:T(8,128)(2,1)} %bitcast.36), custom_call_target="tpu_custom_call" | custom-call | bytes 3000000 | tf_op jit(solution)/shard_map/packgive/pallas_call | solution.py:104
  6.8 2.5 %packgive.3 = bf16[4,2,504,128]{3,2,1,0:T(8,128)(2,1)S(1)} custom-call(s32[2]{0:T(128)S(1)} %pad_add_fusion.3.place_ref, bf16[2,2,8,2,200,160]{5,4,3,2,1,0:T(8,128)(2,1)} %bitcast.37), custom_call_target="tpu_custom_call" | custom-call | bytes 3000000 | tf_op jit(solution)/shard_map/packgive/pallas_call | solution.py:104
  9.9 5.7 %all-to-all-start = ((bf16[16,504,128]{2,1,0:T(8,128)(2,1)}), bf16[16,504,128]{2,1,0:T(8,128)(2,1)}, u32[]{:S(2)}, u32[]{:S(2)}) async-start(bf16[16,504,128]{2,1,0:T(8,128)(2,1)} %packcond.1), calls=%async_computation | async-start | bytes 4128768 | tf_op jit(solution)/shard_map/all_to_all | solution.py:375
  22.7 4.0 %packchoice.3 = (bf16[2,504,128]{2,1,0:T(8,128)(2,1)S(1)}, bf16[2,504,128]{2,1,0:T(8,128)(2,1)S(1)}, bf16[2,504,128]{2,1,0:T(8,128)(2,1)S(1)}, bf16[2,504,128]{2...) custom-call(s32[3]{0:T(128)S(1)} %pad_add_fusion.2.place_ref, ...), custom_call_target="tpu_custom_call" | custom-call | bytes 8000000 | tf_op jit(solution)/shard_map/packchoice/pallas_call | solution.py:136
  26.7 1.9 %collective-permute-start.10 = (bf16[2,504,128]{2,1,0:T(8,128)(2,1)S(1)}, bf16[2,504,128]{2,1,0:T(8,128)(2,1)S(1)}, u32[]{:S(2)}, u32[]{:S(2)}) collective-permute-start(bf16[2,504,128]{2,1,0:T(8,128)(2,1)S(1)} %get-tuple-element.69), channel_id=1, source_target_pairs={{0,32},{8,40},{16,48},{24,56},{32,0},{40,8},{48,16},{56,24},{64,96... | collective-permute-start | bytes 774152 | tf_op jit(solution)/shard_map/ppermute | solution.py:155
  30.3 3.0 %collective-permute-start.13 = (bf16[2,504,128]{2,1,0:T(8,128)(2,1)}, bf16[2,504,128]{2,1,0:T(8,128)(2,1)S(1)}, u32[]{:S(2)}, u32[]{:S(2)}) collective-permute-start(bf16[2,504,128]{2,1,0:T(8,128)(2,1)} %get-tuple-element.72), channel_id=1, source_target_pairs={{0,80},{8,88},{16,64},{24,72},{32,112},{40,120},{48,96},{56,104},{... | collective-permute-start | bytes 774152 | tf_op jit(solution)/shard_map/ppermute | solution.py:155
  34.4 11.4 %collective-permute-done.10.refs_2_ = bf16[2,504,128]{2,1,0:T(8,128)(2,1)S(1)} collective-permute-done((bf16[2,504,128]{2,1,0:T(8,128)(2,1)S(1)}, bf16[2,504,128]{2,1,0:T(8,128)(2,1)S(1)}, u32[]{:S(2)}, u32[]{:S(2)}) %collective-permute-start.10) | collective-permute-done | bytes 258080 | tf_op jit(solution)/shard_map/ppermute | solution.py:155
  47.0 8.3 %collective-permute-done.11.refs_3_ = bf16[2,504,128]{2,1,0:T(8,128)(2,1)S(1)} collective-permute-done((bf16[2,504,128]{2,1,0:T(8,128)(2,1)S(1)}, bf16[2,504,128]{2,1,0:T(8,128)(2,1)S(1)}, u32[]{:S(2)}, u32[]{:S(2)}) %collective-permute-start.11) | collective-permute-done | bytes 258080 | tf_op jit(solution)/shard_map/ppermute | solution.py:155
  59.8 2.4 %collective-permute-done.12.refs_4_ = bf16[2,504,128]{2,1,0:T(8,128)(2,1)S(1)} collective-permute-done((bf16[2,504,128]{2,1,0:T(8,128)(2,1)}, bf16[2,504,128]{2,1,0:T(8,128)(2,1)S(1)}, u32[]{:S(2)}, u32[]{:S(2)}) %collective-permute-start.12) | collective-permute-done | bytes 258080 | tf_op jit(solution)/shard_map/ppermute | solution.py:155
  62.8 3.6 %collective-permute-done.15.refs_7_ = bf16[2,504,128]{2,1,0:T(8,128)(2,1)S(1)} collective-permute-done((bf16[2,504,128]{2,1,0:T(8,128)(2,1)S(1)}, bf16[2,504,128]{2,1,0:T(8,128)(2,1)S(1)}, u32[]{:S(2)}, u32[]{:S(2)}) %collective-permute-start.15) | collective-permute-done | bytes 258080 | tf_op jit(solution)/shard_map/ppermute | solution.py:155
  66.4 5.2 %collective-permute-done.9.refs_1_ = bf16[2,504,128]{2,1,0:T(8,128)(2,1)S(1)} collective-permute-done((bf16[2,504,128]{2,1,0:T(8,128)(2,1)S(1)}, bf16[2,504,128]{2,1,0:T(8,128)(2,1)S(1)}, u32[]{:S(2)}, u32[]{:S(2)}) %collective-permute-start.9) | collective-permute-done | bytes 258080 | tf_op jit(solution)/shard_map/ppermute | solution.py:155
  72.4 10.3 %ztransform.1.plane_ref = bf16[256,512]{1,0:T(8,128)(2,1)S(1)} custom-call(s32[3]{0:T(128)S(1)} %pad_add_fusion.4.where_ref, bf16[2,504,128]{2,1,0:T(8,128)(2,1)S(1)} %get-tuple-element.76.refs_0_, bf16[2,504,128]{2,1,0:T(8,128)(2,1)S(1)} %collective-permute-done.9.refs_1_, bf16[2,504,128]{2,1,0:T(8,128)(2,1)S(1)} %collective-permute-done.10.refs_2_, ...), custom_call_target="tpu_custom_call" | custom-call | tf_op jit(solution)/shard_map/ztransform/pallas_call | solution.py:248
  86.2 3.1 %collective-permute-start.17 = (bf16[128,256]{1,0:T(8,128)(2,1)S(1)}, bf16[128,256]{1,0:T(8,128)(2,1)S(1)}, u32[]{:S(2)}, u32[]{:S(2)}) collective-permute-start(bf16[128,256]{1,0:T(8,128)(2,1)S(1)} %get-tuple-element.86), channel_id=1, source_target_pairs={{0,1},{1,0},{2,3},{3,2},{4,5},{5,4},{6,7},{7,6},{8,9},{9,8},{10,11... | collective-permute-start | bytes 196616 | tf_op jit(solution)/shard_map/ppermute | solution.py:433
  89.3 1.6 %collective-permute-start.18 = (bf16[128,256]{1,0:T(8,128)(2,1)S(1)}, bf16[128,256]{1,0:T(8,128)(2,1)S(1)}, u32[]{:S(2)}, u32[]{:S(2)}) collective-permute-start(bf16[128,256]{1,0:T(8,128)(2,1)S(1)} %get-tuple-element.87), channel_id=1, source_target_pairs={{0,2},{1,3},{2,0},{3,1},{4,6},{5,7},{6,4},{7,5},{8,10},{9,11},{10,... | collective-permute-start | bytes 196616 | tf_op jit(solution)/shard_map/ppermute | solution.py:433
  92.0 3.2 %collective-permute-start.20 = (bf16[128,256]{1,0:T(8,128)(2,1)S(1)}, bf16[128,256]{1,0:T(8,128)(2,1)S(1)}, u32[]{:S(2)}, u32[]{:S(2)}) collective-permute-start(bf16[128,256]{1,0:T(8,128)(2,1)S(1)} %get-tuple-element.89), channel_id=1, source_target_pairs={{0,4},{1,5},{2,6},{3,7},{4,0},{5,1},{6,2},{7,3},{8,12},{9,13},{10,... | collective-permute-start | bytes 196616 | tf_op jit(solution)/shard_map/ppermute | solution.py:433
  95.2 2.8 %collective-permute-start.21 = (bf16[128,256]{1,0:T(8,128)(2,1)S(1)}, bf16[128,256]{1,0:T(8,128)(2,1)S(1)}, u32[]{:S(2)}, u32[]{:S(2)}) collective-permute-start(bf16[128,256]{1,0:T(8,128)(2,1)S(1)} %get-tuple-element.90), channel_id=1, source_target_pairs={{0,5},{1,4},{2,7},{3,6},{4,1},{5,0},{6,3},{7,2},{8,13},{9,12},{10,... | collective-permute-start | bytes 196616 | tf_op jit(solution)/shard_map/ppermute | solution.py:433
  97.9 3.0 %collective-permute-start.22 = (bf16[128,256]{1,0:T(8,128)(2,1)S(1)}, bf16[128,256]{1,0:T(8,128)(2,1)S(1)}, u32[]{:S(2)}, u32[]{:S(2)}) collective-permute-start(bf16[128,256]{1,0:T(8,128)(2,1)S(1)} %get-tuple-element.91), channel_id=1, source_target_pairs={{0,6},{1,7},{2,4},{3,5},{4,2},{5,3},{6,0},{7,1},{8,14},{9,15},{10,... | collective-permute-start | bytes 196616 | tf_op jit(solution)/shard_map/ppermute | solution.py:433
  104.7 4.1 %collective-permute-done.23 = bf16[128,256]{1,0:T(8,128)(2,1)S(1)} collective-permute-done((bf16[128,256]{1,0:T(8,128)(2,1)S(1)}, bf16[128,256]{1,0:T(8,128)(2,1)S(1)}, u32[]{:S(2)}, u32[]{:S(2)}) %collective-permute-start.23) | collective-permute-done | bytes 65568 | tf_op jit(solution)/shard_map/ppermute | solution.py:433
  109.3 4.0 %collective-permute-done.24 = bf16[128,256]{1,0:T(8,128)(2,1)S(1)} collective-permute-done((bf16[128,256]{1,0:T(8,128)(2,1)S(1)}, bf16[128,256]{1,0:T(8,128)(2,1)S(1)}, u32[]{:S(2)}, u32[]{:S(2)}) %collective-permute-start.24) | collective-permute-done | bytes 65568 | tf_op jit(solution)/shard_map/ppermute | solution.py:434
  114.0 2.2 %collective-permute-start.26 = (bf16[128,256]{1,0:T(8,128)(2,1)S(1)}, bf16[128,256]{1,0:T(8,128)(2,1)S(1)}, u32[]{:S(2)}, u32[]{:S(2)}) collective-permute-start(bf16[128,256]{1,0:T(8,128)(2,1)S(1)} %fusion), channel_id=1, source_target_pairs={{0,64},{8,72},{16,80},{24,88},{32,96},{40,104},{48,112},{56,120},{... | collective-permute-start | bytes 196616 | tf_op jit(solution)/shard_map/ppermute | solution.py:438
  117.6 2.1 %collective-permute-done.26 = bf16[128,256]{1,0:T(8,128)(2,1)S(1)} collective-permute-done((bf16[128,256]{1,0:T(8,128)(2,1)S(1)}, bf16[128,256]{1,0:T(8,128)(2,1)S(1)}, u32[]{:S(2)}, u32[]{:S(2)}) %collective-permute-start.26) | collective-permute-done | bytes 65568 | tf_op jit(solution)/shard_map/ppermute | solution.py:438
  119.8 1.9 %collective-permute-done.27 = bf16[128,256]{1,0:T(8,128)(2,1)S(1)} collective-permute-done((bf16[128,256]{1,0:T(8,128)(2,1)S(1)}, bf16[128,256]{1,0:T(8,128)(2,1)S(1)}, u32[]{:S(2)}, u32[]{:S(2)}) %collective-permute-start.27) | collective-permute-done | bytes 65568 | tf_op jit(solution)/shard_map/ppermute | solution.py:438
  123.1 7.5 %collective-permute-done.29.column_ref = bf16[128,256]{1,0:T(8,128)(2,1)S(1)} collective-permute-done((bf16[128,256]{1,0:T(8,128)(2,1)S(1)}, bf16[128,256]{1,0:T(8,128)(2,1)S(1)}, u32[]{:S(2)}, u32[]{:S(2)}) %collective-permute-start.29) | collective-permute-done | bytes 65568 | tf_op jit(solution)/shard_map/ppermute | solution.py:448
  (83 shorter events, 28.3 us)
Async XLA Ops:
  6.8 14.9 %collective-permute-start.7 = (bf16[4,2,504,128]{3,2,1,0:T(8,128)(2,1)S(1)}, bf16[4,2,504,128]{3,2,1,0:T(8,128)(2,1)S(1)}, u32[]{:S(2)}, u32[]{:S(2)}) collective-permute-start(bf16[4,2,504,128]{3,2,1,0:T(8,128)(2,1)S(1)} %packgive.2), channel_id=1, source_target_pairs={{0,8},{8,0},{16,24},{24,16},{32,40},{40,32},{48,56},{56,48},{64,72... | collective-permute-start | bytes 3096584 | tf_op jit(solution)/shard_map/ppermute | solution.py:382
  9.3 13.3 %collective-permute-start.8 = (bf16[4,2,504,128]{3,2,1,0:T(8,128)(2,1)S(1)}, bf16[4,2,504,128]{3,2,1,0:T(8,128)(2,1)}, u32[]{:S(2)}, u32[]{:S(2)}) collective-permute-start(bf16[4,2,504,128]{3,2,1,0:T(8,128)(2,1)S(1)} %packgive.3), channel_id=1, source_target_pairs={{0,8},{8,0},{16,24},{24,16},{32,40},{40,32},{48,56},{56,48},{64,72... | collective-permute-start | bytes 3096584 | tf_op jit(solution)/shard_map/ppermute | solution.py:382
  9.9 61.7 %all-to-all-start = ((bf16[16,504,128]{2,1,0:T(8,128)(2,1)}), bf16[16,504,128]{2,1,0:T(8,128)(2,1)}, u32[]{:S(2)}, u32[]{:S(2)}) async-start(bf16[16,504,128]{2,1,0:T(8,128)(2,1)} %packcond.1), calls=%async_computation | async-start | bytes 4128768 | tf_op jit(solution)/shard_map/all_to_all | solution.py:375
  26.7 19.2 %collective-permute-start.10 = (bf16[2,504,128]{2,1,0:T(8,128)(2,1)S(1)}, bf16[2,504,128]{2,1,0:T(8,128)(2,1)S(1)}, u32[]{:S(2)}, u32[]{:S(2)}) collective-permute-start(bf16[2,504,128]{2,1,0:T(8,128)(2,1)S(1)} %get-tuple-element.69), channel_id=1, source_target_pairs={{0,32},{8,40},{16,48},{24,56},{32,0},{40,8},{48,16},{56,24},{64,96... | collective-permute-start | bytes 774152 | tf_op jit(solution)/shard_map/ppermute | solution.py:155
  28.5 26.8 %collective-permute-start.11 = (bf16[2,504,128]{2,1,0:T(8,128)(2,1)S(1)}, bf16[2,504,128]{2,1,0:T(8,128)(2,1)S(1)}, u32[]{:S(2)}, u32[]{:S(2)}) collective-permute-start(bf16[2,504,128]{2,1,0:T(8,128)(2,1)S(1)} %get-tuple-element.70), channel_id=1, source_target_pairs={{0,48},{8,56},{16,32},{24,40},{32,16},{40,24},{48,0},{56,8},{64,11... | collective-permute-start | bytes 774152 | tf_op jit(solution)/shard_map/ppermute | solution.py:155
  28.8 33.4 %collective-permute-start.12 = (bf16[2,504,128]{2,1,0:T(8,128)(2,1)}, bf16[2,504,128]{2,1,0:T(8,128)(2,1)S(1)}, u32[]{:S(2)}, u32[]{:S(2)}) collective-permute-start(bf16[2,504,128]{2,1,0:T(8,128)(2,1)} %get-tuple-element.71), channel_id=1, source_target_pairs={{0,64},{8,72},{16,80},{24,88},{32,96},{40,104},{48,112},{56,120},{... | collective-permute-start | bytes 774152 | tf_op jit(solution)/shard_map/ppermute | solution.py:155
  30.3 32.5 %collective-permute-start.13 = (bf16[2,504,128]{2,1,0:T(8,128)(2,1)}, bf16[2,504,128]{2,1,0:T(8,128)(2,1)S(1)}, u32[]{:S(2)}, u32[]{:S(2)}) collective-permute-start(bf16[2,504,128]{2,1,0:T(8,128)(2,1)} %get-tuple-element.72), channel_id=1, source_target_pairs={{0,80},{8,88},{16,64},{24,72},{32,112},{40,120},{48,96},{56,104},{... | collective-permute-start | bytes 774152 | tf_op jit(solution)/shard_map/ppermute | solution.py:155
  33.3 29.5 %collective-permute-start.14 = (bf16[2,504,128]{2,1,0:T(8,128)(2,1)S(1)}, bf16[2,504,128]{2,1,0:T(8,128)(2,1)S(1)}, u32[]{:S(2)}, u32[]{:S(2)}) collective-permute-start(bf16[2,504,128]{2,1,0:T(8,128)(2,1)S(1)} %get-tuple-element.73), channel_id=1, source_target_pairs={{0,96},{8,104},{16,112},{24,120},{32,64},{40,72},{48,80},{56,88},{... | collective-permute-start | bytes 774152 | tf_op jit(solution)/shard_map/ppermute | solution.py:155
  45.9 20.6 %collective-permute-start.15 = (bf16[2,504,128]{2,1,0:T(8,128)(2,1)S(1)}, bf16[2,504,128]{2,1,0:T(8,128)(2,1)S(1)}, u32[]{:S(2)}, u32[]{:S(2)}) collective-permute-start(bf16[2,504,128]{2,1,0:T(8,128)(2,1)S(1)} %get-tuple-element.74), channel_id=1, source_target_pairs={{0,112},{8,120},{16,96},{24,104},{32,80},{40,88},{48,64},{56,72},{... | collective-permute-start | bytes 774152 | tf_op jit(solution)/shard_map/ppermute | solution.py:155
  55.4 16.2 %collective-permute-start.9 = (bf16[2,504,128]{2,1,0:T(8,128)(2,1)S(1)}, bf16[2,504,128]{2,1,0:T(8,128)(2,1)S(1)}, u32[]{:S(2)}, u32[]{:S(2)}) collective-permute-start(bf16[2,504,128]{2,1,0:T(8,128)(2,1)S(1)} %get-tuple-element.68), channel_id=1, source_target_pairs={{0,16},{8,24},{16,0},{24,8},{32,48},{40,56},{48,32},{56,40},{64,80... | collective-permute-start | bytes 774152 | tf_op jit(solution)/shard_map/ppermute | solution.py:155
  84.1 2.0 %collective-permute-start.16 = (bf16[8,128,256]{2,1,0:T(8,128)(2,1)S(1)}, bf16[8,128,256]{2,1,0:T(8,128)(2,1)S(1)}, u32[]{:S(2)}, u32[]{:S(2)}) collective-permute-start(bf16[8,128,256]{2,1,0:T(8,128)(2,1)S(1)} %gelements.3), channel_id=1, source_target_pairs={{0,8},{8,0},{16,24},{24,16},{32,40},{40,32},{48,56},{56,48},{64,72... | collective-permute-start | bytes 1572872 | tf_op jit(solution)/shard_map/ppermute | solution.py:428
  86.2 11.7 %collective-permute-start.17 = (bf16[128,256]{1,0:T(8,128)(2,1)S(1)}, bf16[128,256]{1,0:T(8,128)(2,1)S(1)}, u32[]{:S(2)}, u32[]{:S(2)}) collective-permute-start(bf16[128,256]{1,0:T(8,128)(2,1)S(1)} %get-tuple-element.86), channel_id=1, source_target_pairs={{0,1},{1,0},{2,3},{3,2},{4,5},{5,4},{6,7},{7,6},{8,9},{9,8},{10,11... | collective-permute-start | bytes 196616 | tf_op jit(solution)/shard_map/ppermute | solution.py:433
  89.3 11.6 %collective-permute-start.18 = (bf16[128,256]{1,0:T(8,128)(2,1)S(1)}, bf16[128,256]{1,0:T(8,128)(2,1)S(1)}, u32[]{:S(2)}, u32[]{:S(2)}) collective-permute-start(bf16[128,256]{1,0:T(8,128)(2,1)S(1)} %get-tuple-element.87), channel_id=1, source_target_pairs={{0,2},{1,3},{2,0},{3,1},{4,6},{5,7},{6,4},{7,5},{8,10},{9,11},{10,... | collective-permute-start | bytes 196616 | tf_op jit(solution)/shard_map/ppermute | solution.py:433
  91.5 10.8 %collective-permute-start.19 = (bf16[128,256]{1,0:T(8,128)(2,1)S(1)}, bf16[128,256]{1,0:T(8,128)(2,1)S(1)}, u32[]{:S(2)}, u32[]{:S(2)}) collective-permute-start(bf16[128,256]{1,0:T(8,128)(2,1)S(1)} %get-tuple-element.88), channel_id=1, source_target_pairs={{0,3},{1,2},{2,1},{3,0},{4,7},{5,6},{6,5},{7,4},{8,11},{9,10},{10,... | collective-permute-start | bytes 196616 | tf_op jit(solution)/shard_map/ppermute | solution.py:433
  92.0 10.4 %collective-permute-start.20 = (bf16[128,256]{1,0:T(8,128)(2,1)S(1)}, bf16[128,256]{1,0:T(8,128)(2,1)S(1)}, u32[]{:S(2)}, u32[]{:S(2)}) collective-permute-start(bf16[128,256]{1,0:T(8,128)(2,1)S(1)} %get-tuple-element.89), channel_id=1, source_target_pairs={{0,4},{1,5},{2,6},{3,7},{4,0},{5,1},{6,2},{7,3},{8,12},{9,13},{10,... | collective-permute-start | bytes 196616 | tf_op jit(solution)/shard_map/ppermute | solution.py:433
  95.2 8.2 %collective-permute-start.21 = (bf16[128,256]{1,0:T(8,128)(2,1)S(1)}, bf16[128,256]{1,0:T(8,128)(2,1)S(1)}, u32[]{:S(2)}, u32[]{:S(2)}) collective-permute-start(bf16[128,256]{1,0:T(8,128)(2,1)S(1)} %get-tuple-element.90), channel_id=1, source_target_pairs={{0,5},{1,4},{2,7},{3,6},{4,1},{5,0},{6,3},{7,2},{8,13},{9,12},{10,... | collective-permute-start | bytes 196616 | tf_op jit(solution)/shard_map/ppermute | solution.py:433
  97.9 6.8 %collective-permute-start.22 = (bf16[128,256]{1,0:T(8,128)(2,1)S(1)}, bf16[128,256]{1,0:T(8,128)(2,1)S(1)}, u32[]{:S(2)}, u32[]{:S(2)}) collective-permute-start(bf16[128,256]{1,0:T(8,128)(2,1)S(1)} %get-tuple-element.91), channel_id=1, source_target_pairs={{0,6},{1,7},{2,4},{3,5},{4,2},{5,3},{6,0},{7,1},{8,14},{9,15},{10,... | collective-permute-start | bytes 196616 | tf_op jit(solution)/shard_map/ppermute | solution.py:433
  100.9 7.9 %collective-permute-start.23 = (bf16[128,256]{1,0:T(8,128)(2,1)S(1)}, bf16[128,256]{1,0:T(8,128)(2,1)S(1)}, u32[]{:S(2)}, u32[]{:S(2)}) collective-permute-start(bf16[128,256]{1,0:T(8,128)(2,1)S(1)} %get-tuple-element.92), channel_id=1, source_target_pairs={{0,7},{1,6},{2,5},{3,4},{4,3},{5,2},{6,1},{7,0},{8,15},{9,14},{10,... | collective-permute-start | bytes 196616 | tf_op jit(solution)/shard_map/ppermute | solution.py:433
  108.9 4.3 %collective-permute-start.24 = (bf16[128,256]{1,0:T(8,128)(2,1)S(1)}, bf16[128,256]{1,0:T(8,128)(2,1)S(1)}, u32[]{:S(2)}, u32[]{:S(2)}) collective-permute-start(bf16[128,256]{1,0:T(8,128)(2,1)S(1)} %get-tuple-element.93), channel_id=1, source_target_pairs={{0,16},{8,24},{16,0},{24,8},{32,48},{40,56},{48,32},{56,40},{64,80... | collective-permute-start | bytes 196616 | tf_op jit(solution)/shard_map/ppermute | solution.py:434
  113.3 4.3 %collective-permute-start.25 = (bf16[128,256]{1,0:T(8,128)(2,1)S(1)}, bf16[128,256]{1,0:T(8,128)(2,1)S(1)}, u32[]{:S(2)}, u32[]{:S(2)}) collective-permute-start(bf16[128,256]{1,0:T(8,128)(2,1)S(1)} %fusion), channel_id=1, source_target_pairs={{0,32},{8,40},{16,48},{24,56},{32,64},{40,72},{48,80},{56,88},{64,... | collective-permute-start | bytes 196616 | tf_op jit(solution)/shard_map/ppermute | solution.py:438
  114.0 5.8 %collective-permute-start.26 = (bf16[128,256]{1,0:T(8,128)(2,1)S(1)}, bf16[128,256]{1,0:T(8,128)(2,1)S(1)}, u32[]{:S(2)}, u32[]{:S(2)}) collective-permute-start(bf16[128,256]{1,0:T(8,128)(2,1)S(1)} %fusion), channel_id=1, source_target_pairs={{0,64},{8,72},{16,80},{24,88},{32,96},{40,104},{48,112},{56,120},{... | collective-permute-start | bytes 196616 | tf_op jit(solution)/shard_map/ppermute | solution.py:438
  116.3 5.5 %collective-permute-start.27 = (bf16[128,256]{1,0:T(8,128)(2,1)S(1)}, bf16[128,256]{1,0:T(8,128)(2,1)S(1)}, u32[]{:S(2)}, u32[]{:S(2)}) collective-permute-start(bf16[128,256]{1,0:T(8,128)(2,1)S(1)} %fusion), channel_id=1, source_target_pairs={{0,96},{8,104},{16,112},{24,120},{32,0},{40,8},{48,16},{56,24},{64... | collective-permute-start | bytes 196616 | tf_op jit(solution)/shard_map/ppermute | solution.py:438
  121.8 1.3 %collective-permute-start.28 = (bf16[128,256]{1,0:T(8,128)(2,1)S(1)}, bf16[128,256]{1,0:T(8,128)(2,1)S(1)}, u32[]{:S(2)}, u32[]{:S(2)}) collective-permute-start(bf16[128,256]{1,0:T(8,128)(2,1)S(1)} %add_convert_fusion.mine_ref), channel_id=1, source_target_pairs={{0,8},{8,0},{16,24},{24,16},{32,40},{40,32},{48,56},{56,48},{64,72... | collective-permute-start | bytes 196616 | tf_op jit(solution)/shard_map/ppermute | solution.py:449
  121.9 8.7 %collective-permute-start.29 = (bf16[128,256]{1,0:T(8,128)(2,1)S(1)}, bf16[128,256]{1,0:T(8,128)(2,1)S(1)}, u32[]{:S(2)}, u32[]{:S(2)}) collective-permute-start(bf16[128,256]{1,0:T(8,128)(2,1)S(1)} %add_convert_fusion.mine_ref), channel_id=1, source_target_pairs={{0,4},{1,20},{2,32},{3,48},{4,68},{5,84},{6,96},{7,112},{8,12},{9,... | collective-permute-start | bytes 196616 | tf_op jit(solution)/shard_map/ppermute | solution.py:448
  (8 other events, 177.4 us)

commit v6 on v4

--- a/solution.py
+++ b/solution.py
@@ -19,6 +19,7 @@
 PAIRS = 64
 PACK = 8
 CHIPS = 8
+ORDER = (0, 2, 6, 4, 1, 3, 7, 5)
 CONDS = 4
 SLOTS = 12
 KROWS = 24
@@ -150,7 +151,7 @@
 
 def send_to_chips(pieces):
     got = [pieces[0]]
-    for s in range(1, CHIPS):
+    for s in ORDER[1:]:
         got.append(lax.ppermute(pieces[s], "band", [(b, b ^ (2 * s)) for b in range(PARTS)]))
     return got
 
@@ -170,12 +171,12 @@
     cond_ref, table_ref, ytab_ref, out_ref, raw_ref, val_main, val_tail, low_ref, high_ref = refs[CHIPS + 1 :]
     step = pl.program_id(0)
 
-    for s in range(CHIPS):
+    for slot, s in enumerate(ORDER):
         for r in range(2):
 
             @pl.when((step == 0) & (where_ref[r] == s))
             def _():
-                raw_ref[r] = val_refs[s][...]
+                raw_ref[r] = val_refs[slot][...]
 
     @pl.when((step == 0) & (where_ref[2] == 1))
     def _():
@@ -370,8 +371,8 @@
         place = jnp.stack([core, chip, (second == band_pos).astype(jnp.int32)])
         again = send_to_chips(pack_choice(bands, place, sibling))
         found = again[0]
-        for s in range(1, CHIPS):
-            found = jnp.where((second >> 1) == chip ^ s, again[s], found)
+        for slot, s in enumerate(ORDER[1:], 1):
+            found = jnp.where((second >> 1) == chip ^ s, again[slot], found)
         return found
 
     def nothing_more(operands):

time: 124 us -> 123 us (level)
  waiting for transfers between devices: 47.3 us -> 44 us
  starting transfers between devices: 32.8 us -> 36 us
    ppermute x7, waiting for transfers between devices: 26 us -> 22 us  [send_to_chips(): lax.ppermute(pieces[s], 'band', [(b, b ^ 2 * s) for b in range(PARTS)])]
    ppermute x3, starting transfers between devices: 3.3 us -> 6.19 us  [shards(): block = block + lax.ppermute(narrow, 'band', step).astype(F32)]
    ppermute x1, starting transfers between devices: 1.78 us -> 3.28 us  [shards(): lax.ppermute(block.astype(BF), 'band', [(b, b ^ 2) for b in range(PARTS)])]
    ppermute x1, waiting for transfers between devices: 5.14 us -> 6.57 us  [shards(): column = lax.ppermute(narrow, ('band', 'grid'), far)]
    ppermute x1, starting transfers between devices: 3.68 us -> 2.25 us  [shards(): column = lax.ppermute(narrow, ('band', 'grid'), far)]
  transfers between devices with their start and end apart: 18 -> 18, of which waited for: 12 -> 10; matrix products, arithmetic and copies ran while one was open for 7% -> 7% of each run, Pallas kernels for 8% -> 8%
where the time goes in v6:
time: 123 us; the launch traced here: 121 us
  waiting for transfers between devices  44 us (36%)
  starting transfers between devices  36 us (29%)
  Pallas kernels  25.9 us (21%)
  local copies, waits for them, and re-layouts  5.63 us (5%)
  other arithmetic  5 us (4%)
  between operations  4.72 us (4%)
    ppermute x7, waiting for transfers between devices, send_to_chips(): lax.ppermute(pieces[s], 'band', [(b, b ^ 2 * s) for b in range(PARTS)])  22 us
    ppermute x7, starting transfers between devices, send_to_chips(): lax.ppermute(pieces[s], 'band', [(b, b ^ 2 * s) for b in range(PARTS)])  10.8 us
    pallas_call x1, Pallas kernels, z_transform(): pl.pallas_call(z_kernel, out_shape=jax.ShapeDtypeStruct((256, 512), BF),...  10.3 us
    all_to_all x1, waiting for transfers between devices, shards(): parts = lax.all_to_all(parts, 'grid', 0, 0, tiled=True)  9.16 us
    all_to_all x1, starting transfers between devices, shards(): parts = lax.all_to_all(parts, 'grid', 0, 0, tiled=True)  6.89 us
    ppermute x1, waiting for transfers between devices, shards(): column = lax.ppermute(narrow, ('band', 'grid'), far)  6.57 us
    ppermute x3, starting transfers between devices, shards(): block = block + lax.ppermute(narrow, 'band', step).astype(F32)  6.19 us
    all_to_all x1, starting transfers between devices, shards(): cond_wire = lax.all_to_all(cond_wire, 'band', 0, 0, tiled=True)  5.7 us
  transfers between devices with their start and end apart: 18, of which 10 were waited for; matrix products, arithmetic and copies ran while one was open for 7% of the time, Pallas kernels for 8%

profile of v6, /device:TPU:38, one launch (start us, length us, event | category | flops | bytes accessed | tf_op | source)
XLA Modules:
  0.0 121.3 jit_solution(13516192202947441431)
XLA Ops:
  0.7 3.5 %packcond.1 = bf16[16,504,128]{2,1,0:T(8,128)(2,1)} custom-call(s32[1]{0:T(128)S(6)} %copy.31.number_ref, bf16[2,3200,160]{2,1,0:T(8,128)(2,1)} %bitcast.39), custom_call_target="tpu_custom_call" | custom-call | bytes 6000000 | tf_op jit(solution)/shard_map/packcond/pallas_call | solution.py:81
  4.2 5.7 %all-to-all-start = ((bf16[16,504,128]{2,1,0:T(8,128)(2,1)}), bf16[16,504,128]{2,1,0:T(8,128)(2,1)}, u32[]{:S(2)}, u32[]{:S(2)}) async-start(bf16[16,504,128]{2,1,0:T(8,128)(2,1)} %packcond.1), calls=%async_computation | async-start | bytes 4128768 | tf_op jit(solution)/shard_map/all_to_all | solution.py:355
  9.9 2.5 %packgive.2 = bf16[4,2,504,128]{3,2,1,0:T(8,128)(2,1)S(1)} custom-call(s32[2]{0:T(128)S(1)} %pad_add_fusion.2.place_ref, bf16[2,2,8,2,200,160]{5,4,3,2,1,0:T(8,128)(2,1)} %bitcast.35), custom_call_target="tpu_custom_call" | custom-call | bytes 3000000 | tf_op jit(solution)/shard_map/packgive/pallas_call | solution.py:104
  12.7 2.5 %packgive.3 = bf16[4,2,504,128]{3,2,1,0:T(8,128)(2,1)S(1)} custom-call(s32[2]{0:T(128)S(1)} %pad_add_fusion.2.place_ref, bf16[2,2,8,2,200,160]{5,4,3,2,1,0:T(8,128)(2,1)} %bitcast.36), custom_call_target="tpu_custom_call" | custom-call | bytes 3000000 | tf_op jit(solution)/shard_map/packgive/pallas_call | solution.py:104
  19.4 4.0 %packchoice.3 = (bf16[2,504,128]{2,1,0:T(8,128)(2,1)S(1)}, bf16[2,504,128]{2,1,0:T(8,128)(2,1)}, bf16[2,504,128]{2,1,0:T(8,128)(2,1)S(1)}, bf16[2,504,128]{2,1,0...) custom-call(s32[3]{0:T(128)S(1)} %pad_add_fusion.1.place_ref, ...), custom_call_target="tpu_custom_call" | custom-call | bytes 8000000 | tf_op jit(solution)/shard_map/packchoice/pallas_call | solution.py:136
  24.3 1.2 collective-permute-start.10
  29.0 2.1 %collective-permute-start.11 = (bf16[2,504,128]{2,1,0:T(8,128)(2,1)}, bf16[2,504,128]{2,1,0:T(8,128)(2,1)S(1)}, u32[]{:S(2)}, u32[]{:S(2)}) collective-permute-start(bf16[2,504,128]{2,1,0:T(8,128)(2,1)} %get-tuple-element.62), channel_id=1, source_target_pairs={{0,64},{8,72},{16,80},{24,88},{32,96},{40,104},{48,112},{56,120},{... | collective-permute-start | bytes 774152 | tf_op jit(solution)/shard_map/ppermute | solution.py:155
  31.7 1.8 %collective-permute-start.13 = (bf16[2,504,128]{2,1,0:T(8,128)(2,1)S(1)}, bf16[2,504,128]{2,1,0:T(8,128)(2,1)S(1)}, u32[]{:S(2)}, u32[]{:S(2)}) collective-permute-start(bf16[2,504,128]{2,1,0:T(8,128)(2,1)S(1)} %get-tuple-element.64), channel_id=1, source_target_pairs={{0,48},{8,56},{16,32},{24,40},{32,16},{40,24},{48,0},{56,8},{64,11... | collective-permute-start | bytes 774152 | tf_op jit(solution)/shard_map/ppermute | solution.py:155
  33.4 6.7 %collective-permute-done.9.refs_1_ = bf16[2,504,128]{2,1,0:T(8,128)(2,1)S(1)} collective-permute-done((bf16[2,504,128]{2,1,0:T(8,128)(2,1)S(1)}, bf16[2,504,128]{2,1,0:T(8,128)(2,1)S(1)}, u32[]{:S(2)}, u32[]{:S(2)}) %collective-permute-start.9) | collective-permute-done | bytes 258080 | tf_op jit(solution)/shard_map/ppermute | solution.py:155
  40.1 1.2 collective-permute-start.14
  41.3 3.3 %collective-permute-start.15 = (bf16[2,504,128]{2,1,0:T(8,128)(2,1)S(1)}, bf16[2,504,128]{2,1,0:T(8,128)(2,1)S(1)}, u32[]{:S(2)}, u32[]{:S(2)}) collective-permute-start(bf16[2,504,128]{2,1,0:T(8,128)(2,1)S(1)} %get-tuple-element.66), channel_id=1, source_target_pairs={{0,80},{8,88},{16,64},{24,72},{32,112},{40,120},{48,96},{56,104},{... | collective-permute-start | bytes 774152 | tf_op jit(solution)/shard_map/ppermute | solution.py:155
  47.9 13.5 %collective-permute-done.13.refs_5_ = bf16[2,504,128]{2,1,0:T(8,128)(2,1)S(1)} collective-permute-done((bf16[2,504,128]{2,1,0:T(8,128)(2,1)S(1)}, bf16[2,504,128]{2,1,0:T(8,128)(2,1)S(1)}, u32[]{:S(2)}, u32[]{:S(2)}) %collective-permute-start.13) | collective-permute-done | bytes 258080 | tf_op jit(solution)/shard_map/ppermute | solution.py:155
  63.2 10.3 %ztransform.1.plane_ref = bf16[256,512]{1,0:T(8,128)(2,1)S(1)} custom-call(s32[3]{0:T(128)S(1)} %pad_add_fusion.3.where_ref, bf16[2,504,128]{2,1,0:T(8,128)(2,1)S(1)} %get-tuple-element.68.refs_0_, bf16[2,504,128]{2,1,0:T(8,128)(2,1)S(1)} %collective-permute-done.9.refs_1_, bf16[2,504,128]{2,1,0:T(8,128)(2,1)S(1)} %collective-permute-done.10.refs_2_, ...), custom_call_target="tpu_custom_call" | custom-call | tf_op jit(solution)/shard_map/ztransform/pallas_call | solution.py:248
  77.3 6.9 %all-to-all-start.1 = ((bf16[8,128,256]{2,1,0:T(8,128)(2,1)}), bf16[8,128,256]{2,1,0:T(8,128)(2,1)S(1)}, u32[]{:S(2)}, u32[]{:S(2)}) async-start(bf16[8,128,256]{2,1,0:T(8,128)(2,1)} %add_convert_fusion), calls=%async_computation.1 | async-start | bytes 1048576 | tf_op jit(solution)/shard_map/all_to_all | solution.py:411
  85.0 1.2 convert_reduce_fusion.1
  86.2 9.2 %all-to-all-done.1 = bf16[8,128,256]{2,1,0:T(8,128)(2,1)S(1)} async-done(((bf16[8,128,256]{2,1,0:T(8,128)(2,1)}), bf16[8,128,256]{2,1,0:T(8,128)(2,1)S(1)}, u32[]{:S(2)}, u32[]{:S(2)}) %all-to-all-start.1) | async-done | bytes 524320 | tf_op jit(solution)/shard_map/all_to_all | solution.py:411
  95.4 3.3 %collective-permute-start.17 = (bf16[128,256]{1,0:T(8,128)(2,1)S(1)}, bf16[128,256]{1,0:T(8,128)(2,1)S(1)}, u32[]{:S(2)}, u32[]{:S(2)}) collective-permute-start(bf16[128,256]{1,0:T(8,128)(2,1)S(1)} %convert_element_type.71), channel_id=1, source_target_pairs={{0,16},{8,24},{16,0},{24,8},{32,48},{40,56},{48,32},{56,40},{64,80... | collective-permute-start | bytes 196616 | tf_op jit(solution)/shard_map/ppermute | solution.py:413
  98.9 2.1 %collective-permute-done.17 = bf16[128,256]{1,0:T(8,128)(2,1)S(1)} collective-permute-done((bf16[128,256]{1,0:T(8,128)(2,1)S(1)}, bf16[128,256]{1,0:T(8,128)(2,1)S(1)}, u32[]{:S(2)}, u32[]{:S(2)}) %collective-permute-start.17) | collective-permute-done | bytes 65568 | tf_op jit(solution)/shard_map/ppermute | solution.py:413
  101.1 5.3 %collective-permute-start.19 = (bf16[128,256]{1,0:T(8,128)(2,1)S(1)}, bf16[128,256]{1,0:T(8,128)(2,1)S(1)}, u32[]{:S(2)}, u32[]{:S(2)}) collective-permute-start(bf16[128,256]{1,0:T(8,128)(2,1)S(1)} %fusion), channel_id=1, source_target_pairs={{0,64},{8,72},{16,80},{24,88},{32,96},{40,104},{48,112},{56,120},{... | collective-permute-start | bytes 196616 | tf_op jit(solution)/shard_map/ppermute | solution.py:417
  107.4 1.9 %collective-permute-done.19 = bf16[128,256]{1,0:T(8,128)(2,1)S(1)} collective-permute-done((bf16[128,256]{1,0:T(8,128)(2,1)S(1)}, bf16[128,256]{1,0:T(8,128)(2,1)S(1)}, u32[]{:S(2)}, u32[]{:S(2)}) %collective-permute-start.19) | collective-permute-done | bytes 65568 | tf_op jit(solution)/shard_map/ppermute | solution.py:417
  109.3 1.3 %collective-permute-done.18 = bf16[128,256]{1,0:T(8,128)(2,1)S(1)} collective-permute-done((bf16[128,256]{1,0:T(8,128)(2,1)S(1)}, bf16[128,256]{1,0:T(8,128)(2,1)S(1)}, u32[]{:S(2)}, u32[]{:S(2)}) %collective-permute-start.18) | collective-permute-done | bytes 65568 | tf_op jit(solution)/shard_map/ppermute | solution.py:417
  110.8 2.2 %collective-permute-start.22 = (bf16[128,256]{1,0:T(8,128)(2,1)S(1)}, bf16[128,256]{1,0:T(8,128)(2,1)S(1)}, u32[]{:S(2)}, u32[]{:S(2)}) collective-permute-start(bf16[128,256]{1,0:T(8,128)(2,1)S(1)} %add_convert_fusion.1.mine_ref), channel_id=1, source_target_pairs={{0,4},{1,20},{2,32},{3,48},{4,68},{5,84},{6,96},{7,112},{8,12},{9,... | collective-permute-start | bytes 196616 | tf_op jit(solution)/shard_map/ppermute | solution.py:427
  113.2 6.6 %collective-permute-done.22.column_ref = bf16[128,256]{1,0:T(8,128)(2,1)S(1)} collective-permute-done((bf16[128,256]{1,0:T(8,128)(2,1)S(1)}, bf16[128,256]{1,0:T(8,128)(2,1)S(1)}, u32[]{:S(2)}, u32[]{:S(2)}) %collective-permute-start.22) | collective-permute-done | bytes 65568 | tf_op jit(solution)/shard_map/ppermute | solution.py:427
  119.8 1.5 %chi.1 = f32[2,512,256]{2,1,0:T(8,128)} custom-call(s32[1]{0:T(128)} %bitcast.3.parity_ref.core_ref, bf16[128,256]{1,0:T(8,128)(2,1)S(1)} %add_convert_fusion.1.mine_ref, bf16[128,256]{1,0:T(8,128)(2,1)S(1)} %collective-permute-done.21.other_ref, bf16[128,256]{1,0:T(8,128)(2,1)S(1)} %collective-permute-done.22.column_ref, f32[128,1]{1,0:T(8,128)S(1)} %copy.28.weight_ref), custom_call_target="tpu_custom_call" | custom-call | tf_op jit(solution)/shard_map/chi/pallas_call | solution.py:332
  (62 shorter events, 17.8 us)
Async XLA Ops:
  0.0 84.3 %copy-start = (f32[32]{0:T(128)S(1)}, f32[32]{0:T(128)}, u32[]{:S(2)}) copy-start(f32[32]{0:T(128)} %param.13) | copy-start | bytes 388
  4.2 58.2 %all-to-all-start = ((bf16[16,504,128]{2,1,0:T(8,128)(2,1)}), bf16[16,504,128]{2,1,0:T(8,128)(2,1)}, u32[]{:S(2)}, u32[]{:S(2)}) async-start(bf16[16,504,128]{2,1,0:T(8,128)(2,1)} %packcond.1), calls=%async_computation | async-start | bytes 4128768 | tf_op jit(solution)/shard_map/all_to_all | solution.py:355
  12.4 3.2 %copy-start.3 = (s32[3,4096]{1,0:T(4,128)S(1)}, s32[3,4096]{1,0:T(4,128)}, u32[]{:S(2)}) copy-start(s32[3,4096]{1,0:T(4,128)} %param.17) | copy-start | bytes 147460
  12.4 4.2 %copy-start.4 = (s32[2]{0:T(128)S(1)}, s32[2]{0:T(128)}, u32[]{:S(2)}) copy-start(s32[2]{0:T(128)} %param.16) | copy-start | bytes 28
  12.4 7.0 %collective-permute-start.7 = (bf16[4,2,504,128]{3,2,1,0:T(8,128)(2,1)S(1)}, bf16[4,2,504,128]{3,2,1,0:T(8,128)(2,1)}, u32[]{:S(2)}, u32[]{:S(2)}) collective-permute-start(bf16[4,2,504,128]{3,2,1,0:T(8,128)(2,1)S(1)} %packgive.2), channel_id=1, source_target_pairs={{0,8},{8,0},{16,24},{24,16},{32,40},{40,32},{48,56},{56,48},{64,72... | collective-permute-start | bytes 3096584 | tf_op jit(solution)/shard_map/ppermute | solution.py:362
  15.1 4.3 %collective-permute-start.8 = (bf16[4,2,504,128]{3,2,1,0:T(8,128)(2,1)S(1)}, bf16[4,2,504,128]{3,2,1,0:T(8,128)(2,1)}, u32[]{:S(2)}, u32[]{:S(2)}) collective-permute-start(bf16[4,2,504,128]{3,2,1,0:T(8,128)(2,1)S(1)} %packgive.3), channel_id=1, source_target_pairs={{0,8},{8,0},{16,24},{24,16},{32,40},{40,32},{48,56},{56,48},{64,72... | collective-permute-start | bytes 3096584 | tf_op jit(solution)/shard_map/ppermute | solution.py:362
  23.4 16.7 %collective-permute-start.9 = (bf16[2,504,128]{2,1,0:T(8,128)(2,1)S(1)}, bf16[2,504,128]{2,1,0:T(8,128)(2,1)S(1)}, u32[]{:S(2)}, u32[]{:S(2)}) collective-permute-start(bf16[2,504,128]{2,1,0:T(8,128)(2,1)S(1)} %get-tuple-element.60), channel_id=1, source_target_pairs={{0,32},{8,40},{16,48},{24,56},{32,0},{40,8},{48,16},{56,24},{64,96... | collective-permute-start | bytes 774152 | tf_op jit(solution)/shard_map/ppermute | solution.py:155
  24.3 17.0 %collective-permute-start.10 = (bf16[2,504,128]{2,1,0:T(8,128)(2,1)S(1)}, bf16[2,504,128]{2,1,0:T(8,128)(2,1)S(1)}, u32[]{:S(2)}, u32[]{:S(2)}) collective-permute-start(bf16[2,504,128]{2,1,0:T(8,128)(2,1)S(1)} %get-tuple-element.61), channel_id=1, source_target_pairs={{0,96},{8,104},{16,112},{24,120},{32,64},{40,72},{48,80},{56,88},{... | collective-permute-start | bytes 774152 | tf_op jit(solution)/shard_map/ppermute | solution.py:155
  29.0 18.8 %collective-permute-start.11 = (bf16[2,504,128]{2,1,0:T(8,128)(2,1)}, bf16[2,504,128]{2,1,0:T(8,128)(2,1)S(1)}, u32[]{:S(2)}, u32[]{:S(2)}) collective-permute-start(bf16[2,504,128]{2,1,0:T(8,128)(2,1)} %get-tuple-element.62), channel_id=1, source_target_pairs={{0,64},{8,72},{16,80},{24,88},{32,96},{40,104},{48,112},{56,120},{... | collective-permute-start | bytes 774152 | tf_op jit(solution)/shard_map/ppermute | solution.py:155
  31.1 16.7 %collective-permute-start.12 = (bf16[2,504,128]{2,1,0:T(8,128)(2,1)}, bf16[2,504,128]{2,1,0:T(8,128)(2,1)S(1)}, u32[]{:S(2)}, u32[]{:S(2)}) collective-permute-start(bf16[2,504,128]{2,1,0:T(8,128)(2,1)} %get-tuple-element.63), channel_id=1, source_target_pairs={{0,16},{8,24},{16,0},{24,8},{32,48},{40,56},{48,32},{56,40},{64,80... | collective-permute-start | bytes 774152 | tf_op jit(solution)/shard_map/ppermute | solution.py:155
  31.7 29.7 %collective-permute-start.13 = (bf16[2,504,128]{2,1,0:T(8,128)(2,1)S(1)}, bf16[2,504,128]{2,1,0:T(8,128)(2,1)S(1)}, u32[]{:S(2)}, u32[]{:S(2)}) collective-permute-start(bf16[2,504,128]{2,1,0:T(8,128)(2,1)S(1)} %get-tuple-element.64), channel_id=1, source_target_pairs={{0,48},{8,56},{16,32},{24,40},{32,16},{40,24},{48,0},{56,8},{64,11... | collective-permute-start | bytes 774152 | tf_op jit(solution)/shard_map/ppermute | solution.py:155
  40.1 22.3 %collective-permute-start.14 = (bf16[2,504,128]{2,1,0:T(8,128)(2,1)S(1)}, bf16[2,504,128]{2,1,0:T(8,128)(2,1)S(1)}, u32[]{:S(2)}, u32[]{:S(2)}) collective-permute-start(bf16[2,504,128]{2,1,0:T(8,128)(2,1)S(1)} %get-tuple-element.65), channel_id=1, source_target_pairs={{0,112},{8,120},{16,96},{24,104},{32,80},{40,88},{48,64},{56,72},{... | collective-permute-start | bytes 774152 | tf_op jit(solution)/shard_map/ppermute | solution.py:155
  41.3 21.1 %collective-permute-start.15 = (bf16[2,504,128]{2,1,0:T(8,128)(2,1)S(1)}, bf16[2,504,128]{2,1,0:T(8,128)(2,1)S(1)}, u32[]{:S(2)}, u32[]{:S(2)}) collective-permute-start(bf16[2,504,128]{2,1,0:T(8,128)(2,1)S(1)} %get-tuple-element.66), channel_id=1, source_target_pairs={{0,80},{8,88},{16,64},{24,72},{32,112},{40,120},{48,96},{56,104},{... | collective-permute-start | bytes 774152 | tf_op jit(solution)/shard_map/ppermute | solution.py:155
  74.3 2.0 %collective-permute-start.16 = (bf16[8,128,256]{2,1,0:T(8,128)(2,1)S(1)}, bf16[8,128,256]{2,1,0:T(8,128)(2,1)S(1)}, u32[]{:S(2)}, u32[]{:S(2)}) collective-permute-start(bf16[8,128,256]{2,1,0:T(8,128)(2,1)S(1)} %gelements.3), channel_id=1, source_target_pairs={{0,8},{8,0},{16,24},{24,16},{32,40},{40,32},{48,56},{56,48},{64,72... | collective-permute-start | bytes 1572872 | tf_op jit(solution)/shard_map/ppermute | solution.py:408
  75.3 23.4 %copy-start.5 = (f32[16]{0:T(128)S(1)}, f32[16]{0:T(128)}, u32[]{:S(2)}) copy-start(f32[16]{0:T(128)} %param.14) | copy-start | bytes 196
  77.3 18.1 %all-to-all-start.1 = ((bf16[8,128,256]{2,1,0:T(8,128)(2,1)}), bf16[8,128,256]{2,1,0:T(8,128)(2,1)S(1)}, u32[]{:S(2)}, u32[]{:S(2)}) async-start(bf16[8,128,256]{2,1,0:T(8,128)(2,1)} %add_convert_fusion), calls=%async_computation.1 | async-start | bytes 1048576 | tf_op jit(solution)/shard_map/all_to_all | solution.py:411
  95.4 5.5 %collective-permute-start.17 = (bf16[128,256]{1,0:T(8,128)(2,1)S(1)}, bf16[128,256]{1,0:T(8,128)(2,1)S(1)}, u32[]{:S(2)}, u32[]{:S(2)}) collective-permute-start(bf16[128,256]{1,0:T(8,128)(2,1)S(1)} %convert_element_type.71), channel_id=1, source_target_pairs={{0,16},{8,24},{16,0},{24,8},{32,48},{40,56},{48,32},{56,40},{64,80... | collective-permute-start | bytes 196616 | tf_op jit(solution)/shard_map/ppermute | solution.py:413
  101.0 6.4 %collective-permute-start.20 = (bf16[128,256]{1,0:T(8,128)(2,1)S(1)}, bf16[128,256]{1,0:T(8,128)(2,1)S(1)}, u32[]{:S(2)}, u32[]{:S(2)}) collective-permute-start(bf16[128,256]{1,0:T(8,128)(2,1)S(1)} %fusion), channel_id=1, source_target_pairs={{0,96},{8,104},{16,112},{24,120},{32,0},{40,8},{48,16},{56,24},{64... | collective-permute-start | bytes 196616 | tf_op jit(solution)/shard_map/ppermute | solution.py:417
  101.1 8.2 %collective-permute-start.19 = (bf16[128,256]{1,0:T(8,128)(2,1)S(1)}, bf16[128,256]{1,0:T(8,128)(2,1)S(1)}, u32[]{:S(2)}, u32[]{:S(2)}) collective-permute-start(bf16[128,256]{1,0:T(8,128)(2,1)S(1)} %fusion), channel_id=1, source_target_pairs={{0,64},{8,72},{16,80},{24,88},{32,96},{40,104},{48,112},{56,120},{... | collective-permute-start | bytes 196616 | tf_op jit(solution)/shard_map/ppermute | solution.py:417
  106.4 4.3 %collective-permute-start.18 = (bf16[128,256]{1,0:T(8,128)(2,1)S(1)}, bf16[128,256]{1,0:T(8,128)(2,1)S(1)}, u32[]{:S(2)}, u32[]{:S(2)}) collective-permute-start(bf16[128,256]{1,0:T(8,128)(2,1)S(1)} %fusion), channel_id=1, source_target_pairs={{0,32},{8,40},{16,48},{24,56},{32,64},{40,72},{48,80},{56,88},{64,... | collective-permute-start | bytes 196616 | tf_op jit(solution)/shard_map/ppermute | solution.py:417
  110.7 2.5 %collective-permute-start.21 = (bf16[128,256]{1,0:T(8,128)(2,1)S(1)}, bf16[128,256]{1,0:T(8,128)(2,1)S(1)}, u32[]{:S(2)}, u32[]{:S(2)}) collective-permute-start(bf16[128,256]{1,0:T(8,128)(2,1)S(1)} %add_convert_fusion.1.mine_ref), channel_id=1, source_target_pairs={{0,8},{8,0},{16,24},{24,16},{32,40},{40,32},{48,56},{56,48},{64,72... | collective-permute-start | bytes 196616 | tf_op jit(solution)/shard_map/ppermute | solution.py:428
  110.8 9.0 %collective-permute-start.22 = (bf16[128,256]{1,0:T(8,128)(2,1)S(1)}, bf16[128,256]{1,0:T(8,128)(2,1)S(1)}, u32[]{:S(2)}, u32[]{:S(2)}) collective-permute-start(bf16[128,256]{1,0:T(8,128)(2,1)S(1)} %add_convert_fusion.1.mine_ref), channel_id=1, source_target_pairs={{0,4},{1,20},{2,32},{3,48},{4,68},{5,84},{6,96},{7,112},{8,12},{9,... | collective-permute-start | bytes 196616 | tf_op jit(solution)/shard_map/ppermute | solution.py:427

commit v7 on v6

--- a/solution.py
+++ b/solution.py
@@ -310,7 +310,7 @@
     )(parity, plane, index, phase)
 
 
-def chi_kernel(core_ref, mine_ref, other_ref, column_ref, weight_ref, out_ref):
+def chi_kernel(core_ref, mine_ref, column_ref, other_ref, weight_ref, out_ref):
     real = column_ref[...].astype(F32) * weight_ref[...]
     imag = jnp.concatenate([-real[PAIRS:], real[:PAIRS]], axis=0)
     sides = []
@@ -340,7 +340,7 @@
         ),
         compiler_params=pltpu.CompilerParams(vmem_limit_bytes=8 * 2**20),
         name="chi",
-    )(core, mine, other, column, weight)
+    )(core, mine, column, other, weight)
 
 
 def shards(valence, conduction, val_energy, cond_energy, cond_band, owners, gvectors):

time: 123 us -> 122 us (level)
  no operation moved by 1% of the time
where the time goes in v7:
time: 122 us; the launch traced here: 121 us
  waiting for transfers between devices  44.4 us (36%)
  starting transfers between devices  35.5 us (29%)
  Pallas kernels  25.9 us (21%)
  local copies, waits for them, and re-layouts  5.63 us (5%)
  other arithmetic  5 us (4%)
  between operations  4.71 us (4%)
    ppermute x7, waiting for transfers between devices, send_to_chips(): lax.ppermute(pieces[s], 'band', [(b, b ^ 2 * s) for b in range(PARTS)])  22 us
    ppermute x7, starting transfers between devices, send_to_chips(): lax.ppermute(pieces[s], 'band', [(b, b ^ 2 * s) for b in range(PARTS)])  10.8 us
    pallas_call x1, Pallas kernels, z_transform(): pl.pallas_call(z_kernel, out_shape=jax.ShapeDtypeStruct((256, 512), BF),...  10.3 us
    all_to_all x1, waiting for transfers between devices, shards(): parts = lax.all_to_all(parts, 'grid', 0, 0, tiled=True)  9.16 us
    all_to_all x1, starting transfers between devices, shards(): parts = lax.all_to_all(parts, 'grid', 0, 0, tiled=True)  6.88 us
    ppermute x1, waiting for transfers between devices, shards(): column = lax.ppermute(narrow, ('band', 'grid'), far)  6.51 us
    ppermute x3, starting transfers between devices, shards(): block = block + lax.ppermute(narrow, 'band', step).astype(F32)  6.16 us
    all_to_all x1, starting transfers between devices, shards(): cond_wire = lax.all_to_all(cond_wire, 'band', 0, 0, tiled=True)  5.7 us
  transfers between devices with their start and end apart: 18, of which 10 were waited for; matrix products, arithmetic and copies ran while one was open for 7% of the time, Pallas kernels for 8%

profile of v7, /device:TPU:38, one launch (start us, length us, event | category | flops | bytes accessed | tf_op | source)
XLA Modules:
  0.0 121.1 jit_solution(7320368895637175612)
XLA Ops:
  0.7 3.5 %packcond.1 = bf16[16,504,128]{2,1,0:T(8,128)(2,1)} custom-call(s32[1]{0:T(128)S(6)} %copy.31.number_ref, bf16[2,3200,160]{2,1,0:T(8,128)(2,1)} %bitcast.39), custom_call_target="tpu_custom_call" | custom-call | bytes 6000000 | tf_op jit(solution)/shard_map/packcond/pallas_call | solution.py:81
  4.2 5.7 %all-to-all-start = ((bf16[16,504,128]{2,1,0:T(8,128)(2,1)}), bf16[16,504,128]{2,1,0:T(8,128)(2,1)}, u32[]{:S(2)}, u32[]{:S(2)}) async-start(bf16[16,504,128]{2,1,0:T(8,128)(2,1)} %packcond.1), calls=%async_computation | async-start | bytes 4128768 | tf_op jit(solution)/shard_map/all_to_all | solution.py:355
  9.9 2.5 %packgive.2 = bf16[4,2,504,128]{3,2,1,0:T(8,128)(2,1)S(1)} custom-call(s32[2]{0:T(128)S(1)} %pad_add_fusion.2.place_ref, bf16[2,2,8,2,200,160]{5,4,3,2,1,0:T(8,128)(2,1)} %bitcast.35), custom_call_target="tpu_custom_call" | custom-call | bytes 3000000 | tf_op jit(solution)/shard_map/packgive/pallas_call | solution.py:104
  12.7 2.5 %packgive.3 = bf16[4,2,504,128]{3,2,1,0:T(8,128)(2,1)S(1)} custom-call(s32[2]{0:T(128)S(1)} %pad_add_fusion.2.place_ref, bf16[2,2,8,2,200,160]{5,4,3,2,1,0:T(8,128)(2,1)} %bitcast.36), custom_call_target="tpu_custom_call" | custom-call | bytes 3000000 | tf_op jit(solution)/shard_map/packgive/pallas_call | solution.py:104
  19.4 4.0 %packchoice.3 = (bf16[2,504,128]{2,1,0:T(8,128)(2,1)S(1)}, bf16[2,504,128]{2,1,0:T(8,128)(2,1)}, bf16[2,504,128]{2,1,0:T(8,128)(2,1)S(1)}, bf16[2,504,128]{2,1,0...) custom-call(s32[3]{0:T(128)S(1)} %pad_add_fusion.1.place_ref, ...), custom_call_target="tpu_custom_call" | custom-call | bytes 8000000 | tf_op jit(solution)/shard_map/packchoice/pallas_call | solution.py:136
  24.3 1.2 collective-permute-start.10
  29.0 2.1 %collective-permute-start.11 = (bf16[2,504,128]{2,1,0:T(8,128)(2,1)}, bf16[2,504,128]{2,1,0:T(8,128)(2,1)S(1)}, u32[]{:S(2)}, u32[]{:S(2)}) collective-permute-start(bf16[2,504,128]{2,1,0:T(8,128)(2,1)} %get-tuple-element.62), channel_id=1, source_target_pairs={{0,64},{8,72},{16,80},{24,88},{32,96},{40,104},{48,112},{56,120},{... | collective-permute-start | bytes 774152 | tf_op jit(solution)/shard_map/ppermute | solution.py:155
  31.7 1.8 %collective-permute-start.13 = (bf16[2,504,128]{2,1,0:T(8,128)(2,1)S(1)}, bf16[2,504,128]{2,1,0:T(8,128)(2,1)S(1)}, u32[]{:S(2)}, u32[]{:S(2)}) collective-permute-start(bf16[2,504,128]{2,1,0:T(8,128)(2,1)S(1)} %get-tuple-element.64), channel_id=1, source_target_pairs={{0,48},{8,56},{16,32},{24,40},{32,16},{40,24},{48,0},{56,8},{64,11... | collective-permute-start | bytes 774152 | tf_op jit(solution)/shard_map/ppermute | solution.py:155
  33.4 6.7 %collective-permute-done.9.refs_1_ = bf16[2,504,128]{2,1,0:T(8,128)(2,1)S(1)} collective-permute-done((bf16[2,504,128]{2,1,0:T(8,128)(2,1)S(1)}, bf16[2,504,128]{2,1,0:T(8,128)(2,1)S(1)}, u32[]{:S(2)}, u32[]{:S(2)}) %collective-permute-start.9) | collective-permute-done | bytes 258080 | tf_op jit(solution)/shard_map/ppermute | solution.py:155
  40.1 1.2 collective-permute-start.14
  41.3 3.3 %collective-permute-start.15 = (bf16[2,504,128]{2,1,0:T(8,128)(2,1)S(1)}, bf16[2,504,128]{2,1,0:T(8,128)(2,1)S(1)}, u32[]{:S(2)}, u32[]{:S(2)}) collective-permute-start(bf16[2,504,128]{2,1,0:T(8,128)(2,1)S(1)} %get-tuple-element.66), channel_id=1, source_target_pairs={{0,80},{8,88},{16,64},{24,72},{32,112},{40,120},{48,96},{56,104},{... | collective-permute-start | bytes 774152 | tf_op jit(solution)/shard_map/ppermute | solution.py:155
  47.9 13.5 %collective-permute-done.13.refs_5_ = bf16[2,504,128]{2,1,0:T(8,128)(2,1)S(1)} collective-permute-done((bf16[2,504,128]{2,1,0:T(8,128)(2,1)S(1)}, bf16[2,504,128]{2,1,0:T(8,128)(2,1)S(1)}, u32[]{:S(2)}, u32[]{:S(2)}) %collective-permute-start.13) | collective-permute-done | bytes 258080 | tf_op jit(solution)/shard_map/ppermute | solution.py:155
  63.2 10.3 %ztransform.1.plane_ref = bf16[256,512]{1,0:T(8,128)(2,1)S(1)} custom-call(s32[3]{0:T(128)S(1)} %pad_add_fusion.3.where_ref, bf16[2,504,128]{2,1,0:T(8,128)(2,1)S(1)} %get-tuple-element.68.refs_0_, bf16[2,504,128]{2,1,0:T(8,128)(2,1)S(1)} %collective-permute-done.9.refs_1_, bf16[2,504,128]{2,1,0:T(8,128)(2,1)S(1)} %collective-permute-done.10.refs_2_, ...), custom_call_target="tpu_custom_call" | custom-call | tf_op jit(solution)/shard_map/ztransform/pallas_call | solution.py:248
  77.3 6.9 %all-to-all-start.1 = ((bf16[8,128,256]{2,1,0:T(8,128)(2,1)}), bf16[8,128,256]{2,1,0:T(8,128)(2,1)S(1)}, u32[]{:S(2)}, u32[]{:S(2)}) async-start(bf16[8,128,256]{2,1,0:T(8,128)(2,1)} %add_convert_fusion), calls=%async_computation.1 | async-start | bytes 1048576 | tf_op jit(solution)/shard_map/all_to_all | solution.py:411
  85.0 1.2 convert_reduce_fusion.1
  86.2 9.2 %all-to-all-done.1 = bf16[8,128,256]{2,1,0:T(8,128)(2,1)S(1)} async-done(((bf16[8,128,256]{2,1,0:T(8,128)(2,1)}), bf16[8,128,256]{2,1,0:T(8,128)(2,1)S(1)}, u32[]{:S(2)}, u32[]{:S(2)}) %all-to-all-start.1) | async-done | bytes 524320 | tf_op jit(solution)/shard_map/all_to_all | solution.py:411
  95.4 3.3 %collective-permute-start.17 = (bf16[128,256]{1,0:T(8,128)(2,1)S(1)}, bf16[128,256]{1,0:T(8,128)(2,1)S(1)}, u32[]{:S(2)}, u32[]{:S(2)}) collective-permute-start(bf16[128,256]{1,0:T(8,128)(2,1)S(1)} %convert_element_type.71), channel_id=1, source_target_pairs={{0,16},{8,24},{16,0},{24,8},{32,48},{40,56},{48,32},{56,40},{64,80... | collective-permute-start | bytes 196616 | tf_op jit(solution)/shard_map/ppermute | solution.py:413
  98.9 2.1 %collective-permute-done.17 = bf16[128,256]{1,0:T(8,128)(2,1)S(1)} collective-permute-done((bf16[128,256]{1,0:T(8,128)(2,1)S(1)}, bf16[128,256]{1,0:T(8,128)(2,1)S(1)}, u32[]{:S(2)}, u32[]{:S(2)}) %collective-permute-start.17) | collective-permute-done | bytes 65568 | tf_op jit(solution)/shard_map/ppermute | solution.py:413
  101.1 5.2 %collective-permute-start.19 = (bf16[128,256]{1,0:T(8,128)(2,1)S(1)}, bf16[128,256]{1,0:T(8,128)(2,1)S(1)}, u32[]{:S(2)}, u32[]{:S(2)}) collective-permute-start(bf16[128,256]{1,0:T(8,128)(2,1)S(1)} %fusion), channel_id=1, source_target_pairs={{0,64},{8,72},{16,80},{24,88},{32,96},{40,104},{48,112},{56,120},{... | collective-permute-start | bytes 196616 | tf_op jit(solution)/shard_map/ppermute | solution.py:417
  107.4 1.9 %collective-permute-done.19 = bf16[128,256]{1,0:T(8,128)(2,1)S(1)} collective-permute-done((bf16[128,256]{1,0:T(8,128)(2,1)S(1)}, bf16[128,256]{1,0:T(8,128)(2,1)S(1)}, u32[]{:S(2)}, u32[]{:S(2)}) %collective-permute-start.19) | collective-permute-done | bytes 65568 | tf_op jit(solution)/shard_map/ppermute | solution.py:417
  109.3 1.8 %collective-permute-done.18 = bf16[128,256]{1,0:T(8,128)(2,1)S(1)} collective-permute-done((bf16[128,256]{1,0:T(8,128)(2,1)S(1)}, bf16[128,256]{1,0:T(8,128)(2,1)S(1)}, u32[]{:S(2)}, u32[]{:S(2)}) %collective-permute-start.18) | collective-permute-done | bytes 65568 | tf_op jit(solution)/shard_map/ppermute | solution.py:417
  111.1 1.8 %collective-permute-start.21 = (bf16[128,256]{1,0:T(8,128)(2,1)S(1)}, bf16[128,256]{1,0:T(8,128)(2,1)S(1)}, u32[]{:S(2)}, u32[]{:S(2)}) collective-permute-start(bf16[128,256]{1,0:T(8,128)(2,1)S(1)} %add_convert_fusion.1.mine_ref), channel_id=1, source_target_pairs={{0,4},{1,20},{2,32},{3,48},{4,68},{5,84},{6,96},{7,112},{8,12},{9,... | collective-permute-start | bytes 196616 | tf_op jit(solution)/shard_map/ppermute | solution.py:427
  113.1 6.5 %collective-permute-done.21.column_ref = bf16[128,256]{1,0:T(8,128)(2,1)S(1)} collective-permute-done((bf16[128,256]{1,0:T(8,128)(2,1)S(1)}, bf16[128,256]{1,0:T(8,128)(2,1)S(1)}, u32[]{:S(2)}, u32[]{:S(2)}) %collective-permute-start.21) | collective-permute-done | bytes 65568 | tf_op jit(solution)/shard_map/ppermute | solution.py:427
  119.6 1.5 %chi.1 = f32[2,512,256]{2,1,0:T(8,128)} custom-call(s32[1]{0:T(128)} %bitcast.3.parity_ref.core_ref, bf16[128,256]{1,0:T(8,128)(2,1)S(1)} %add_convert_fusion.1.mine_ref, bf16[128,256]{1,0:T(8,128)(2,1)S(1)} %collective-permute-done.21.column_ref, bf16[128,256]{1,0:T(8,128)(2,1)S(1)} %collective-permute-done.22.other_ref, f32[128,1]{1,0:T(8,128)S(1)} %copy.28.weight_ref), custom_call_target="tpu_custom_call" | custom-call | tf_op jit(solution)/shard_map/chi/pallas_call | solution.py:332
  (62 shorter events, 17.8 us)
Async XLA Ops:
  0.0 84.3 %copy-start = (f32[32]{0:T(128)S(1)}, f32[32]{0:T(128)}, u32[]{:S(2)}) copy-start(f32[32]{0:T(128)} %param.13) | copy-start | bytes 388
  4.2 58.2 %all-to-all-start = ((bf16[16,504,128]{2,1,0:T(8,128)(2,1)}), bf16[16,504,128]{2,1,0:T(8,128)(2,1)}, u32[]{:S(2)}, u32[]{:S(2)}) async-start(bf16[16,504,128]{2,1,0:T(8,128)(2,1)} %packcond.1), calls=%async_computation | async-start | bytes 4128768 | tf_op jit(solution)/shard_map/all_to_all | solution.py:355
  12.4 3.2 %copy-start.3 = (s32[3,4096]{1,0:T(4,128)S(1)}, s32[3,4096]{1,0:T(4,128)}, u32[]{:S(2)}) copy-start(s32[3,4096]{1,0:T(4,128)} %param.17) | copy-start | bytes 147460
  12.4 4.2 %copy-start.4 = (s32[2]{0:T(128)S(1)}, s32[2]{0:T(128)}, u32[]{:S(2)}) copy-start(s32[2]{0:T(128)} %param.16) | copy-start | bytes 28
  12.4 7.0 %collective-permute-start.7 = (bf16[4,2,504,128]{3,2,1,0:T(8,128)(2,1)S(1)}, bf16[4,2,504,128]{3,2,1,0:T(8,128)(2,1)}, u32[]{:S(2)}, u32[]{:S(2)}) collective-permute-start(bf16[4,2,504,128]{3,2,1,0:T(8,128)(2,1)S(1)} %packgive.2), channel_id=1, source_target_pairs={{0,8},{8,0},{16,24},{24,16},{32,40},{40,32},{48,56},{56,48},{64,72... | collective-permute-start | bytes 3096584 | tf_op jit(solution)/shard_map/ppermute | solution.py:362
  15.1 4.3 %collective-permute-start.8 = (bf16[4,2,504,128]{3,2,1,0:T(8,128)(2,1)S(1)}, bf16[4,2,504,128]{3,2,1,0:T(8,128)(2,1)}, u32[]{:S(2)}, u32[]{:S(2)}) collective-permute-start(bf16[4,2,504,128]{3,2,1,0:T(8,128)(2,1)S(1)} %packgive.3), channel_id=1, source_target_pairs={{0,8},{8,0},{16,24},{24,16},{32,40},{40,32},{48,56},{56,48},{64,72... | collective-permute-start | bytes 3096584 | tf_op jit(solution)/shard_map/ppermute | solution.py:362
  23.4 16.7 %collective-permute-start.9 = (bf16[2,504,128]{2,1,0:T(8,128)(2,1)S(1)}, bf16[2,504,128]{2,1,0:T(8,128)(2,1)S(1)}, u32[]{:S(2)}, u32[]{:S(2)}) collective-permute-start(bf16[2,504,128]{2,1,0:T(8,128)(2,1)S(1)} %get-tuple-element.60), channel_id=1, source_target_pairs={{0,32},{8,40},{16,48},{24,56},{32,0},{40,8},{48,16},{56,24},{64,96... | collective-permute-start | bytes 774152 | tf_op jit(solution)/shard_map/ppermute | solution.py:155
  24.3 17.0 %collective-permute-start.10 = (bf16[2,504,128]{2,1,0:T(8,128)(2,1)S(1)}, bf16[2,504,128]{2,1,0:T(8,128)(2,1)S(1)}, u32[]{:S(2)}, u32[]{:S(2)}) collective-permute-start(bf16[2,504,128]{2,1,0:T(8,128)(2,1)S(1)} %get-tuple-element.61), channel_id=1, source_target_pairs={{0,96},{8,104},{16,112},{24,120},{32,64},{40,72},{48,80},{56,88},{... | collective-permute-start | bytes 774152 | tf_op jit(solution)/shard_map/ppermute | solution.py:155
  29.0 18.8 %collective-permute-start.11 = (bf16[2,504,128]{2,1,0:T(8,128)(2,1)}, bf16[2,504,128]{2,1,0:T(8,128)(2,1)S(1)}, u32[]{:S(2)}, u32[]{:S(2)}) collective-permute-start(bf16[2,504,128]{2,1,0:T(8,128)(2,1)} %get-tuple-element.62), channel_id=1, source_target_pairs={{0,64},{8,72},{16,80},{24,88},{32,96},{40,104},{48,112},{56,120},{... | collective-permute-start | bytes 774152 | tf_op jit(solution)/shard_map/ppermute | solution.py:155
  31.1 16.7 %collective-permute-start.12 = (bf16[2,504,128]{2,1,0:T(8,128)(2,1)}, bf16[2,504,128]{2,1,0:T(8,128)(2,1)S(1)}, u32[]{:S(2)}, u32[]{:S(2)}) collective-permute-start(bf16[2,504,128]{2,1,0:T(8,128)(2,1)} %get-tuple-element.63), channel_id=1, source_target_pairs={{0,16},{8,24},{16,0},{24,8},{32,48},{40,56},{48,32},{56,40},{64,80... | collective-permute-start | bytes 774152 | tf_op jit(solution)/shard_map/ppermute | solution.py:155
  31.7 29.7 %collective-permute-start.13 = (bf16[2,504,128]{2,1,0:T(8,128)(2,1)S(1)}, bf16[2,504,128]{2,1,0:T(8,128)(2,1)S(1)}, u32[]{:S(2)}, u32[]{:S(2)}) collective-permute-start(bf16[2,504,128]{2,1,0:T(8,128)(2,1)S(1)} %get-tuple-element.64), channel_id=1, source_target_pairs={{0,48},{8,56},{16,32},{24,40},{32,16},{40,24},{48,0},{56,8},{64,11... | collective-permute-start | bytes 774152 | tf_op jit(solution)/shard_map/ppermute | solution.py:155
  40.1 22.3 %collective-permute-start.14 = (bf16[2,504,128]{2,1,0:T(8,128)(2,1)S(1)}, bf16[2,504,128]{2,1,0:T(8,128)(2,1)S(1)}, u32[]{:S(2)}, u32[]{:S(2)}) collective-permute-start(bf16[2,504,128]{2,1,0:T(8,128)(2,1)S(1)} %get-tuple-element.65), channel_id=1, source_target_pairs={{0,112},{8,120},{16,96},{24,104},{32,80},{40,88},{48,64},{56,72},{... | collective-permute-start | bytes 774152 | tf_op jit(solution)/shard_map/ppermute | solution.py:155
  41.3 21.1 %collective-permute-start.15 = (bf16[2,504,128]{2,1,0:T(8,128)(2,1)S(1)}, bf16[2,504,128]{2,1,0:T(8,128)(2,1)S(1)}, u32[]{:S(2)}, u32[]{:S(2)}) collective-permute-start(bf16[2,504,128]{2,1,0:T(8,128)(2,1)S(1)} %get-tuple-element.66), channel_id=1, source_target_pairs={{0,80},{8,88},{16,64},{24,72},{32,112},{40,120},{48,96},{56,104},{... | collective-permute-start | bytes 774152 | tf_op jit(solution)/shard_map/ppermute | solution.py:155
  74.4 2.0 %collective-permute-start.16 = (bf16[8,128,256]{2,1,0:T(8,128)(2,1)S(1)}, bf16[8,128,256]{2,1,0:T(8,128)(2,1)S(1)}, u32[]{:S(2)}, u32[]{:S(2)}) collective-permute-start(bf16[8,128,256]{2,1,0:T(8,128)(2,1)S(1)} %gelements.3), channel_id=1, source_target_pairs={{0,8},{8,0},{16,24},{24,16},{32,40},{40,32},{48,56},{56,48},{64,72... | collective-permute-start | bytes 1572872 | tf_op jit(solution)/shard_map/ppermute | solution.py:408
  75.3 23.4 %copy-start.5 = (f32[16]{0:T(128)S(1)}, f32[16]{0:T(128)}, u32[]{:S(2)}) copy-start(f32[16]{0:T(128)} %param.14) | copy-start | bytes 196
  77.3 18.1 %all-to-all-start.1 = ((bf16[8,128,256]{2,1,0:T(8,128)(2,1)}), bf16[8,128,256]{2,1,0:T(8,128)(2,1)S(1)}, u32[]{:S(2)}, u32[]{:S(2)}) async-start(bf16[8,128,256]{2,1,0:T(8,128)(2,1)} %add_convert_fusion), calls=%async_computation.1 | async-start | bytes 1048576 | tf_op jit(solution)/shard_map/all_to_all | solution.py:411
  95.4 5.5 %collective-permute-start.17 = (bf16[128,256]{1,0:T(8,128)(2,1)S(1)}, bf16[128,256]{1,0:T(8,128)(2,1)S(1)}, u32[]{:S(2)}, u32[]{:S(2)}) collective-permute-start(bf16[128,256]{1,0:T(8,128)(2,1)S(1)} %convert_element_type.71), channel_id=1, source_target_pairs={{0,16},{8,24},{16,0},{24,8},{32,48},{40,56},{48,32},{56,40},{64,80... | collective-permute-start | bytes 196616 | tf_op jit(solution)/shard_map/ppermute | solution.py:413
  101.0 6.3 %collective-permute-start.20 = (bf16[128,256]{1,0:T(8,128)(2,1)S(1)}, bf16[128,256]{1,0:T(8,128)(2,1)S(1)}, u32[]{:S(2)}, u32[]{:S(2)}) collective-permute-start(bf16[128,256]{1,0:T(8,128)(2,1)S(1)} %fusion), channel_id=1, source_target_pairs={{0,96},{8,104},{16,112},{24,120},{32,0},{40,8},{48,16},{56,24},{64... | collective-permute-start | bytes 196616 | tf_op jit(solution)/shard_map/ppermute | solution.py:417
  101.1 8.2 %collective-permute-start.19 = (bf16[128,256]{1,0:T(8,128)(2,1)S(1)}, bf16[128,256]{1,0:T(8,128)(2,1)S(1)}, u32[]{:S(2)}, u32[]{:S(2)}) collective-permute-start(bf16[128,256]{1,0:T(8,128)(2,1)S(1)} %fusion), channel_id=1, source_target_pairs={{0,64},{8,72},{16,80},{24,88},{32,96},{40,104},{48,112},{56,120},{... | collective-permute-start | bytes 196616 | tf_op jit(solution)/shard_map/ppermute | solution.py:417
  106.3 4.7 %collective-permute-start.18 = (bf16[128,256]{1,0:T(8,128)(2,1)S(1)}, bf16[128,256]{1,0:T(8,128)(2,1)S(1)}, u32[]{:S(2)}, u32[]{:S(2)}) collective-permute-start(bf16[128,256]{1,0:T(8,128)(2,1)S(1)} %fusion), channel_id=1, source_target_pairs={{0,32},{8,40},{16,48},{24,56},{32,64},{40,72},{48,80},{56,88},{64,... | collective-permute-start | bytes 196616 | tf_op jit(solution)/shard_map/ppermute | solution.py:417
  111.1 8.6 %collective-permute-start.21 = (bf16[128,256]{1,0:T(8,128)(2,1)S(1)}, bf16[128,256]{1,0:T(8,128)(2,1)S(1)}, u32[]{:S(2)}, u32[]{:S(2)}) collective-permute-start(bf16[128,256]{1,0:T(8,128)(2,1)S(1)} %add_convert_fusion.1.mine_ref), channel_id=1, source_target_pairs={{0,4},{1,20},{2,32},{3,48},{4,68},{5,84},{6,96},{7,112},{8,12},{9,... | collective-permute-start | bytes 196616 | tf_op jit(solution)/shard_map/ppermute | solution.py:427
  112.9 6.7 %collective-permute-start.22 = (bf16[128,256]{1,0:T(8,128)(2,1)S(1)}, bf16[128,256]{1,0:T(8,128)(2,1)S(1)}, u32[]{:S(2)}, u32[]{:S(2)}) collective-permute-start(bf16[128,256]{1,0:T(8,128)(2,1)S(1)} %add_convert_fusion.1.mine_ref), channel_id=1, source_target_pairs={{0,8},{8,0},{16,24},{24,16},{32,40},{40,32},{48,56},{56,48},{64,72... | collective-permute-start | bytes 196616 | tf_op jit(solution)/shard_map/ppermute | solution.py:428

commit v8 on v7

--- a/solution.py
+++ b/solution.py
@@ -20,7 +20,7 @@
 PACK = 8
 CHIPS = 8
 ORDER = (0, 2, 6, 4, 1, 3, 7, 5)
-CONDS = 4
+CONDS = 8
 SLOTS = 12
 KROWS = 24
 GCHUNK = 256

time: 122 us -> 121 us (level)
  transfers between devices with their start and end apart: 18 -> 18, of which waited for: 10 -> 10; matrix products, arithmetic and copies ran while one was open for 7% -> 7% of each run, Pallas kernels for 8% -> 9%
where the time goes in v8:
time: 121 us
  waiting for transfers between devices  44.2 us (37%)
  starting transfers between devices  34.6 us (29%)
  Pallas kernels  26.5 us (22%)
  local copies, waits for them, and re-layouts  5.63 us (5%)
  other arithmetic  5 us (4%)
  between operations  4.71 us (4%)
    ppermute x7, waiting for transfers between devices, send_to_chips(): lax.ppermute(pieces[s], 'band', [(b, b ^ 2 * s) for b in range(PARTS)])  21.8 us
    ppermute x7, starting transfers between devices, send_to_chips(): lax.ppermute(pieces[s], 'band', [(b, b ^ 2 * s) for b in range(PARTS)])  9.99 us
    pallas_call x1, Pallas kernels, z_transform(): pl.pallas_call(z_kernel, out_shape=jax.ShapeDtypeStruct((256, 512), BF),...  9.85 us
    all_to_all x1, waiting for transfers between devices, shards(): parts = lax.all_to_all(parts, 'grid', 0, 0, tiled=True)  9.16 us
    all_to_all x1, starting transfers between devices, shards(): parts = lax.all_to_all(parts, 'grid', 0, 0, tiled=True)  6.89 us
    ppermute x1, waiting for transfers between devices, shards(): column = lax.ppermute(narrow, ('band', 'grid'), far)  6.51 us
    ppermute x3, starting transfers between devices, shards(): block = block + lax.ppermute(narrow, 'band', step).astype(F32)  6.2 us
    all_to_all x1, starting transfers between devices, shards(): cond_wire = lax.all_to_all(cond_wire, 'band', 0, 0, tiled=True)  5.7 us
  transfers between devices with their start and end apart: 18, of which 10 were waited for; matrix products, arithmetic and copies ran while one was open for 7% of the time, Pallas kernels for 9%

profile of v8, /device:TPU:38, one launch (start us, length us, event | category | flops | bytes accessed | tf_op | source)
XLA Modules:
  0.0 120.7 jit_solution(3931672494593061087)
XLA Ops:
  0.7 3.5 %packcond.1 = bf16[16,504,128]{2,1,0:T(8,128)(2,1)} custom-call(s32[1]{0:T(128)S(6)} %copy.31.number_ref, bf16[2,3200,160]{2,1,0:T(8,128)(2,1)} %bitcast.39), custom_call_target="tpu_custom_call" | custom-call | bytes 6000000 | tf_op jit(solution)/shard_map/packcond/pallas_call | solution.py:81
  4.2 5.7 %all-to-all-start = ((bf16[16,504,128]{2,1,0:T(8,128)(2,1)}), bf16[16,504,128]{2,1,0:T(8,128)(2,1)}, u32[]{:S(2)}, u32[]{:S(2)}) async-start(bf16[16,504,128]{2,1,0:T(8,128)(2,1)} %packcond.1), calls=%async_computation | async-start | bytes 4128768 | tf_op jit(solution)/shard_map/all_to_all | solution.py:355
  9.9 2.5 %packgive.2 = bf16[4,2,504,128]{3,2,1,0:T(8,128)(2,1)S(1)} custom-call(s32[2]{0:T(128)S(1)} %pad_add_fusion.2.place_ref, bf16[2,2,8,2,200,160]{5,4,3,2,1,0:T(8,128)(2,1)} %bitcast.35), custom_call_target="tpu_custom_call" | custom-call | bytes 3000000 | tf_op jit(solution)/shard_map/packgive/pallas_call | solution.py:104
  12.7 2.5 %packgive.3 = bf16[4,2,504,128]{3,2,1,0:T(8,128)(2,1)S(1)} custom-call(s32[2]{0:T(128)S(1)} %pad_add_fusion.2.place_ref, bf16[2,2,8,2,200,160]{5,4,3,2,1,0:T(8,128)(2,1)} %bitcast.36), custom_call_target="tpu_custom_call" | custom-call | bytes 3000000 | tf_op jit(solution)/shard_map/packgive/pallas_call | solution.py:104
  19.4 5.0 %packchoice.3 = (bf16[2,504,128]{2,1,0:T(8,128)(2,1)S(1)}, bf16[2,504,128]{2,1,0:T(8,128)(2,1)}, bf16[2,504,128]{2,1,0:T(8,128)(2,1)S(1)}, bf16[2,504,128]{2,1,0...) custom-call(s32[3]{0:T(128)S(1)} %pad_add_fusion.1.place_ref, ...), custom_call_target="tpu_custom_call" | custom-call | bytes 8000000 | tf_op jit(solution)/shard_map/packchoice/pallas_call | solution.py:136
  29.0 3.1 %collective-permute-start.11 = (bf16[2,504,128]{2,1,0:T(8,128)(2,1)}, bf16[2,504,128]{2,1,0:T(8,128)(2,1)S(1)}, u32[]{:S(2)}, u32[]{:S(2)}) collective-permute-start(bf16[2,504,128]{2,1,0:T(8,128)(2,1)} %get-tuple-element.62), channel_id=1, source_target_pairs={{0,64},{8,72},{16,80},{24,88},{32,96},{40,104},{48,112},{56,120},{... | collective-permute-start | bytes 774152 | tf_op jit(solution)/shard_map/ppermute | solution.py:155
  32.1 1.5 %collective-permute-start.13 = (bf16[2,504,128]{2,1,0:T(8,128)(2,1)S(1)}, bf16[2,504,128]{2,1,0:T(8,128)(2,1)S(1)}, u32[]{:S(2)}, u32[]{:S(2)}) collective-permute-start(bf16[2,504,128]{2,1,0:T(8,128)(2,1)S(1)} %get-tuple-element.64), channel_id=1, source_target_pairs={{0,48},{8,56},{16,32},{24,40},{32,16},{40,24},{48,0},{56,8},{64,11... | collective-permute-start | bytes 774152 | tf_op jit(solution)/shard_map/ppermute | solution.py:155
  33.6 6.5 %collective-permute-done.9.refs_1_ = bf16[2,504,128]{2,1,0:T(8,128)(2,1)S(1)} collective-permute-done((bf16[2,504,128]{2,1,0:T(8,128)(2,1)S(1)}, bf16[2,504,128]{2,1,0:T(8,128)(2,1)S(1)}, u32[]{:S(2)}, u32[]{:S(2)}) %collective-permute-start.9) | collective-permute-done | bytes 258080 | tf_op jit(solution)/shard_map/ppermute | solution.py:155
  40.1 1.2 collective-permute-start.14
  41.3 3.3 %collective-permute-start.15 = (bf16[2,504,128]{2,1,0:T(8,128)(2,1)S(1)}, bf16[2,504,128]{2,1,0:T(8,128)(2,1)S(1)}, u32[]{:S(2)}, u32[]{:S(2)}) collective-permute-start(bf16[2,504,128]{2,1,0:T(8,128)(2,1)S(1)} %get-tuple-element.66), channel_id=1, source_target_pairs={{0,80},{8,88},{16,64},{24,72},{32,112},{40,120},{48,96},{56,104},{... | collective-permute-start | bytes 774152 | tf_op jit(solution)/shard_map/ppermute | solution.py:155
  44.7 1.2 copy.23
  47.9 13.5 %collective-permute-done.13.refs_5_ = bf16[2,504,128]{2,1,0:T(8,128)(2,1)S(1)} collective-permute-done((bf16[2,504,128]{2,1,0:T(8,128)(2,1)S(1)}, bf16[2,504,128]{2,1,0:T(8,128)(2,1)S(1)}, u32[]{:S(2)}, u32[]{:S(2)}) %collective-permute-start.13) | collective-permute-done | bytes 258080 | tf_op jit(solution)/shard_map/ppermute | solution.py:155
  63.2 9.9 %ztransform.1.plane_ref = bf16[256,512]{1,0:T(8,128)(2,1)S(1)} custom-call(s32[3]{0:T(128)S(1)} %pad_add_fusion.3.where_ref, bf16[2,504,128]{2,1,0:T(8,128)(2,1)S(1)} %get-tuple-element.68.refs_0_, bf16[2,504,128]{2,1,0:T(8,128)(2,1)S(1)} %collective-permute-done.9.refs_1_, bf16[2,504,128]{2,1,0:T(8,128)(2,1)S(1)} %collective-permute-done.10.refs_2_, ...), custom_call_target="tpu_custom_call" | custom-call | tf_op jit(solution)/shard_map/ztransform/pallas_call | solution.py:248
  76.9 6.9 %all-to-all-start.1 = ((bf16[8,128,256]{2,1,0:T(8,128)(2,1)}), bf16[8,128,256]{2,1,0:T(8,128)(2,1)S(1)}, u32[]{:S(2)}, u32[]{:S(2)}) async-start(bf16[8,128,256]{2,1,0:T(8,128)(2,1)} %add_convert_fusion), calls=%async_computation.1 | async-start | bytes 1048576 | tf_op jit(solution)/shard_map/all_to_all | solution.py:411
  84.6 1.2 convert_reduce_fusion.1
  85.8 9.2 %all-to-all-done.1 = bf16[8,128,256]{2,1,0:T(8,128)(2,1)S(1)} async-done(((bf16[8,128,256]{2,1,0:T(8,128)(2,1)}), bf16[8,128,256]{2,1,0:T(8,128)(2,1)S(1)}, u32[]{:S(2)}, u32[]{:S(2)}) %all-to-all-start.1) | async-done | bytes 524320 | tf_op jit(solution)/shard_map/all_to_all | solution.py:411
  95.0 3.3 %collective-permute-start.17 = (bf16[128,256]{1,0:T(8,128)(2,1)S(1)}, bf16[128,256]{1,0:T(8,128)(2,1)S(1)}, u32[]{:S(2)}, u32[]{:S(2)}) collective-permute-start(bf16[128,256]{1,0:T(8,128)(2,1)S(1)} %convert_element_type.71), channel_id=1, source_target_pairs={{0,16},{8,24},{16,0},{24,8},{32,48},{40,56},{48,32},{56,40},{64,80... | collective-permute-start | bytes 196616 | tf_op jit(solution)/shard_map/ppermute | solution.py:413
  98.5 2.1 %collective-permute-done.17 = bf16[128,256]{1,0:T(8,128)(2,1)S(1)} collective-permute-done((bf16[128,256]{1,0:T(8,128)(2,1)S(1)}, bf16[128,256]{1,0:T(8,128)(2,1)S(1)}, u32[]{:S(2)}, u32[]{:S(2)}) %collective-permute-start.17) | collective-permute-done | bytes 65568 | tf_op jit(solution)/shard_map/ppermute | solution.py:413
  100.6 5.3 %collective-permute-start.19 = (bf16[128,256]{1,0:T(8,128)(2,1)S(1)}, bf16[128,256]{1,0:T(8,128)(2,1)S(1)}, u32[]{:S(2)}, u32[]{:S(2)}) collective-permute-start(bf16[128,256]{1,0:T(8,128)(2,1)S(1)} %fusion), channel_id=1, source_target_pairs={{0,64},{8,72},{16,80},{24,88},{32,96},{40,104},{48,112},{56,120},{... | collective-permute-start | bytes 196616 | tf_op jit(solution)/shard_map/ppermute | solution.py:417
  106.9 1.9 %collective-permute-done.19 = bf16[128,256]{1,0:T(8,128)(2,1)S(1)} collective-permute-done((bf16[128,256]{1,0:T(8,128)(2,1)S(1)}, bf16[128,256]{1,0:T(8,128)(2,1)S(1)}, u32[]{:S(2)}, u32[]{:S(2)}) %collective-permute-start.19) | collective-permute-done | bytes 65568 | tf_op jit(solution)/shard_map/ppermute | solution.py:417
  108.8 1.8 %collective-permute-done.18 = bf16[128,256]{1,0:T(8,128)(2,1)S(1)} collective-permute-done((bf16[128,256]{1,0:T(8,128)(2,1)S(1)}, bf16[128,256]{1,0:T(8,128)(2,1)S(1)}, u32[]{:S(2)}, u32[]{:S(2)}) %collective-permute-start.18) | collective-permute-done | bytes 65568 | tf_op jit(solution)/shard_map/ppermute | solution.py:417
  110.7 1.8 %collective-permute-start.21 = (bf16[128,256]{1,0:T(8,128)(2,1)S(1)}, bf16[128,256]{1,0:T(8,128)(2,1)S(1)}, u32[]{:S(2)}, u32[]{:S(2)}) collective-permute-start(bf16[128,256]{1,0:T(8,128)(2,1)S(1)} %add_convert_fusion.1.mine_ref), channel_id=1, source_target_pairs={{0,4},{1,20},{2,32},{3,48},{4,68},{5,84},{6,96},{7,112},{8,12},{9,... | collective-permute-start | bytes 196616 | tf_op jit(solution)/shard_map/ppermute | solution.py:427
  112.7 6.5 %collective-permute-done.21.column_ref = bf16[128,256]{1,0:T(8,128)(2,1)S(1)} collective-permute-done((bf16[128,256]{1,0:T(8,128)(2,1)S(1)}, bf16[128,256]{1,0:T(8,128)(2,1)S(1)}, u32[]{:S(2)}, u32[]{:S(2)}) %collective-permute-start.21) | collective-permute-done | bytes 65568 | tf_op jit(solution)/shard_map/ppermute | solution.py:427
  119.2 1.5 %chi.1 = f32[2,512,256]{2,1,0:T(8,128)} custom-call(s32[1]{0:T(128)} %bitcast.3.parity_ref.core_ref, bf16[128,256]{1,0:T(8,128)(2,1)S(1)} %add_convert_fusion.1.mine_ref, bf16[128,256]{1,0:T(8,128)(2,1)S(1)} %collective-permute-done.21.column_ref, bf16[128,256]{1,0:T(8,128)(2,1)S(1)} %collective-permute-done.22.other_ref, f32[128,1]{1,0:T(8,128)S(1)} %copy.28.weight_ref), custom_call_target="tpu_custom_call" | custom-call | tf_op jit(solution)/shard_map/chi/pallas_call | solution.py:332
  (62 shorter events, 16.2 us)
Async XLA Ops:
  0.0 83.9 %copy-start = (f32[32]{0:T(128)S(1)}, f32[32]{0:T(128)}, u32[]{:S(2)}) copy-start(f32[32]{0:T(128)} %param.13) | copy-start | bytes 388
  4.2 58.2 %all-to-all-start = ((bf16[16,504,128]{2,1,0:T(8,128)(2,1)}), bf16[16,504,128]{2,1,0:T(8,128)(2,1)}, u32[]{:S(2)}, u32[]{:S(2)}) async-start(bf16[16,504,128]{2,1,0:T(8,128)(2,1)} %packcond.1), calls=%async_computation | async-start | bytes 4128768 | tf_op jit(solution)/shard_map/all_to_all | solution.py:355
  12.4 3.2 %copy-start.3 = (s32[3,4096]{1,0:T(4,128)S(1)}, s32[3,4096]{1,0:T(4,128)}, u32[]{:S(2)}) copy-start(s32[3,4096]{1,0:T(4,128)} %param.17) | copy-start | bytes 147460
  12.4 4.2 %copy-start.4 = (s32[2]{0:T(128)S(1)}, s32[2]{0:T(128)}, u32[]{:S(2)}) copy-start(s32[2]{0:T(128)} %param.16) | copy-start | bytes 28
  12.4 7.0 %collective-permute-start.7 = (bf16[4,2,504,128]{3,2,1,0:T(8,128)(2,1)S(1)}, bf16[4,2,504,128]{3,2,1,0:T(8,128)(2,1)}, u32[]{:S(2)}, u32[]{:S(2)}) collective-permute-start(bf16[4,2,504,128]{3,2,1,0:T(8,128)(2,1)S(1)} %packgive.2), channel_id=1, source_target_pairs={{0,8},{8,0},{16,24},{24,16},{32,40},{40,32},{48,56},{56,48},{64,72... | collective-permute-start | bytes 3096584 | tf_op jit(solution)/shard_map/ppermute | solution.py:362
  15.1 4.3 %collective-permute-start.8 = (bf16[4,2,504,128]{3,2,1,0:T(8,128)(2,1)S(1)}, bf16[4,2,504,128]{3,2,1,0:T(8,128)(2,1)}, u32[]{:S(2)}, u32[]{:S(2)}) collective-permute-start(bf16[4,2,504,128]{3,2,1,0:T(8,128)(2,1)S(1)} %packgive.3), channel_id=1, source_target_pairs={{0,8},{8,0},{16,24},{24,16},{32,40},{40,32},{48,56},{56,48},{64,72... | collective-permute-start | bytes 3096584 | tf_op jit(solution)/shard_map/ppermute | solution.py:362
  24.4 15.7 %collective-permute-start.9 = (bf16[2,504,128]{2,1,0:T(8,128)(2,1)S(1)}, bf16[2,504,128]{2,1,0:T(8,128)(2,1)S(1)}, u32[]{:S(2)}, u32[]{:S(2)}) collective-permute-start(bf16[2,504,128]{2,1,0:T(8,128)(2,1)S(1)} %get-tuple-element.60), channel_id=1, source_target_pairs={{0,32},{8,40},{16,48},{24,56},{32,0},{40,8},{48,16},{56,24},{64,96... | collective-permute-start | bytes 774152 | tf_op jit(solution)/shard_map/ppermute | solution.py:155
  24.4 16.9 %collective-permute-start.10 = (bf16[2,504,128]{2,1,0:T(8,128)(2,1)S(1)}, bf16[2,504,128]{2,1,0:T(8,128)(2,1)S(1)}, u32[]{:S(2)}, u32[]{:S(2)}) collective-permute-start(bf16[2,504,128]{2,1,0:T(8,128)(2,1)S(1)} %get-tuple-element.61), channel_id=1, source_target_pairs={{0,96},{8,104},{16,112},{24,120},{32,64},{40,72},{48,80},{56,88},{... | collective-permute-start | bytes 774152 | tf_op jit(solution)/shard_map/ppermute | solution.py:155
  29.0 18.8 %collective-permute-start.11 = (bf16[2,504,128]{2,1,0:T(8,128)(2,1)}, bf16[2,504,128]{2,1,0:T(8,128)(2,1)S(1)}, u32[]{:S(2)}, u32[]{:S(2)}) collective-permute-start(bf16[2,504,128]{2,1,0:T(8,128)(2,1)} %get-tuple-element.62), channel_id=1, source_target_pairs={{0,64},{8,72},{16,80},{24,88},{32,96},{40,104},{48,112},{56,120},{... | collective-permute-start | bytes 774152 | tf_op jit(solution)/shard_map/ppermute | solution.py:155
  32.1 15.7 %collective-permute-start.12 = (bf16[2,504,128]{2,1,0:T(8,128)(2,1)}, bf16[2,504,128]{2,1,0:T(8,128)(2,1)S(1)}, u32[]{:S(2)}, u32[]{:S(2)}) collective-permute-start(bf16[2,504,128]{2,1,0:T(8,128)(2,1)} %get-tuple-element.63), channel_id=1, source_target_pairs={{0,16},{8,24},{16,0},{24,8},{32,48},{40,56},{48,32},{56,40},{64,80... | collective-permute-start | bytes 774152 | tf_op jit(solution)/shard_map/ppermute | solution.py:155
  32.1 29.2 %collective-permute-start.13 = (bf16[2,504,128]{2,1,0:T(8,128)(2,1)S(1)}, bf16[2,504,128]{2,1,0:T(8,128)(2,1)S(1)}, u32[]{:S(2)}, u32[]{:S(2)}) collective-permute-start(bf16[2,504,128]{2,1,0:T(8,128)(2,1)S(1)} %get-tuple-element.64), channel_id=1, source_target_pairs={{0,48},{8,56},{16,32},{24,40},{32,16},{40,24},{48,0},{56,8},{64,11... | collective-permute-start | bytes 774152 | tf_op jit(solution)/shard_map/ppermute | solution.py:155
  40.1 22.3 %collective-permute-start.14 = (bf16[2,504,128]{2,1,0:T(8,128)(2,1)S(1)}, bf16[2,504,128]{2,1,0:T(8,128)(2,1)S(1)}, u32[]{:S(2)}, u32[]{:S(2)}) collective-permute-start(bf16[2,504,128]{2,1,0:T(8,128)(2,1)S(1)} %get-tuple-element.65), channel_id=1, source_target_pairs={{0,112},{8,120},{16,96},{24,104},{32,80},{40,88},{48,64},{56,72},{... | collective-permute-start | bytes 774152 | tf_op jit(solution)/shard_map/ppermute | solution.py:155
  41.3 21.1 %collective-permute-start.15 = (bf16[2,504,128]{2,1,0:T(8,128)(2,1)S(1)}, bf16[2,504,128]{2,1,0:T(8,128)(2,1)S(1)}, u32[]{:S(2)}, u32[]{:S(2)}) collective-permute-start(bf16[2,504,128]{2,1,0:T(8,128)(2,1)S(1)} %get-tuple-element.66), channel_id=1, source_target_pairs={{0,80},{8,88},{16,64},{24,72},{32,112},{40,120},{48,96},{56,104},{... | collective-permute-start | bytes 774152 | tf_op jit(solution)/shard_map/ppermute | solution.py:155
  73.9 2.0 %collective-permute-start.16 = (bf16[8,128,256]{2,1,0:T(8,128)(2,1)S(1)}, bf16[8,128,256]{2,1,0:T(8,128)(2,1)S(1)}, u32[]{:S(2)}, u32[]{:S(2)}) collective-permute-start(bf16[8,128,256]{2,1,0:T(8,128)(2,1)S(1)} %gelements.3), channel_id=1, source_target_pairs={{0,8},{8,0},{16,24},{24,16},{32,40},{40,32},{48,56},{56,48},{64,72... | collective-permute-start | bytes 1572872 | tf_op jit(solution)/shard_map/ppermute | solution.py:408
  74.9 23.4 %copy-start.5 = (f32[16]{0:T(128)S(1)}, f32[16]{0:T(128)}, u32[]{:S(2)}) copy-start(f32[16]{0:T(128)} %param.14) | copy-start | bytes 196
  76.9 18.1 %all-to-all-start.1 = ((bf16[8,128,256]{2,1,0:T(8,128)(2,1)}), bf16[8,128,256]{2,1,0:T(8,128)(2,1)S(1)}, u32[]{:S(2)}, u32[]{:S(2)}) async-start(bf16[8,128,256]{2,1,0:T(8,128)(2,1)} %add_convert_fusion), calls=%async_computation.1 | async-start | bytes 1048576 | tf_op jit(solution)/shard_map/all_to_all | solution.py:411
  95.0 5.5 %collective-permute-start.17 = (bf16[128,256]{1,0:T(8,128)(2,1)S(1)}, bf16[128,256]{1,0:T(8,128)(2,1)S(1)}, u32[]{:S(2)}, u32[]{:S(2)}) collective-permute-start(bf16[128,256]{1,0:T(8,128)(2,1)S(1)} %convert_element_type.71), channel_id=1, source_target_pairs={{0,16},{8,24},{16,0},{24,8},{32,48},{40,56},{48,32},{56,40},{64,80... | collective-permute-start | bytes 196616 | tf_op jit(solution)/shard_map/ppermute | solution.py:413
  100.6 6.4 %collective-permute-start.20 = (bf16[128,256]{1,0:T(8,128)(2,1)S(1)}, bf16[128,256]{1,0:T(8,128)(2,1)S(1)}, u32[]{:S(2)}, u32[]{:S(2)}) collective-permute-start(bf16[128,256]{1,0:T(8,128)(2,1)S(1)} %fusion), channel_id=1, source_target_pairs={{0,96},{8,104},{16,112},{24,120},{32,0},{40,8},{48,16},{56,24},{64... | collective-permute-start | bytes 196616 | tf_op jit(solution)/shard_map/ppermute | solution.py:417
  100.6 8.2 %collective-permute-start.19 = (bf16[128,256]{1,0:T(8,128)(2,1)S(1)}, bf16[128,256]{1,0:T(8,128)(2,1)S(1)}, u32[]{:S(2)}, u32[]{:S(2)}) collective-permute-start(bf16[128,256]{1,0:T(8,128)(2,1)S(1)} %fusion), channel_id=1, source_target_pairs={{0,64},{8,72},{16,80},{24,88},{32,96},{40,104},{48,112},{56,120},{... | collective-permute-start | bytes 196616 | tf_op jit(solution)/shard_map/ppermute | solution.py:417
  105.9 4.7 %collective-permute-start.18 = (bf16[128,256]{1,0:T(8,128)(2,1)S(1)}, bf16[128,256]{1,0:T(8,128)(2,1)S(1)}, u32[]{:S(2)}, u32[]{:S(2)}) collective-permute-start(bf16[128,256]{1,0:T(8,128)(2,1)S(1)} %fusion), channel_id=1, source_target_pairs={{0,32},{8,40},{16,48},{24,56},{32,64},{40,72},{48,80},{56,88},{64,... | collective-permute-start | bytes 196616 | tf_op jit(solution)/shard_map/ppermute | solution.py:417
  110.7 8.6 %collective-permute-start.21 = (bf16[128,256]{1,0:T(8,128)(2,1)S(1)}, bf16[128,256]{1,0:T(8,128)(2,1)S(1)}, u32[]{:S(2)}, u32[]{:S(2)}) collective-permute-start(bf16[128,256]{1,0:T(8,128)(2,1)S(1)} %add_convert_fusion.1.mine_ref), channel_id=1, source_target_pairs={{0,4},{1,20},{2,32},{3,48},{4,68},{5,84},{6,96},{7,112},{8,12},{9,... | collective-permute-start | bytes 196616 | tf_op jit(solution)/shard_map/ppermute | solution.py:427
  112.5 6.7 %collective-permute-start.22 = (bf16[128,256]{1,0:T(8,128)(2,1)S(1)}, bf16[128,256]{1,0:T(8,128)(2,1)S(1)}, u32[]{:S(2)}, u32[]{:S(2)}) collective-permute-start(bf16[128,256]{1,0:T(8,128)(2,1)S(1)} %add_convert_fusion.1.mine_ref), channel_id=1, source_target_pairs={{0,8},{8,0},{16,24},{24,16},{32,40},{40,32},{48,56},{56,48},{64,72... | collective-permute-start | bytes 196616 | tf_op jit(solution)/shard_map/ppermute | solution.py:428
